TPU v7x, 32 devices: a whole 2x2x4 slice. The times are simulated.
32 devices in a mesh: pairs: 16 (over z, y, core), mod: 2 (over x).
Axes of the slice: x: 2, y: 2, z: 4, core: 2. Of those that a mesh axis runs over, the one named last changes fastest.
Arguments:
- inputs: bfloat16 [2, 64, 240, 768], P('mod', 'pairs'), may hold values from -6 to 6
- cotangent: bfloat16 [2, 64, 240, 768], P('mod', 'pairs'), may hold values from -6 to 6
- text_len: int32 [64], P('pairs'), may hold values from 8 to 40, as said below
- patch_count: int32 [64], P('pairs'), may hold values from 100 to 240, as said below
- norm1_gain: float32 [768], replicated, may hold values from 0.5 to 1.5
- norm1_bias: float32 [768], replicated, may hold values from -3 to 3
- qkv_weight: bfloat16 [768, 2304], replicated, may hold values from -0.21875 to 0.21875
- query_bias: float32 [768], replicated, may hold values from -3 to 3
- value_bias: float32 [768], replicated, may hold values from -3 to 3
- out_weight: bfloat16 [768, 768], replicated, may hold values from -0.875 to 0.875
- out_bias: float32 [768], replicated, may hold values from -3 to 3
- norm2_gain: float32 [768], replicated, may hold values from 0.5 to 1.5
- norm2_bias: float32 [768], replicated, may hold values from -3 to 3
- hidden_weight: bfloat16 [768, 3072], replicated, may hold values from -0.21875 to 0.21875
- hidden_bias: float32 [3072], replicated, may hold values from -3 to 3
- down_weight: bfloat16 [3072, 768], replicated, may hold values from -0.109375 to 0.109375
- down_bias: float32 [768], replicated, may hold values from -3 to 3
Outputs:
- block_out: bfloat16 [2, 64, 240, 768], P('mod', 'pairs')
- input_grad: bfloat16 [2, 64, 240, 768], P('mod', 'pairs')
- norm1_gain_grad: float32 [768], P(('pairs', 'mod'))
- norm1_bias_grad: float32 [768], P(('pairs', 'mod'))
- qkv_weight_grad: float32 [768, 2304], P(('pairs', 'mod'))
- query_bias_grad: float32 [768], P(('pairs', 'mod'))
- value_bias_grad: float32 [768], P(('pairs', 'mod'))
- out_weight_grad: float32 [768, 768], P(('pairs', 'mod'))
- out_bias_grad: float32 [768], P(('pairs', 'mod'))
- norm2_gain_grad: float32 [768], P(('pairs', 'mod'))
- norm2_bias_grad: float32 [768], P(('pairs', 'mod'))
- hidden_weight_grad: float32 [768, 3072], P(('pairs', 'mod'))
- hidden_bias_grad: float32 [3072], P(('pairs', 'mod'))
- down_weight_grad: float32 [3072, 768], P(('pairs', 'mod'))
- down_bias_grad: float32 [768], P(('pairs', 'mod'))
Inputs may be any that keep to these rules, and one draw needn't show every extreme that they name: Rows 0 to text_len[p] - 1 of pair p's text slots are words, the rest padding; some pair has all 40. Rows 0 to patch_count[p] - 1 of pair p's patch slots are patches, the rest padding; some pair has all 240.
All inputs are finite; a program needn't handle non-finite values.
Results may differ from a plain program's by a relative error of at most 0.012.
Values may be sent and summed in bfloat16 or wider, within the bound.
A program may use at most 192 MiB of HBM per device.

v0:
```python
import jax
import jax.numpy as jnp
from jax import lax
from jax.sharding import PartitionSpec as P

HEADS = 12
HEAD_DIM = 64
TEXT = 40


EPSILON = 1e-06
MASKED = -1e30


def swapped(array, axis, bit):
    return lax.ppermute(array, axis, [(i, i ^ 1 << bit) for i in range(lax.axis_size(axis))])


def norm_parts(values):
    centre = jnp.mean(values, axis=-1, keepdims=True)
    centred = values - centre
    spread = jnp.mean(centred * centred, axis=-1, keepdims=True)
    factor = lax.rsqrt(spread + EPSILON)
    return (centred * factor, factor)


def norm_back(grad_out, normed, factor, norm_gain):
    grad_norm = grad_out * norm_gain
    mean_grad = jnp.mean(grad_norm, axis=-1, keepdims=True)
    second = jnp.mean(grad_norm * normed, axis=-1, keepdims=True)
    return (grad_norm - mean_grad - normed * second) * factor


def gelu_slope(values):
    cumulative = 0.5 * (1.0 + lax.erf(values * 0.7071067811865476))
    density = jnp.exp(-0.5 * values * values) * 0.3989422804014327
    return cumulative + values * density


def outer_sum(left_side, right_side):
    return lax.dot_general(
        left_side, right_side, (((0,), (0,)), ((), ())), preferred_element_type=jnp.float32
    )


def times_transposed(left_side, right_side):
    return lax.dot_general(
        left_side, right_side, (((1,), (1,)), ((), ())), preferred_element_type=jnp.float32
    )


def layer(tokens, cot_rows, row_live, key_live, pair_count, row_count, is_text, weights_all):
    (
        norm1_gain,
        norm1_bias,
        qkv_weight,
        query_bias,
        value_bias,
        out_weight,
        out_bias,
        norm2_gain,
        norm2_bias,
        hidden_weight,
        hidden_bias,
        down_weight,
        down_bias,
    ) = weights_all
    model_width = tokens.shape[1]
    normed1, factor1 = norm_parts(tokens)
    normal1 = (normed1 * norm1_gain + norm1_bias).astype(jnp.bfloat16)
    projected = jnp.dot(normal1, qkv_weight, preferred_element_type=jnp.float32)
    queries = ((projected[:, :model_width] + query_bias) * 0.125).astype(jnp.bfloat16)
    value_shift = jnp.concatenate([jnp.zeros_like(value_bias), value_bias])
    own_keys = (projected[:, model_width:] + value_shift).astype(jnp.bfloat16)
    far_keys = swapped(own_keys, "mod", 0)
    own_three = own_keys.reshape(pair_count, row_count, 2 * model_width)
    far_three = far_keys.reshape(pair_count, row_count, 2 * model_width)
    text_keys = jnp.where(is_text, own_three, far_three)[:, :TEXT]
    patch_keys = jnp.where(is_text, far_three, own_three)
    all_keys = jnp.concatenate([text_keys, patch_keys], axis=1)
    key_count = all_keys.shape[1]
    key_heads = all_keys[..., :model_width].reshape(pair_count, key_count, HEADS, HEAD_DIM)
    value_heads = all_keys[..., model_width:].reshape(pair_count, key_count, HEADS, HEAD_DIM)
    query_heads = queries.reshape(pair_count, row_count, HEADS, HEAD_DIM)
    live_mask = key_live[:, None, None, :]

    def scores_now():
        raw_scores = jnp.einsum(
            "pqhe,pkhe->phqk", query_heads, key_heads, preferred_element_type=jnp.float32
        )
        return jnp.where(live_mask, raw_scores, MASKED)

    scores = scores_now()
    highest = jnp.max(scores, axis=-1, keepdims=True)
    shifted = jnp.exp(scores - highest)
    totals = jnp.sum(shifted, axis=-1, keepdims=True)
    log_totals = highest + jnp.log(totals)
    probs_first = (shifted / totals).astype(jnp.bfloat16)
    mixed_rows = jnp.einsum(
        "phqk,pkhe->pqhe", probs_first, value_heads, preferred_element_type=jnp.float32
    )
    mixed_rows = mixed_rows.reshape(-1, model_width).astype(jnp.bfloat16)
    attended = jnp.dot(mixed_rows, out_weight, preferred_element_type=jnp.float32) + out_bias
    hidden = tokens + attended
    normed2, factor2 = norm_parts(hidden)
    normal2 = (normed2 * norm2_gain + norm2_bias).astype(jnp.bfloat16)
    before = jnp.dot(normal2, hidden_weight, preferred_element_type=jnp.float32) + hidden_bias
    activated = jax.nn.gelu(before, approximate=False).astype(jnp.bfloat16)
    result = (
        hidden + jnp.dot(activated, down_weight, preferred_element_type=jnp.float32) + down_bias
    )
    out_rows = (result * row_live).astype(jnp.bfloat16)
    grad_result = cot_rows * row_live
    grad_down = grad_result.astype(jnp.bfloat16)
    down_weight_grad = outer_sum(activated, grad_down)
    down_bias_grad = jnp.sum(grad_down, axis=0, dtype=jnp.float32)
    grad_before = (times_transposed(grad_down, down_weight) * gelu_slope(before)).astype(
        jnp.bfloat16
    )
    hidden_weight_grad = outer_sum(normal2, grad_before)
    hidden_bias_grad = jnp.sum(grad_before, axis=0, dtype=jnp.float32)
    grad_normal2 = times_transposed(grad_before, hidden_weight)
    norm2_gain_grad = jnp.sum(grad_normal2 * normed2, axis=0)
    norm2_bias_grad = jnp.sum(grad_normal2, axis=0)
    grad_hidden = grad_result + norm_back(grad_normal2, normed2, factor2, norm2_gain)
    grad_attended = grad_hidden.astype(jnp.bfloat16)
    out_weight_grad = outer_sum(mixed_rows, grad_attended)
    out_bias_grad = jnp.sum(grad_attended, axis=0, dtype=jnp.float32)
    grad_mixed = times_transposed(grad_attended, out_weight).astype(jnp.bfloat16)
    grad_mixed = grad_mixed.reshape(pair_count, row_count, HEADS, HEAD_DIM)
    probabilities = jnp.exp(scores_now() - log_totals)
    probs_low = probabilities.astype(jnp.bfloat16)
    grad_probs = jnp.einsum(
        "pqhe,pkhe->phqk", grad_mixed, value_heads, preferred_element_type=jnp.float32
    )
    row_dot = jnp.sum(probabilities * grad_probs, axis=-1, keepdims=True)
    grad_scores = (probabilities * (grad_probs - row_dot)).astype(jnp.bfloat16)
    grad_queries = jnp.einsum(
        "phqk,pkhe->pqhe", grad_scores, key_heads, preferred_element_type=jnp.float32
    ).astype(jnp.bfloat16)
    grad_key_heads = jnp.einsum(
        "phqk,pqhe->pkhe", grad_scores, query_heads, preferred_element_type=jnp.float32
    )
    grad_value_heads = jnp.einsum(
        "phqk,pqhe->pkhe", probs_low, grad_mixed, preferred_element_type=jnp.float32
    )
    grad_keys = jnp.concatenate(
        [
            grad_key_heads.reshape(pair_count, key_count, model_width),
            grad_value_heads.reshape(pair_count, key_count, model_width),
        ],
        axis=2,
    )
    text_grad = jnp.pad(grad_keys[:, :TEXT], ((0, 0), (0, row_count - TEXT), (0, 0)))
    patch_grad = grad_keys[:, TEXT:]
    own_grad = jnp.where(is_text, text_grad, patch_grad)
    far_grad = jnp.where(is_text, patch_grad, text_grad)
    returned = swapped(far_grad.astype(jnp.bfloat16), "mod", 0).astype(far_grad.dtype)
    grad_own_keys = (own_grad + returned).astype(jnp.bfloat16).reshape(-1, 2 * model_width)
    grad_query_rows = grad_queries.reshape(-1, model_width) * 0.125
    grad_projected = jnp.concatenate([grad_query_rows, grad_own_keys], axis=1)
    qkv_weight_grad = outer_sum(normal1, grad_projected)
    query_bias_grad = jnp.sum(grad_query_rows, axis=0, dtype=jnp.float32)
    value_bias_grad = jnp.sum(grad_own_keys[:, model_width:], axis=0, dtype=jnp.float32)
    grad_normal1 = times_transposed(grad_projected, qkv_weight)
    norm1_gain_grad = jnp.sum(grad_normal1 * normed1, axis=0)
    norm1_bias_grad = jnp.sum(grad_normal1, axis=0)
    grad_tokens = grad_hidden + norm_back(grad_normal1, normed1, factor1, norm1_gain)
    grad_rows = (grad_tokens * row_live).astype(jnp.bfloat16)
    summed = (
        lax.psum_scatter(norm1_gain_grad, ("pairs", "mod"), scatter_dimension=0, tiled=True),
        lax.psum_scatter(norm1_bias_grad, ("pairs", "mod"), scatter_dimension=0, tiled=True),
        lax.psum_scatter(qkv_weight_grad, ("pairs", "mod"), scatter_dimension=0, tiled=True),
        lax.psum_scatter(query_bias_grad, ("pairs", "mod"), scatter_dimension=0, tiled=True),
        lax.psum_scatter(value_bias_grad, ("pairs", "mod"), scatter_dimension=0, tiled=True),
        lax.psum_scatter(out_weight_grad, ("pairs", "mod"), scatter_dimension=0, tiled=True),
        lax.psum_scatter(out_bias_grad, ("pairs", "mod"), scatter_dimension=0, tiled=True),
        lax.psum_scatter(norm2_gain_grad, ("pairs", "mod"), scatter_dimension=0, tiled=True),
        lax.psum_scatter(norm2_bias_grad, ("pairs", "mod"), scatter_dimension=0, tiled=True),
        lax.psum_scatter(hidden_weight_grad, ("pairs", "mod"), scatter_dimension=0, tiled=True),
        lax.psum_scatter(hidden_bias_grad, ("pairs", "mod"), scatter_dimension=0, tiled=True),
        lax.psum_scatter(down_weight_grad, ("pairs", "mod"), scatter_dimension=0, tiled=True),
        lax.psum_scatter(down_bias_grad, ("pairs", "mod"), scatter_dimension=0, tiled=True),
    )
    return (out_rows, grad_rows, summed)


def on_device(
    inputs,
    cotangent,
    text_len,
    patch_count,
    norm1_gain,
    norm1_bias,
    qkv_weight,
    query_bias,
    value_bias,
    out_weight,
    out_bias,
    norm2_gain,
    norm2_bias,
    hidden_weight,
    hidden_bias,
    down_weight,
    down_bias,
):
    weights_all = (
        norm1_gain,
        norm1_bias,
        qkv_weight,
        query_bias,
        value_bias,
        out_weight,
        out_bias,
        norm2_gain,
        norm2_bias,
        hidden_weight,
        hidden_bias,
        down_weight,
        down_bias,
    )
    model_width = inputs.shape[3]
    slot_count = inputs.shape[2]
    pair_count = inputs.shape[1]
    slot_index = jnp.arange(slot_count, dtype=jnp.int32)
    is_text = lax.axis_index("mod") == 0
    text_live = (slot_index[None, :TEXT] < text_len[:, None]).astype(jnp.float32)
    patch_live = (slot_index[None, :] < patch_count[:, None]).astype(jnp.float32)
    key_live = jnp.concatenate([text_live, patch_live], axis=1) > 0
    text_rows = jnp.pad(text_live, ((0, 0), (0, slot_count - TEXT)))
    row_live = jnp.where(is_text, text_rows, patch_live).reshape(-1, 1)
    tokens = inputs.reshape(-1, model_width).astype(jnp.float32)
    cot_rows = cotangent.reshape(-1, model_width).astype(jnp.float32)
    out_rows, grad_rows, summed = layer(
        tokens, cot_rows, row_live, key_live, pair_count, slot_count, is_text, weights_all
    )
    block_out = out_rows.reshape(inputs.shape)
    input_grad = grad_rows.reshape(inputs.shape)
    return (
        block_out,
        input_grad,
        summed[0],
        summed[1],
        summed[2],
        summed[3],
        summed[4],
        summed[5],
        summed[6],
        summed[7],
        summed[8],
        summed[9],
        summed[10],
        summed[11],
        summed[12],
    )


def solution(mesh):
    return jax.shard_map(
        on_device,
        mesh=mesh,
        in_specs=(
            P("mod", "pairs", None, None),
            P("mod", "pairs", None, None),
            P("pairs"),
            P("pairs"),
            P(),
            P(),
            P(),
            P(),
            P(),
            P(),
            P(),
            P(),
            P(),
            P(),
            P(),
            P(),
            P(),
        ),
        out_specs=(
            P("mod", "pairs", None, None),
            P("mod", "pairs", None, None),
            P(("pairs", "mod")),
            P(("pairs", "mod")),
            P(("pairs", "mod"), None),
            P(("pairs", "mod")),
            P(("pairs", "mod")),
            P(("pairs", "mod"), None),
            P(("pairs", "mod")),
            P(("pairs", "mod")),
            P(("pairs", "mod")),
            P(("pairs", "mod"), None),
            P(("pairs", "mod")),
            P(("pairs", "mod"), None),
            P(("pairs", "mod")),
        ),
        check_vma=False,
    )
```

profile of v0, /device:TPU:0, one launch (start us, length us, event | category | flops | bytes accessed | tf_op | source)
XLA Modules:
  0.0 784.8 jit_solution(2856247809190221614)
XLA Ops:
  34.0 4.1 reshape.195
  42.3 47.8 %collective-permute-done = bf16[960,1536]{1,0:T(8,128)(2,1)} collective-permute-done((bf16[960,1536]{1,0:T(8,128)(2,1)}, bf16[960,1536]{1,0:T(8,128)(2,1)}, u32[]{:S(2)}, u32[]{:S(2)}) %collective-permute-start) | collective-permute-done | bytes 2949152 | tf_op jit(solution)/shard_map/ppermute | solution.py:16
  90.1 4.1 broadcast_select_fusion
  96.3 4.0 copy.53
  104.3 9.8 %select_reduce_fusion = (f32[4,12,240]{2,1,0:T(8,128)S(1)}, f32[4,12,240,280]{2,3,1,0:T(8,128)}) fusion(pred[4,280]{1,0:T(4,128)(4,1)S(1)} %maximum_compare_fusion, bf16[4,280,12,64]{1,3,2,0:T(8,128)(2,1)} %bitcast.61, bf16[4,240,12,64]{1,0,3,2:T(4,128)(2,1)} %reshape.195), kind=kOutput, calls=%fused_computation.33 | convolution fusion | flops 419316480 | bytes 16144480 | tf_op jit(solution)/shard_map/pqhe,pkhe->phqk/dot_general | solution.py:88
  114.2 8.2 %fusion = f32[4,12,240]{2,1,0:T(8,128)S(1)} fusion(f32[4,12,240,280]{2,3,1,0:T(8,128)} %get-tuple-element.39, f32[4,12,240]{2,1,0:T(8,128)S(1)} %get-tuple-element.38, pred[4,280]{1,0:T(4,128)(4,1)S(1)} %maximum_compare_fusion), kind=kLoop, calls=%fused_computation.7 | loop fusion | flops 9665280 | bytes 12995680 | tf_op jit(solution)/shard_map/reduce_sum | solution.py:96
  123.1 6.7 fusion.35
  132.2 4.2 convert_element_type.129
  140.9 35.3 %fusion.3 = (bf16[960,3072]{1,0:T(8,128)(2,1)}, f32[960,3072]{1,0:T(8,128)}) fusion(f32[3072]{0:T(1024)S(1)} %copy-done.38, bf16[768,3072]{1,0:T(8,128)(2,1)} %param.30, f32[960,768]{1,0:T(8,128)S(1)} %get-tuple-element.41, f32[768]{0:T(1024)S(1)} %copy-done.30, f32[768]{0:T(1024)S(1)} %copy-done.24, f32[960]{0:T(1024)S(1)} %add_rsqrt_fusion, ...), kind=kOutput, calls=%fused_computation.10 | convolution fusion | flops 4728176640 | bytes 25388544 | tf_op jit(solution)/shard_map/dot_general | solution.py:107
  176.2 12.1 %convert_reduce_fusion = (f32[3072]{0:T(1024)}, bf16[960,3072]{1,0:T(8,128)(2,1)S(1)}) fusion(f32[960,3072]{1,0:T(8,128)} %get-tuple-element.43, f32[3072]{0:T(1024)S(1)} %copy-done.38, bf16[960,768]{1,0:T(8,128)(2,1)S(1)} %copy-done.18, bf16[3072,768]{1,0:T(8,128)(2,1)S(1)} %bitcast.78), kind=kOutput, calls=%fused_computation.17 | convolution fusion | flops 4568183808 | bytes 23912448 | tf_op jit(solution)/shard_map/dot_general | solution.py:47
  188.3 5.9 multiply_reduce_fusion.1
  202.8 4.1 reshape.198
  206.9 10.4 %fusion.18 = f32[4,12,64,280]{3,2,1,0:T(8,128)} fusion(f32[4,12,240,280]{2,3,1,0:T(8,128)} %get-tuple-element.39, f32[4,12,240]{2,1,0:T(8,128)} %log_add_fusion, pred[4,280]{1,0:T(4,128)(4,1)S(1)} %maximum_compare_fusion, bf16[4,240,12,64]{1,0,3,2:T(4,128)(2,1)} %reshape.198), kind=kOutput, calls=%fused_computation.35 | convolution fusion | flops 422553600 | bytes 17864800 | tf_op jit(solution)/shard_map/phqk,pqhe->pkhe/dot_general | solution.py:144
  217.3 11.2 %multiply_reduce_fusion = (f32[4,12,240]{2,1,0:T(8,128)}, f32[4,12,240,280]{2,3,1,0:T(8,128)}) fusion(f32[4,12,240,280]{2,3,1,0:T(8,128)} %get-tuple-element.39, f32[4,12,240]{2,1,0:T(8,128)S(1)} %copy-done.21, pred[4,280]{1,0:T(4,128)(4,1)S(1)} %maximum_compare_fusion, bf16[4,280,12,64]{1,3,2,0:T(8,128)(2,1)S(1)} %bitcast.67, ...), kind=kOutput, calls=%fused_computation.3 | convolution fusion | flops 425767680 | bytes 29092960 | tf_op jit(solution)/shard_map/pqhe,pkhe->phqk/dot_general | solution.py:133
  228.4 5.6 copy.62
  234.0 10.2 %multiply_convert_fusion = bf16[4,12,240,280]{2,3,1,0:T(8,128)(2,1)S(1)} fusion(f32[4,12,240,280]{2,3,1,0:T(8,128)} %get-tuple-element.46, f32[4,12,240,280]{2,3,1,0:T(8,128)} %get-tuple-element.39, f32[4,12,240]{2,1,0:T(8,128)} %get-tuple-element.45, f32[4,12,240]{2,1,0:T(8,128)} %log_add_fusion, pred[4,280]{1,0:T(4,128)(4,1)S(1)} %maximum_compare_fusion), kind=kLoop, calls=%fused_computation.2 | loop fusion | flops 16128000 | bytes 32349280 | tf_op jit(solution)/shard_map/convert_element_type | solution.py:137
  244.3 4.3 fusion.39
  248.6 5.6 copy.61
  254.2 6.6 select_convert_fusion
  265.6 6.1 convert_reduce_fusion.1
  280.7 49.8 %collective-permute-done.1 = bf16[4,240,1536]{2,1,0:T(8,128)(2,1)} collective-permute-done((bf16[4,240,1536]{2,1,0:T(8,128)(2,1)}, bf16[4,240,1536]{2,1,0:T(8,128)(2,1)}, u32[]{:S(2)}, u32[]{:S(2)}) %collective-permute-start.1) | collective-permute-done | bytes 2949152 | tf_op jit(solution)/shard_map/ppermute | solution.py:16
  330.5 6.2 add_convert_fusion
  338.2 5.9 fusion.29
  344.2 9.9 %fusion.55 = f32[3072,768]{1,0:T(8,128)} fusion(bf16[960,3072]{1,0:T(8,128)(2,1)} %get-tuple-element.42, bf16[960,768]{1,0:T(8,128)(2,1)} %fusion.31), kind=kOutput, calls=%fused_computation.122 | convolution fusion | flops 4529848320 | bytes 16809984 | tf_op jit(solution)/shard_map/dot_general | solution.py:41
  354.8 11.2 %fusion.51 = f32[768,3072]{1,0:T(8,128)} fusion(bf16[960,3072]{1,0:T(8,128)(2,1)} %copy-done.12, f32[960,768]{1,0:T(8,128)} %copy-done.2, f32[768]{0:T(1024)} %param.29, f32[768]{0:T(1024)S(1)} %copy-done.25, f32[960]{0:T(1024)S(1)} %add_rsqrt_fusion, f32[960]{0:T(1024)S(1)} %broadcast_multiply_fusion.4), kind=kOutput, calls=%fused_computation.118 | convolution fusion | flops 4533534720 | bytes 18298368 | tf_op jit(solution)/shard_map/dot_general | solution.py:41
  369.6 10.9 %multiply_convert_fusion.3 = bf16[960,768]{1,0:T(8,128)(2,1)} fusion(f32[960,768]{1,0:T(8,128)} %copy-done.2, bf16[960,3072]{1,0:T(8,128)(2,1)} %get-tuple-element.42, bf16[3072,768]{1,0:T(8,128)(2,1)} %param.32, f32[960]{0:T(1024)S(1)} %copy-done.23, f32[768]{0:T(1024)} %param.33), kind=kOutput, calls=%fused_computation.67 | convolution fusion | flops 4532797440 | bytes 15047424 | tf_op jit(solution)/shard_map/dot_general | solution.py:110
  381.4 6.5 multiply_reduce_fusion.2
  387.9 42.4 %all-reduce.11 = (f32[768]{0:T(1024)}, f32[768]{0:T(1024)}, f32[768]{0:T(1024)}, f32[768]{0:T(1024)}, f32[768]{0:T(1024)}, /*index=5*/f32[768]{0:T(1024)}, f32[768]{0:T(1024)}, f32[3072]{0:T(1024)}, f32[768]{0:T(1024)}) all-reduce(f32[768]{0:T(1024)} %get-tuple-element.17, ...), channel_id=2, replica_groups=mesh['pairs'=16,'mod'=2] {'pairs','mod'}, use_global_device_ids=true, to_apply=%region_12.13.clone | all-reduce | flops 9216 | bytes 73728
  443.0 4.9 multiply_convert_fusion.2
  447.9 47.0 %reduce-scatter.5.cloned.1.call-done = f32[24,2304]{1,0:T(8,128)} async-done(((f32[768,2304]{1,0:T(8,128)}), f32[24,2304]{1,0:T(8,128)}) %reduce-scatter.5.cloned.1.call-update) | async-done | bytes 221200 | tf_op jit(solution)/shard_map/reduce_scatter | solution.py:173
  494.9 141.6 %reduce-scatter.11.cloned.1.call-done = f32[96,768]{1,0:T(8,128)} async-done(((f32[3072,768]{1,0:T(8,128)}), f32[96,768]{1,0:T(8,128)}) %reduce-scatter.11.cloned.1.call-update) | async-done | bytes 294928 | tf_op jit(solution)/shard_map/reduce_scatter | solution.py:182
  636.6 141.5 %reduce-scatter.9.cloned.1.call-done = f32[24,3072]{1,0:T(8,128)} async-done(((f32[768,3072]{1,0:T(8,128)}), f32[24,3072]{1,0:T(8,128)}) %reduce-scatter.9.cloned.1.call-update) | async-done | bytes 294928 | tf_op jit(solution)/shard_map/reduce_scatter | solution.py:180
  (152 shorter events, 86.4 us)
Async XLA Ops:
  7.2 7.8 copy-start
  7.2 440.7 %reduce-scatter.7.cloned.1.call-start = ((), (), s32[]{:S(2)}) async-start(), calls=%async_computation.5 | async-start | bytes 2433024 | tf_op jit(solution)/shard_map/reduce_scatter | solution.py:176
  9.1 9.5 %copy-start.26 = (f32[960]{0:T(1024)}, f32[960]{0:T(1024)S(1)}, u32[]{:S(2)}) copy-start(f32[960]{0:T(1024)S(1)} %div.35) | copy-start | bytes 11524
  11.1 7.5 copy-start.28
  23.0 67.2 %collective-permute-start = (bf16[960,1536]{1,0:T(8,128)(2,1)}, bf16[960,1536]{1,0:T(8,128)(2,1)}, u32[]{:S(2)}, u32[]{:S(2)}) collective-permute-start(bf16[960,1536]{1,0:T(8,128)(2,1)} %fusion.26), channel_id=1, source_target_pairs={{0,1},{1,0},{2,3},{3,2},{4,5},{5,4},{6,7},{7,6},{8,9},{9,8},{10,11... | collective-permute-start | bytes 8847368 | tf_op jit(solution)/shard_map/ppermute | solution.py:16
  28.1 11.5 %copy-start.22 = (f32[960]{0:T(1024)}, f32[960]{0:T(1024)S(1)}, u32[]{:S(2)}) copy-start(f32[960]{0:T(1024)S(1)} %mul.195) | copy-start | bytes 11524
  114.2 8.9 %copy-start.7 = (bf16[4,280,768]{1,2,0:T(8,128)(2,1)S(1)}, bf16[4,280,768]{1,2,0:T(8,128)(2,1)}, u32[]{:S(2)}) copy-start(bf16[4,280,768]{1,2,0:T(8,128)(2,1)} %copy.51) | copy-start | bytes 5160964
  129.8 6.6 copy-start.39
  136.4 39.7 %slice-start.2 = ((s8[4718592]{0:T(1024)(128)(4,1)}), s8[4194304]{0:T(1024)(128)(4,1)S(1)}, s32[]{:S(2)}) async-start(s8[4718592]{0:T(1024)(128)(4,1)} %bitcast.77), calls=%async_computation.10 | async-start | bytes 8388608
  136.4 51.8 %slice-start = ((s8[4718592]{0:T(1024)(128)(4,1)}), s8[4194304]{0:T(1024)(128)(4,1)S(1)}, s32[]{:S(2)}) async-start(s8[4718592]{0:T(1024)(128)(4,1)} %bitcast.75), calls=%async_computation.8 | async-start | bytes 8388608
  140.3 53.9 %copy-start.2 = (f32[960,768]{1,0:T(8,128)}, f32[960,768]{1,0:T(8,128)S(1)}, u32[]{:S(2)}) copy-start(f32[960,768]{1,0:T(8,128)S(1)} %get-tuple-element.41) | copy-start | bytes 8847364
  140.9 35.3 %copy-start.18 = (bf16[960,768]{1,0:T(8,128)(2,1)S(1)}, bf16[960,768]{1,0:T(8,128)(2,1)}, u32[]{:S(2)}) copy-start(bf16[960,768]{1,0:T(8,128)(2,1)} %fusion.31) | copy-start | bytes 4423684
  140.9 35.3 %slice-start.3 = ((s8[4718592]{0:T(1024)(128)(4,1)}), s8[524288]{0:T(1024)(128)(4,1)S(1)}, s32[]{:S(2)}) async-start(s8[4718592]{0:T(1024)(128)(4,1)} %bitcast.77), calls=%async_computation.11 | async-start | bytes 1048576
  140.9 47.4 %slice-start.1 = ((s8[4718592]{0:T(1024)(128)(4,1)}), s8[524288]{0:T(1024)(128)(4,1)S(1)}, s32[]{:S(2)}) async-start(s8[4718592]{0:T(1024)(128)(4,1)} %bitcast.75), calls=%async_computation.9 | async-start | bytes 1048576
  206.9 10.4 %copy-start.6 = (bf16[4,240,12,64]{1,0,3,2:T(4,128)(2,1)S(1)}, bf16[4,240,12,64]{1,0,3,2:T(4,128)(2,1)}, u32[]{:S(2)}) copy-start(bf16[4,240,12,64]{1,0,3,2:T(4,128)(2,1)} %reshape.198) | copy-start | bytes 4423684
  206.9 10.4 %copy-start.8 = (bf16[4,280,768]{1,2,0:T(8,128)(2,1)S(1)}, bf16[4,280,768]{1,2,0:T(8,128)(2,1)}, u32[]{:S(2)}) copy-start(bf16[4,280,768]{1,2,0:T(8,128)(2,1)} %copy.51) | copy-start | bytes 5160964
  206.9 10.4 %copy-start.21 = (f32[4,12,240]{2,1,0:T(8,128)S(1)}, f32[4,12,240]{2,1,0:T(8,128)}, u32[]{:S(2)}) copy-start(f32[4,12,240]{2,1,0:T(8,128)} %log_add_fusion) | copy-start | bytes 138244
  234.0 10.2 %copy-start.3 = (bf16[4,240,12,64]{1,0,3,2:T(4,128)(2,1)S(1)}, bf16[4,240,12,64]{1,0,3,2:T(4,128)(2,1)}, u32[]{:S(2)}) copy-start(bf16[4,240,12,64]{1,0,3,2:T(4,128)(2,1)} %reshape.195) | copy-start | bytes 4423684
  254.2 8.4 %copy-start.11 = (f32[960,768]{1,0:T(8,128)S(1)}, f32[960,768]{1,0:T(8,128)}, u32[]{:S(2)}) copy-start(f32[960,768]{1,0:T(8,128)} %copy-done.10) | copy-start | bytes 8847364
  254.2 8.4 %copy-start.15 = (bf16[960,768]{0,1:T(8,128)(2,1)S(1)}, bf16[960,768]{0,1:T(8,128)(2,1)}, u32[]{:S(2)}) copy-start(bf16[960,768]{0,1:T(8,128)(2,1)} %convert_element_type.129) | copy-start | bytes 4423684
  260.9 69.6 %collective-permute-start.1 = (bf16[4,240,1536]{2,1,0:T(8,128)(2,1)}, bf16[4,240,1536]{2,1,0:T(8,128)(2,1)}, u32[]{:S(2)}, u32[]{:S(2)}) collective-permute-start(bf16[4,240,1536]{2,1,0:T(8,128)(2,1)} %select_convert_fusion), channel_id=1, source_target_pairs={{0,1},{1,0},{2,3},{3,2},{4,5},{5,4},{6,7},{7,6},{8,9},{9,8},{10,11... | collective-permute-start | bytes 8847368 | tf_op jit(solution)/shard_map/ppermute | solution.py:16
  265.5 229.4 %reduce-scatter.5.cloned.1.call-start = ((), (), s32[]{:S(2)}) async-start(), calls=%async_computation.4 | async-start | bytes 7299072 | tf_op jit(solution)/shard_map/reduce_scatter | solution.py:173
  280.7 57.5 %copy-start.17 = (bf16[960,768]{1,0:T(8,128)(2,1)S(1)}, bf16[960,768]{1,0:T(8,128)(2,1)}, u32[]{:S(2)}) copy-start(bf16[960,768]{1,0:T(8,128)(2,1)} %copy-done.16) | copy-start | bytes 4423684
  280.7 57.5 %copy-start.19 = (bf16[960,768]{1,0:T(8,128)(2,1)S(1)}, bf16[960,768]{1,0:T(8,128)(2,1)}, u32[]{:S(2)}) copy-start(bf16[960,768]{1,0:T(8,128)(2,1)} %copy.63) | copy-start | bytes 4423684
  344.2 292.4 %reduce-scatter.11.cloned.1.call-start = ((), (), s32[]{:S(2)}) async-start(), calls=%async_computation.7 | async-start | bytes 9732096 | tf_op jit(solution)/shard_map/reduce_scatter | solution.py:182
  354.1 424.0 %reduce-scatter.9.cloned.1.call-start = ((), (), s32[]{:S(2)}) async-start(), calls=%async_computation.6 | async-start | bytes 9732096 | tf_op jit(solution)/shard_map/reduce_scatter | solution.py:180
  369.6 11.0 %copy-start.14 = (bf16[4,240,1536]{2,1,0:T(8,128)(2,1)S(1)}, bf16[4,240,1536]{2,1,0:T(8,128)(2,1)}, u32[]{:S(2)}) copy-start(bf16[4,240,1536]{2,1,0:T(8,128)(2,1)} %copy-done.13) | copy-start | bytes 8847364
  369.6 11.8 %copy-start.5 = (bf16[1,4,240,768]{3,2,1,0:T(8,128)(2,1)S(1)}, bf16[1,4,240,768]{3,2,1,0:T(8,128)(2,1)}, u32[]{:S(2)}) copy-start(bf16[1,4,240,768]{3,2,1,0:T(8,128)(2,1)} %param.17) | copy-start | bytes 4423684
  369.6 11.8 %copy-start.20 = (bf16[960,768]{1,0:T(8,128)(2,1)S(1)}, bf16[960,768]{1,0:T(8,128)(2,1)}, u32[]{:S(2)}) copy-start(bf16[960,768]{1,0:T(8,128)(2,1)} %copy.63) | copy-start | bytes 4423684
  369.6 11.8 %copy-start.27 = (f32[960]{0:T(1024)S(1)}, f32[960]{0:T(1024)}, u32[]{:S(2)}) copy-start(f32[960]{0:T(1024)} %copy-done.26) | copy-start | bytes 11524
  369.6 11.8 %copy-start.29 = (f32[960]{0:T(1024)S(1)}, f32[960]{0:T(1024)}, u32[]{:S(2)}) copy-start(f32[960]{0:T(1024)} %copy-done.28) | copy-start | bytes 11524
  369.6 11.8 %copy-start.35 = (f32[768]{0:T(1024)S(1)}, f32[768]{0:T(1024)}, u32[]{:S(2)}) copy-start(f32[768]{0:T(1024)} %param.21) | copy-start | bytes 9220
  (18 other events, 64.2 us)
Sparse Core Ops, SparseCore 0:
  265.6 104.2 reduce-scatter.6
  376.1 118.7 reduce-scatter.4
  501.4 135.1 reduce-scatter.10
  642.9 135.1 reduce-scatter.8
where the time goes:
time: 790 us; the launch traced here: 785 us
  waiting for transfers between devices  428 us (54%)
  matrix products  159 us (20%)
  local copies, waits for them, and re-layouts  69.4 us (9%)
  other arithmetic  67 us (8%)
  blocking collectives  42.4 us (5%)
  between operations  14.4 us (2%)
    reduce_scatter x1, waiting for transfers between devices, layer(): lax.psum_scatter(down_weight_grad, ('pairs', 'mod'), scatter_dimension=0,...  142 us
    reduce_scatter x1, waiting for transfers between devices, layer(): lax.psum_scatter(hidden_weight_grad, ('pairs', 'mod'), scatter_dimension=...  141 us
    ppermute x2, waiting for transfers between devices, swapped(): lax.ppermute(array, axis, [(i, i ^ 1 << bit) for i in range(lax.axis_size...  97.6 us
    reduce_scatter x1, waiting for transfers between devices, layer(): lax.psum_scatter(qkv_weight_grad, ('pairs', 'mod'), scatter_dimension=0,...  47 us
    unnamed x1, blocking collectives  42.4 us
    dot_general x1, matrix products, layer(): jnp.dot(normal2, hidden_weight, preferred_element_type=jnp.float32)  35.3 us
    dot_general x4, matrix products, outer_sum(): lax.dot_general(left_side, right_side, (((0,), (0,)), ((), ())), preferre...  29.8 us
    dot_general x4, matrix products, times_transposed(): lax.dot_general(left_side, right_side, (((1,), (1,)), ((), ())), preferre...  26.9 us
  transfers between devices with their start and end apart: 6, of which 5 were waited for; matrix products, arithmetic and copies ran while one was open for 13% of the time, Pallas kernels for 0%

commit v1 on v0

v1 whole, which is shorter than its diff:
```python
import functools

import jax
import jax.numpy as jnp
from jax import lax
from jax.experimental import pallas as pl
from jax.experimental.pallas import tpu as pltpu
from jax.sharding import PartitionSpec as P

HEADS = 12
HEAD_DIM = 64
TEXT = 40
EPSILON = 1e-06
MASKED = -1e30
F32 = jnp.float32
BF16 = jnp.bfloat16
VMEM_LIMIT = 60 * 1024 * 1024


def padded(count):
    return -(-count // 32) * 32


def dot(a, b, ca=1, cb=0):
    return lax.dot_general(a, b, (((ca,), (cb,)), ((), ())), preferred_element_type=F32)


def norm_parts(values):
    centre = jnp.mean(values, axis=-1, keepdims=True)
    centred = values - centre
    spread = jnp.mean(centred * centred, axis=-1, keepdims=True)
    factor = lax.rsqrt(spread + EPSILON)
    return centred * factor, factor


def norm_back(grad_out, normed, factor, norm_gain):
    grad_norm = grad_out * norm_gain
    mean_grad = jnp.mean(grad_norm, axis=-1, keepdims=True)
    second = jnp.mean(grad_norm * normed, axis=-1, keepdims=True)
    return (grad_norm - mean_grad - normed * second) * factor


def live_slots(index, text_count, patch_count, slots):
    return (index < patch_count) | ((index >= slots) & (index - slots < text_count))


def live_rows(lens, pairs, rows, slots):
    parts = []
    for pair in range(pairs):
        index = lax.broadcasted_iota(jnp.int32, (rows, 1), 0)
        parts.append(live_slots(index, lens[pair], lens[pairs + pair], slots).astype(F32))
    return jnp.concatenate(parts, axis=0)


def forward_kernel(
    slots, lens, seq, gain, shift, wqkv, qkv_bias, wout, out_bias, q_out, k_out, v_out, mixed, hidden
):
    pairs, rows, width = seq.shape
    tokens = seq[...].reshape(pairs * rows, width).astype(F32)
    normed, _ = norm_parts(tokens)
    normal = (normed * gain[...] + shift[...]).astype(BF16)
    for part, ref in enumerate((q_out, k_out, v_out)):
        cols = slice(part * width, (part + 1) * width)
        made = dot(normal, wqkv[:, cols]) + qkv_bias[:, cols]
        if part == 0:
            made = made * 0.125
        ref[...] = made.astype(BF16).reshape(pairs, rows, width)
    first = lax.broadcasted_iota(jnp.int32, (rows, 128), 1) < HEAD_DIM
    column = lax.broadcasted_iota(jnp.int32, (1, rows), 1)
    groups = width // 128

    def step(it, carry):
        pair = it // groups
        off = pl.multiple_of((it % groups) * 128, 128)
        live = live_slots(column, lens[pair], lens[pairs + pair], slots)
        q2 = q_out[pair, :, pl.ds(off, 128)]
        k2 = k_out[pair, :, pl.ds(off, 128)]
        v2 = v_out[pair, :, pl.ds(off, 128)]
        halves = []
        for half in range(2):
            keep = first if half == 0 else ~first
            qm = jnp.where(keep, q2, jnp.zeros_like(q2))
            scores = jnp.where(live, dot(qm, k2, 1, 1), MASKED)
            highest = jnp.max(scores, axis=-1, keepdims=True)
            shifted = jnp.exp(scores - highest)
            total = jnp.sum(shifted, axis=-1, keepdims=True)
            halves.append(dot(shifted.astype(BF16), v2) / total)
        mixed[pair, :, pl.ds(off, 128)] = jnp.where(first, halves[0], halves[1]).astype(BF16)
        return carry

    lax.fori_loop(0, pairs * groups, step, 0)
    rows_mixed = mixed[...].reshape(pairs * rows, width)
    hidden[...] = tokens + dot(rows_mixed, wout[...]) + out_bias[...]


def gelu_parts(values):
    cumulative = 0.5 * (1.0 + lax.erf(values * 0.7071067811865476))
    density = jnp.exp(-0.5 * values * values) * 0.3989422804014327
    return values * cumulative, cumulative + values * density


def feed_kernel(
    pairs,
    slots,
    lens,
    hidden,
    cot,
    gain,
    shift,
    wh,
    hbias,
    wd,
    dbias,
    result,
    grad_hidden,
    wh_grad,
    wd_grad,
    hb_grad,
    vectors,
    normal,
    gdown,
    total,
    gnormal,
):
    chunk = pl.program_id(0)
    count = pl.num_programs(0)
    rows = hidden.shape[0] // pairs
    live = live_rows(lens, pairs, rows, slots)

    @pl.when(chunk == 0)
    def _():
        normed, _ = norm_parts(hidden[...])
        normal[...] = (normed * gain[...] + shift[...]).astype(BF16)
        gdown[...] = (cot[...].astype(F32) * live).astype(BF16)
        total[...] = hidden[...] + dbias[...]
        gnormal[...] = jnp.zeros_like(gnormal)

    before = dot(normal[...], wh[...]) + hbias[...]
    active, slope = gelu_parts(before)
    active = active.astype(BF16)
    total[...] += dot(active, wd[...])
    wd_grad[...] = dot(active, gdown[...], 0, 0).astype(BF16)
    gbefore = (dot(gdown[...], wd[...], 1, 1) * slope).astype(BF16)
    gnormal[...] += dot(gbefore, wh[...], 1, 1)
    wh_grad[...] = dot(normal[...], gbefore, 0, 0).astype(BF16)
    hb_grad[...] = jnp.sum(gbefore.astype(F32), axis=0, keepdims=True)

    @pl.when(chunk == count - 1)
    def _():
        result[...] = (total[...] * live).astype(BF16)
        normed, factor = norm_parts(hidden[...])
        gnorm = gnormal[...]
        vectors[0:1, :] = jnp.sum(gnorm * normed, axis=0, keepdims=True)
        vectors[1:2, :] = jnp.sum(gnorm, axis=0, keepdims=True)
        down = gdown[...].astype(F32)
        vectors[2:3, :] = jnp.sum(down, axis=0, keepdims=True)
        made = down + norm_back(gnorm, normed, factor, gain[...])
        vectors[3:4, :] = jnp.sum(made.astype(BF16).astype(F32), axis=0, keepdims=True)
        grad_hidden[...] = made


def backward_kernel(
    slots,
    lens,
    seq,
    gain,
    shift,
    q_in,
    k_in,
    v_in,
    mixed,
    ghidden,
    wqkv,
    wout,
    input_grad,
    weight_grad,
    vectors,
    gmixed,
    gproj,
):
    pairs, rows, width = seq.shape
    every = pairs * rows
    gattended = ghidden[...].astype(BF16)
    gmixed[...] = dot(gattended, wout[...], 1, 1).astype(BF16).reshape(pairs, rows, width)
    weight_grad[:, 3 * width : 4 * width] = dot(
        mixed[...].reshape(every, width), gattended, 0, 0
    ).astype(BF16)
    first = lax.broadcasted_iota(jnp.int32, (rows, 128), 1) < HEAD_DIM
    index = lax.broadcasted_iota(jnp.int32, (rows, 1), 0)
    groups = width // 128

    def step(it, carry):
        pair = it // groups
        base = (it % groups) * 128
        off = pl.multiple_of(base, 128)
        live = live_slots(index, lens[pair], lens[pairs + pair], slots)
        q2 = q_in[pair, :, pl.ds(off, 128)]
        k2 = k_in[pair, :, pl.ds(off, 128)]
        v2 = v_in[pair, :, pl.ds(off, 128)]
        g2 = gmixed[pair, :, pl.ds(off, 128)]
        gq = gk = gv = None
        for half in range(2):
            keep = first if half == 0 else ~first
            zero = jnp.zeros_like(q2)
            qm = jnp.where(keep, q2, zero)
            km = jnp.where(keep, k2, zero)
            gm = jnp.where(keep, g2, zero)
            scores = jnp.where(live, dot(k2, qm, 1, 1), MASKED)
            highest = jnp.max(scores, axis=0, keepdims=True)
            shifted = jnp.exp(scores - highest)
            probs = shifted * (1.0 / jnp.sum(shifted, axis=0, keepdims=True))
            gprobs = dot(v2, gm, 1, 1)
            row_dot = jnp.sum(probs * gprobs, axis=0, keepdims=True)
            gscores = (probs * (gprobs - row_dot)).astype(BF16)
            new_v = dot(probs.astype(BF16), gm)
            new_k = dot(gscores, qm)
            new_q = dot(gscores, km, 0, 0)
            gq = new_q if gq is None else gq + new_q
            gk = new_k if gk is None else gk + new_k
            gv = new_v if gv is None else gv + new_v
        gproj[pair, :, pl.ds(off, 128)] = (gq * 0.125).astype(BF16)
        gproj[pair, :, pl.ds(pl.multiple_of(base + width, 128), 128)] = gk.astype(BF16)
        gproj[pair, :, pl.ds(pl.multiple_of(base + 2 * width, 128), 128)] = gv.astype(BF16)
        return carry

    lax.fori_loop(0, pairs * groups, step, 0)
    tokens = seq[...].reshape(every, width).astype(F32)
    normed, factor = norm_parts(tokens)
    normal = (normed * gain[...] + shift[...]).astype(BF16)
    gnormal = jnp.zeros((every, width), F32)
    for part in range(3):
        cols = slice(part * width, (part + 1) * width)
        piece = gproj[:, :, cols].reshape(every, width)
        gnormal += dot(piece, wqkv[:, cols], 1, 1)
        weight_grad[:, cols] = dot(normal, piece, 0, 0).astype(BF16)
        if part == 0:
            vectors[2:3, :] = jnp.sum(piece.astype(F32), axis=0, keepdims=True)
        if part == 2:
            vectors[3:4, :] = jnp.sum(piece.astype(F32), axis=0, keepdims=True)
    vectors[0:1, :] = jnp.sum(gnormal * normed, axis=0, keepdims=True)
    vectors[1:2, :] = jnp.sum(gnormal, axis=0, keepdims=True)
    live = live_rows(lens, pairs, rows, slots)
    made = ghidden[...] + norm_back(gnormal, normed, factor, gain[...])
    input_grad[...] = (made * live).astype(BF16).reshape(pairs, rows, width)


def whole_spec():
    return pl.BlockSpec(memory_space=pltpu.VMEM)


def smem_spec():
    return pl.BlockSpec(memory_space=pltpu.SMEM)


def shape(dims, kind):
    return jax.ShapeDtypeStruct(dims, kind)


def run_forward(lens, seq, gain, shift, wqkv, qkv_bias, wout, out_bias, slots):
    pairs, rows, width = seq.shape
    seq_shape = shape((pairs, rows, width), BF16)
    every = pairs * rows
    return pl.pallas_call(
        functools.partial(forward_kernel, slots),
        out_shape=[seq_shape] * 4 + [shape((every, width), F32)],
        in_specs=[smem_spec()] + [whole_spec()] * 7,
        out_specs=[whole_spec()] * 5,
        compiler_params=pltpu.CompilerParams(vmem_limit_bytes=VMEM_LIMIT),
        cost_estimate=pl.CostEstimate(
            flops=2 * every * width * width * 4 + 8 * every * rows * width,
            bytes_accessed=12 * 2**20,
            transcendentals=every * rows * HEADS,
        ),
        name="attention_forward",
    )(lens, seq, gain, shift, wqkv, qkv_bias, wout, out_bias)


def run_feed(lens, hidden, cot, gain, shift, wh, hbias, wd, dbias, pairs, slots, chunks):
    every, width = hidden.shape
    ff = wh.shape[1]
    size = ff // chunks
    fixed = lambda dims: pl.BlockSpec(dims, lambda c: (0, 0))
    columns = lambda r: pl.BlockSpec((r, size), lambda c: (0, c))
    rows = pl.BlockSpec((size, width), lambda c: (c, 0))
    return pl.pallas_call(
        functools.partial(feed_kernel, pairs, slots),
        grid=(chunks,),
        out_shape=[
            shape((every, width), BF16),
            shape((every, width), F32),
            shape((width, ff), BF16),
            shape((ff, width), BF16),
            shape((1, ff), F32),
            shape((8, width), F32),
        ],
        in_specs=[
            smem_spec(),
            fixed((every, width)),
            fixed((every, width)),
            fixed((1, width)),
            fixed((1, width)),
            columns(width),
            columns(1),
            rows,
            fixed((1, width)),
        ],
        out_specs=[
            fixed((every, width)),
            fixed((every, width)),
            columns(width),
            rows,
            columns(1),
            fixed((8, width)),
        ],
        scratch_shapes=[
            pltpu.VMEM((every, width), BF16),
            pltpu.VMEM((every, width), BF16),
            pltpu.VMEM((every, width), F32),
            pltpu.VMEM((every, width), F32),
        ],
        compiler_params=pltpu.CompilerParams(vmem_limit_bytes=VMEM_LIMIT),
        cost_estimate=pl.CostEstimate(
            flops=12 * every * width * ff,
            bytes_accessed=24 * 2**20,
            transcendentals=2 * every * ff,
        ),
        name="feed_forward",
    )(lens, hidden, cot, gain, shift, wh, hbias, wd, dbias)


def run_backward(lens, seq, gain, shift, q, k, v, mixed, ghidden, wqkv, wout, slots):
    pairs, rows, width = seq.shape
    every = pairs * rows
    return pl.pallas_call(
        functools.partial(backward_kernel, slots),
        out_shape=[
            shape((pairs, rows, width), BF16),
            shape((width, 4 * width), BF16),
            shape((8, width), F32),
        ],
        in_specs=[smem_spec()] + [whole_spec()] * 10,
        out_specs=[whole_spec()] * 3,
        scratch_shapes=[
            pltpu.VMEM((pairs, rows, width), BF16),
            pltpu.VMEM((pairs, rows, 3 * width), BF16),
        ],
        compiler_params=pltpu.CompilerParams(vmem_limit_bytes=VMEM_LIMIT),
        cost_estimate=pl.CostEstimate(
            flops=4 * every * width * width * 4 + 20 * every * rows * width,
            bytes_accessed=20 * 2**20,
            transcendentals=every * rows * HEADS,
        ),
        name="attention_backward",
    )(lens, seq, gain, shift, q, k, v, mixed, ghidden, wqkv, wout)


def pair_bits():
    return lax.axis_size("pairs").bit_length() - 1


def swapped(array, axis, bit):
    size = lax.axis_size(axis)
    return lax.ppermute(array, axis, [(i, i ^ (1 << bit)) for i in range(size)])


def split_dims(array):
    bits = pair_bits() + 1
    return array.reshape((2,) * bits + (array.shape[0] >> bits,) + array.shape[1:])


def stage_orders():
    bits = pair_bits()
    ring = ["mod", 1, 2]
    orders = []
    for turn in range(3):
        orders.append([0] + ring[turn:] + ring[:turn] + list(range(3, bits)))
    return orders


def half_sum(array, names, name, last):
    axis, bit = ("mod", 0) if name == "mod" else ("pairs", name)
    mine = (lax.axis_index(axis) >> bit) & 1
    dim = names.index(name)
    sent = lax.dynamic_index_in_dim(array, 1 - mine, dim, keepdims=False)
    kept = lax.dynamic_index_in_dim(array, mine, dim, keepdims=False)
    came = swapped(sent, axis, bit)
    total = kept.astype(F32) + came.astype(F32)
    return (total if last else total.astype(BF16)), names[:dim] + names[dim + 1 :]


def scattered(array):
    width = array.shape[1]
    names0 = list(range(pair_bits() - 1, -1, -1)) + ["mod"]
    first, names1 = half_sum(split_dims(array), names0, 0, False)
    third = -(-width // 3 // 128) * 128
    pieces = []
    for turn, order in enumerate(stage_orders()):
        piece = first[..., turn * third : min(width, (turn + 1) * third)]
        names = list(names1)
        for place, name in enumerate(order[1:]):
            piece, names = half_sum(piece, names, name, place == len(order) - 2)
        pieces.append(piece)
    return jnp.concatenate(pieces, axis=1)


def on_device(
    inputs,
    cotangent,
    text_len,
    patch_count,
    norm1_gain,
    norm1_bias,
    qkv_weight,
    query_bias,
    value_bias,
    out_weight,
    out_bias,
    norm2_gain,
    norm2_bias,
    hidden_weight,
    hidden_bias,
    down_weight,
    down_bias,
):
    _, group, slots, width = inputs.shape
    half = group // 2
    rows = padded(TEXT + slots)
    mod = lax.axis_index("mod")
    is_text = mod == 0
    lens = lax.dynamic_slice_in_dim(jnp.stack([text_len, patch_count]), mod * half, half, 1)
    lens = lens.reshape(-1)

    def gathered(array):
        local = array[0]
        patches = lax.ppermute(local[:half], "mod", [(1, 0)])
        texts = lax.ppermute(local[half:, :TEXT], "mod", [(0, 1)])
        patches = jnp.where(is_text, patches, local[half:])
        texts = jnp.where(is_text, local[:half, :TEXT], texts)
        blank = jnp.zeros((half, rows - slots - TEXT, width), array.dtype)
        return jnp.concatenate([patches, texts, blank], axis=1)

    def returned(array):
        patches, texts = array[:, :slots], array[:, slots : slots + TEXT]
        far_patches = lax.ppermute(patches, "mod", [(0, 1)])
        far_texts = lax.ppermute(texts, "mod", [(1, 0)])
        texts = jnp.concatenate([texts, far_texts], axis=0)
        texts = jnp.pad(texts, ((0, 0), (0, slots - TEXT), (0, 0)))
        patches = jnp.concatenate([far_patches, patches], axis=0)
        return jnp.where(is_text, texts, patches)[None]

    row = lambda vector: vector.reshape(1, -1)
    seq = gathered(inputs)
    cot = gathered(cotangent)
    qkv_bias = row(jnp.concatenate([query_bias, jnp.zeros_like(query_bias), value_bias]))
    q, k, v, mixed, hidden = run_forward(
        lens, seq, row(norm1_gain), row(norm1_bias), qkv_weight, qkv_bias, out_weight, row(out_bias), slots
    )
    result, ghidden, wh_grad, wd_grad, hb_grad, vec2 = run_feed(
        lens,
        hidden,
        cot.reshape(half * rows, width),
        row(norm2_gain),
        row(norm2_bias),
        hidden_weight,
        row(hidden_bias),
        down_weight,
        row(down_bias),
        half,
        slots,
        8,
    )
    block_out = returned(result.reshape(half, rows, width))
    wd_out = scattered(wd_grad)
    wh_out = scattered(wh_grad)
    input_rows, qkvo_grad, vec1 = run_backward(
        lens, seq, row(norm1_gain), row(norm1_bias), q, k, v, mixed, ghidden, qkv_weight, out_weight, slots
    )
    input_grad = returned(input_rows)
    strip = jnp.concatenate([vec1[:4], vec2[:4]], axis=0).T
    strip = jnp.concatenate([strip, hb_grad.reshape(width, -1)], axis=1).astype(BF16)
    strip = jnp.pad(strip, ((0, 0), (0, 128 - strip.shape[1])))
    qkvo_out = scattered(jnp.concatenate([qkvo_grad, strip], axis=1))
    vec_out = qkvo_out[:, 4 * width :]
    return (
        block_out,
        input_grad,
        vec_out[:, 0],
        vec_out[:, 1],
        qkvo_out[:, : 3 * width],
        vec_out[:, 2],
        vec_out[:, 3],
        qkvo_out[:, 3 * width : 4 * width],
        vec_out[:, 7],
        vec_out[:, 4],
        vec_out[:, 5],
        wh_out,
        vec_out[:, 8 : 8 + hidden_bias.shape[0] // width].reshape(-1),
        wd_out,
        vec_out[:, 6],
    )


def solution(mesh):
    whole = P()
    split = P("mod", "pairs", None, None)
    vector = P(("pairs", "mod"))
    matrix = P(("pairs", "mod"), None)
    return jax.shard_map(
        on_device,
        mesh=mesh,
        in_specs=(split, split, P("pairs"), P("pairs")) + (whole,) * 13,
        out_specs=(
            split,
            split,
            vector,
            vector,
            matrix,
            vector,
            vector,
            matrix,
            vector,
            vector,
            vector,
            matrix,
            vector,
            matrix,
            vector,
        ),
        check_vma=False,
    )
```

time: 790 us -> 275 us (0.35)
  waiting for transfers between devices: 428 us -> 83.4 us
  matrix products: 159 us -> 0 us
  Pallas kernels: 0 us -> 76 us
  starting transfers between devices: 4.87 us -> 64.4 us
  other arithmetic: 67 us -> 19.3 us
  blocking collectives: 42.4 us -> 0 us
  local copies, waits for them, and re-layouts: 69.4 us -> 29.5 us
  between operations: 14.4 us -> 1.61 us
    reduce_scatter x4 -> x0, waiting for transfers between devices: 330 us -> none  [the longest x1 142 us: layer(): lax.psum_scatter(down_weight_grad, ('pairs', 'mod'), scatter_dimension=0,...]
    dot_general x18 -> x0, matrix products: 159 us -> none  [the longest x1 35.3 us: layer(): jnp.dot(normal2, hidden_weight, preferred_element_type=jnp.float32)]
    pallas_call x0 -> x3, Pallas kernels: none -> 76 us  [the longest x1 32 us: run_feed(): pl.pallas_call(functools.partial(feed_kernel, pairs, slots), grid=(chunks...]
    ppermute x2 -> x47, starting transfers between devices: 4.71 us -> 64.4 us  [the longest x39 46.9 us: swapped(): return lax.ppermute(array, axis, [(i, i ^ 1 << bit) for i in range(size)])]
    unnamed x1 -> x0, blocking collectives: 42.4 us -> none
    convert_element_type x10 -> x30, other arithmetic: 39.8 us -> 7.38 us  [half_sum(): total.astype(BF16)]
    unnamed x97 -> x34, local copies, waits for them, and re-layouts: 19.5 us -> 0.29 us
    reduce_sum x7 -> x0, other arithmetic: 17.6 us -> none  [the longest x1 8.24 us: layer(): totals = jnp.sum(shifted, axis=-1, keepdims=True)]
  transfers between devices with their start and end apart: 6 -> 47, of which waited for: 5 -> 24; matrix products, arithmetic and copies ran while one was open for 13% -> 13% of each run, Pallas kernels for 0% -> 0%
where the time goes in v1:
time: 275 us; the launch traced here: 274 us
  waiting for transfers between devices  83.4 us (30%)
  Pallas kernels  76 us (28%)
  starting transfers between devices  64.4 us (23%)
  local copies, waits for them, and re-layouts  29.5 us (11%)
  other arithmetic  19.3 us (7%)
    ppermute x39, starting transfers between devices, swapped(): return lax.ppermute(array, axis, [(i, i ^ 1 << bit) for i in range(size)])  46.9 us
    ppermute x39, waiting for transfers between devices, swapped(): return lax.ppermute(array, axis, [(i, i ^ 1 << bit) for i in range(size)])  40.5 us
    pallas_call x1, Pallas kernels, run_feed(): pl.pallas_call(functools.partial(feed_kernel, pairs, slots), grid=(chunks...  32 us
    pallas_call x1, Pallas kernels, run_backward(): pl.pallas_call(functools.partial(backward_kernel, slots), out_shape=[shap...  26.9 us
    ppermute x2, waiting for transfers between devices, gathered(): patches = lax.ppermute(local[:half], 'mod', [(1, 0)])  25.1 us
    pallas_call x1, Pallas kernels, run_forward(): pl.pallas_call(functools.partial(forward_kernel, slots), out_shape=[seq_s...  17.2 us
    ppermute x2, waiting for transfers between devices, returned(): far_patches = lax.ppermute(patches, 'mod', [(0, 1)])  13.9 us
    convert_element_type x30, other arithmetic, half_sum(): total.astype(BF16)  7.38 us
  transfers between devices with their start and end apart: 47, of which 24 were waited for; matrix products, arithmetic and copies ran while one was open for 13% of the time, Pallas kernels for 0%

profile of v1, /device:TPU:0, one launch (start us, length us, event | category | flops | bytes accessed | tf_op | source)
XLA Modules:
  0.0 274.1 jit_solution(814949559949761042)
XLA Ops:
  1.9 4.9 %collective-permute-start.3 = (bf16[2,40,768]{2,1,0:T(8,128)(2,1)S(1)}, bf16[2,40,768]{2,1,0:T(8,128)(2,1)S(1)}, u32[]{:S(2)}, u32[]{:S(2)}) collective-permute-start(bf16[2,40,768]{2,1,0:T(8,128)(2,1)S(1)} %slice.163), channel_id=1, source_target_pairs={{0,1},{2,3},{4,5},{6,7},{8,9},{10,11},{12,13},{14,15},{16,17},{18,... | collective-permute-start | bytes 368648 | tf_op jit(solution)/shard_map/ppermute | solution.py:436
  9.0 2.0 slice_bitcast_fusion
  12.3 2.0 slice_bitcast_fusion.1
  20.6 11.9 %collective-permute-done.2 = bf16[2,240,768]{2,1,0:T(8,128)(2,1)} collective-permute-done((bf16[2,240,768]{2,1,0:T(8,128)(2,1)}, bf16[2,240,768]{2,1,0:T(8,128)(2,1)}, u32[]{:S(2)}, u32[]{:S(2)}) %collective-permute-start.2) | collective-permute-done | bytes 737312 | tf_op jit(solution)/shard_map/ppermute | solution.py:435
  33.7 13.2 %collective-permute-done = bf16[2,240,768]{2,1,0:T(8,128)(2,1)} collective-permute-done((bf16[2,240,768]{2,1,0:T(8,128)(2,1)}, bf16[2,240,768]{2,1,0:T(8,128)(2,1)}, u32[]{:S(2)}, u32[]{:S(2)}) %collective-permute-start) | collective-permute-done | bytes 737312 | tf_op jit(solution)/shard_map/ppermute | solution.py:435
  49.8 17.2 %attention_forward.1 = (bf16[2,288,768]{2,1,0:T(8,128)(2,1)}, bf16[2,288,768]{2,1,0:T(8,128)(2,1)}, bf16[2,288,768]{2,1,0:T(8,128)(2,1)}, bf16[2,288,768]{2,1,0:T(8,128)(2,1)}, f32[576,768]{1,0:T(8,128)}) custom-call(s32[4]{0:T(128)} %reshape.163.lens, bf16[2,288,768]{2,1,0:T(8,128)(2,1)} %get-tuple-element.68.seq, f32[1,768]{1,0:T(1,128)} %reshape.164.gain, ...), custom_call_target="tpu_custom_call" | custom-call | flops 3737124864 | bytes 12582912 | tf_op jit(solution)/shard_map/attention_forward/pallas_call | solution.py:263
  66.9 32.0 %feed_forward.1 = (bf16[576,768]{1,0:T(8,128)(2,1)}, f32[576,768]{1,0:T(8,128)}, bf16[768,3072]{1,0:T(8,128)(2,1)}, bf16[3072,768]{1,0:T(8,128)(2,1)}, f32[1,3072]{1,0:T(1,128)}, /*index=5*/f32[8,768]{1,0:T(8,128)}) custom-call(s32[4]{0:T(128)} %reshape.163.lens, f32[576,768]{1,0:T(8,128)} %get-tuple-element.29.hidden, bf16[576,768]{1,0:T(8,128)(2,1)} %bitcast.241, ...), custom_call_target="tpu_custom_call" | custom-call | flops 16307453952 | bytes 25165824 | tf_op jit(solution)/shard_map/feed_forward/pallas_call | solution.py:285
  98.9 26.9 %attention_backward.1 = (bf16[2,288,768]{2,1,0:T(8,128)(2,1)}, bf16[768,3072]{1,0:T(8,128)(2,1)}, f32[8,768]{1,0:T(8,128)}) custom-call(s32[4]{0:T(128)} %reshape.163.lens, bf16[2,288,768]{2,1,0:T(8,128)(2,1)} %get-tuple-element.68.seq, f32[1,768]{1,0:T(1,128)} %reshape.164.gain, f32[1,768]{1,0:T(1,128)} %reshape.165.shift, ...), custom_call_target="tpu_custom_call" | custom-call | flops 7983857664 | bytes 20971520 | tf_op jit(solution)/shard_map/attention_backward/pallas_call | solution.py:334
  127.9 4.3 %constant_dynamic-slice_fusion.1 = (bf16[2,2,2,1,2,96,768]{6,5,4,3,2,1,0:T(8,128)(2,1)}, bf16[2,2,2,1,2,96,768]{6,5,4,3,2,1,0:T(8,128)(2,1)S(1)}) fusion(bf16[2,2,2,2,2,96,768]{6,5,4,3,2,1,0:T(8,128)(2,1)} %bitcast.235, s32[]{:T(128)S(6)} %select_n.174, s32[]{:T(128)S(6)} %select_n.175), kind=kLoop, calls=%fused_computation.139 | loop fusion | bytes 9437192 | tf_op jit(solution)/shard_map/jit(dynamic_index_in_dim)/dynamic_slice | solution.py:385
  142.4 4.6 %collective-permute-start.5 = (bf16[2,240,768]{2,1,0:T(8,128)(2,1)S(1)}, bf16[2,240,768]{2,1,0:T(8,128)(2,1)S(1)}, u32[]{:S(2)}, u32[]{:S(2)}) collective-permute-start(bf16[2,240,768]{2,1,0:T(8,128)(2,1)S(1)} %slice.165), channel_id=1, source_target_pairs={{0,1},{2,3},{4,5},{6,7},{8,9},{10,11},{12,13},{14,15},{16,17},{18,... | collective-permute-start | bytes 2211848 | tf_op jit(solution)/shard_map/ppermute | solution.py:444
  147.0 2.7 fusion.1
  151.3 5.5 %collective-permute-done.7 = bf16[2,240,768]{2,1,0:T(8,128)(2,1)S(1)} collective-permute-done((bf16[2,240,768]{2,1,0:T(8,128)(2,1)S(1)}, bf16[2,240,768]{2,1,0:T(8,128)(2,1)S(1)}, u32[]{:S(2)}, u32[]{:S(2)}) %collective-permute-start.7) | collective-permute-done | bytes 737312 | tf_op jit(solution)/shard_map/ppermute | solution.py:444
  159.7 3.8 %collective-permute-done.4 = bf16[2,40,768]{2,1,0:T(8,128)(2,1)S(1)} collective-permute-done((bf16[2,40,768]{2,1,0:T(8,128)(2,1)S(1)}, bf16[2,40,768]{2,1,0:T(8,128)(2,1)S(1)}, u32[]{:S(2)}, u32[]{:S(2)}) %collective-permute-start.4) | collective-permute-done | bytes 122912 | tf_op jit(solution)/shard_map/ppermute | solution.py:445
  163.5 8.4 %collective-permute-done.5 = bf16[2,240,768]{2,1,0:T(8,128)(2,1)S(1)} collective-permute-done((bf16[2,240,768]{2,1,0:T(8,128)(2,1)S(1)}, bf16[2,240,768]{2,1,0:T(8,128)(2,1)S(1)}, u32[]{:S(2)}, u32[]{:S(2)}) %collective-permute-start.5) | collective-permute-done | bytes 737312 | tf_op jit(solution)/shard_map/ppermute | solution.py:444
  173.3 2.4 fusion.3
  176.0 2.5 collective-permute-start.35
  181.9 2.5 fusion.4
  186.5 2.1 collective-permute-done.35
  194.3 2.7 collective-permute-done.22
  202.6 5.3 %collective-permute-done.9 = bf16[2,2,2,24,896]{4,3,0,1,2:T(8,128)(2,1)S(1)} collective-permute-done((bf16[2,2,2,24,896]{4,3,0,1,2:T(8,128)(2,1)S(1)}, bf16[2,2,2,24,896]{4,3,0,1,2:T(8,128)(2,1)S(1)}, u32[]{:S(2)}, u32[]{:S(2)}) %collective-permute-start.9) | collective-permute-done | bytes 344096 | tf_op jit(solution)/shard_map/ppermute | solution.py:363
  213.0 2.0 collective-permute-start.10
  220.8 1.8 collective-permute-done.10
  231.4 2.4 collective-permute-start.38
  234.8 2.2 collective-permute-start.25
  237.0 3.9 %collective-permute-done.25 = bf16[24,1024]{1,0:T(8,128)(2,1)S(1)} collective-permute-done((bf16[24,1024]{1,0:T(8,128)(2,1)S(1)}, bf16[24,1024]{1,0:T(8,128)(2,1)S(1)}, u32[]{:S(2)}, u32[]{:S(2)}) %collective-permute-start.25) | collective-permute-done | bytes 49184 | tf_op jit(solution)/shard_map/ppermute | solution.py:363
  242.0 5.5 %collective-permute-done.29 = bf16[24,1024]{1,0:T(8,128)(2,1)S(1)} collective-permute-done((bf16[24,1024]{1,0:T(8,128)(2,1)S(1)}, bf16[24,1024]{1,0:T(8,128)(2,1)S(1)}, u32[]{:S(2)}, u32[]{:S(2)}) %collective-permute-start.29) | collective-permute-done | bytes 49184 | tf_op jit(solution)/shard_map/ppermute | solution.py:363
  247.5 5.0 %collective-permute-done.33 = bf16[24,1024]{1,0:T(8,128)(2,1)S(1)} collective-permute-done((bf16[24,1024]{1,0:T(8,128)(2,1)S(1)}, bf16[24,1024]{1,0:T(8,128)(2,1)S(1)}, u32[]{:S(2)}, u32[]{:S(2)}) %collective-permute-start.33) | collective-permute-done | bytes 49184 | tf_op jit(solution)/shard_map/ppermute | solution.py:363
  253.2 2.9 %collective-permute-start.12 = (bf16[24,896]{1,0:T(8,128)(2,1)S(1)}, bf16[24,896]{1,0:T(8,128)(2,1)S(1)}, u32[]{:S(2)}, u32[]{:S(2)}) collective-permute-start(bf16[24,896]{1,0:T(8,128)(2,1)S(1)} %dynamic-slice_bitcast_fusion.34), channel_id=1, source_target_pairs={{0,16},{2,18},{4,20},{6,22},{8,24},{10,26},{12,28},{14,30},{16,0},... | collective-permute-start | bytes 129032 | tf_op jit(solution)/shard_map/ppermute | solution.py:363
  260.4 2.0 collective-permute-start.15
  265.3 2.9 %collective-permute-start.16 = (bf16[24,1152]{1,0:T(8,128)(2,1)S(1)}, bf16[24,1152]{1,0:T(8,128)(2,1)S(1)}, u32[]{:S(2)}, u32[]{:S(2)}) collective-permute-start(bf16[24,1152]{1,0:T(8,128)(2,1)S(1)} %dynamic-slice_bitcast_fusion.27), channel_id=1, source_target_pairs={{0,16},{2,18},{4,20},{6,22},{8,24},{10,26},{12,28},{14,30},{16,0},... | collective-permute-start | bytes 165896 | tf_op jit(solution)/shard_map/ppermute | solution.py:363
  268.4 2.0 collective-permute-done.16
  270.4 3.0 %collective-permute-done.20 = bf16[24,1152]{1,0:T(8,128)(2,1)S(1)} collective-permute-done((bf16[24,1152]{1,0:T(8,128)(2,1)S(1)}, bf16[24,1152]{1,0:T(8,128)(2,1)S(1)}, u32[]{:S(2)}, u32[]{:S(2)}) %collective-permute-start.20) | collective-permute-done | bytes 55328 | tf_op jit(solution)/shard_map/ppermute | solution.py:363
  (229 shorter events, 80.1 us)
Async XLA Ops:
  1.9 18.7 %collective-permute-start.3 = (bf16[2,40,768]{2,1,0:T(8,128)(2,1)S(1)}, bf16[2,40,768]{2,1,0:T(8,128)(2,1)S(1)}, u32[]{:S(2)}, u32[]{:S(2)}) collective-permute-start(bf16[2,40,768]{2,1,0:T(8,128)(2,1)S(1)} %slice.163), channel_id=1, source_target_pairs={{0,1},{2,3},{4,5},{6,7},{8,9},{10,11},{12,13},{14,15},{16,17},{18,... | collective-permute-start | bytes 368648 | tf_op jit(solution)/shard_map/ppermute | solution.py:436
  7.7 12.9 %collective-permute-start.1 = (bf16[2,40,768]{2,1,0:T(8,128)(2,1)S(1)}, bf16[2,40,768]{2,1,0:T(8,128)(2,1)S(1)}, u32[]{:S(2)}, u32[]{:S(2)}) collective-permute-start(bf16[2,40,768]{2,1,0:T(8,128)(2,1)S(1)} %slice.161), channel_id=1, source_target_pairs={{0,1},{2,3},{4,5},{6,7},{8,9},{10,11},{12,13},{14,15},{16,17},{18,... | collective-permute-start | bytes 368648 | tf_op jit(solution)/shard_map/ppermute | solution.py:436
  11.0 21.6 %collective-permute-start.2 = (bf16[2,240,768]{2,1,0:T(8,128)(2,1)}, bf16[2,240,768]{2,1,0:T(8,128)(2,1)}, u32[]{:S(2)}, u32[]{:S(2)}) collective-permute-start(bf16[2,240,768]{2,1,0:T(8,128)(2,1)} %slice_bitcast_fusion), channel_id=1, source_target_pairs={{1,0},{3,2},{5,4},{7,6},{9,8},{11,10},{13,12},{15,14},{17,16},{19,... | collective-permute-start | bytes 2211848 | tf_op jit(solution)/shard_map/ppermute | solution.py:435
  14.3 32.6 %collective-permute-start = (bf16[2,240,768]{2,1,0:T(8,128)(2,1)}, bf16[2,240,768]{2,1,0:T(8,128)(2,1)}, u32[]{:S(2)}, u32[]{:S(2)}) collective-permute-start(bf16[2,240,768]{2,1,0:T(8,128)(2,1)} %slice_bitcast_fusion.1), channel_id=1, source_target_pairs={{1,0},{3,2},{5,4},{7,6},{9,8},{11,10},{13,12},{15,14},{17,16},{19,... | collective-permute-start | bytes 2211848 | tf_op jit(solution)/shard_map/ppermute | solution.py:435
  133.7 39.6 %collective-permute-start.34 = (bf16[2,2,2,2,96,768]{5,4,0,2,3,1:T(8,128)(2,1)}, bf16[2,2,2,2,96,768]{5,4,0,2,3,1:T(8,128)(2,1)}, u32[]{:S(2)}, u32[]{:S(2)}) collective-permute-start(bf16[2,2,2,2,96,768]{5,4,0,2,3,1:T(8,128)(2,1)} %bitcast.228), channel_id=1, source_target_pairs={{0,2},{2,0},{4,6},{6,4},{8,10},{10,8},{12,14},{14,12},{16,18},{18,... | collective-permute-start | bytes 7077896 | tf_op jit(solution)/shard_map/ppermute | solution.py:363
  135.8 46.1 %collective-permute-start.21 = (bf16[2,2,2,2,24,3072]{5,4,0,2,3,1:T(8,128)(2,1)}, bf16[2,2,2,2,24,3072]{5,4,0,2,3,1:T(8,128)(2,1)}, u32[]{:S(2)}, u32[]{:S(2)}) collective-permute-start(bf16[2,2,2,2,24,3072]{5,4,0,2,3,1:T(8,128)(2,1)} %bitcast.229), channel_id=1, source_target_pairs={{0,2},{2,0},{4,6},{6,4},{8,10},{10,8},{12,14},{14,12},{16,18},{18,... | collective-permute-start | bytes 7077896 | tf_op jit(solution)/shard_map/ppermute | solution.py:363
  138.6 18.2 %collective-permute-start.7 = (bf16[2,240,768]{2,1,0:T(8,128)(2,1)S(1)}, bf16[2,240,768]{2,1,0:T(8,128)(2,1)S(1)}, u32[]{:S(2)}, u32[]{:S(2)}) collective-permute-start(bf16[2,240,768]{2,1,0:T(8,128)(2,1)S(1)} %slice.138), channel_id=1, source_target_pairs={{0,1},{2,3},{4,5},{6,7},{8,9},{10,11},{12,13},{14,15},{16,17},{18,... | collective-permute-start | bytes 2211848 | tf_op jit(solution)/shard_map/ppermute | solution.py:444
  140.0 11.2 %collective-permute-start.6 = (bf16[2,40,768]{2,1,0:T(8,128)(2,1)S(1)}, bf16[2,40,768]{2,1,0:T(8,128)(2,1)S(1)}, u32[]{:S(2)}, u32[]{:S(2)}) collective-permute-start(bf16[2,40,768]{2,1,0:T(8,128)(2,1)S(1)} %slice.137), channel_id=1, source_target_pairs={{1,0},{3,2},{5,4},{7,6},{9,8},{11,10},{13,12},{15,14},{17,16},{19,... | collective-permute-start | bytes 368648 | tf_op jit(solution)/shard_map/ppermute | solution.py:445
  142.4 29.5 %collective-permute-start.5 = (bf16[2,240,768]{2,1,0:T(8,128)(2,1)S(1)}, bf16[2,240,768]{2,1,0:T(8,128)(2,1)S(1)}, u32[]{:S(2)}, u32[]{:S(2)}) collective-permute-start(bf16[2,240,768]{2,1,0:T(8,128)(2,1)S(1)} %slice.165), channel_id=1, source_target_pairs={{0,1},{2,3},{4,5},{6,7},{8,9},{10,11},{12,13},{14,15},{16,17},{18,... | collective-permute-start | bytes 2211848 | tf_op jit(solution)/shard_map/ppermute | solution.py:444
  151.2 33.7 %collective-permute-start.8 = (bf16[2,2,2,2,24,3200]{5,4,0,2,3,1:T(8,128)(2,1)S(1)}, bf16[2,2,2,2,24,3200]{5,4,0,2,3,1:T(8,128)(2,1)S(1)}, u32[]{:S(2)}, u32[]{:S(2)}) collective-permute-start(bf16[2,2,2,2,24,3200]{5,4,0,2,3,1:T(8,128)(2,1)S(1)} %bitcast.236), channel_id=1, source_target_pairs={{0,2},{2,0},{4,6},{6,4},{8,10},{10,8},{12,14},{14,12},{16,18},{18,... | collective-permute-start | bytes 7372808 | tf_op jit(solution)/shard_map/ppermute | solution.py:363
  156.8 6.8 %collective-permute-start.4 = (bf16[2,40,768]{2,1,0:T(8,128)(2,1)S(1)}, bf16[2,40,768]{2,1,0:T(8,128)(2,1)S(1)}, u32[]{:S(2)}, u32[]{:S(2)}) collective-permute-start(bf16[2,40,768]{2,1,0:T(8,128)(2,1)S(1)} %slice.164), channel_id=1, source_target_pairs={{1,0},{3,2},{5,4},{7,6},{9,8},{11,10},{13,12},{15,14},{17,16},{19,... | collective-permute-start | bytes 368648 | tf_op jit(solution)/shard_map/ppermute | solution.py:445
  176.0 12.5 %collective-permute-start.35 = (bf16[2,2,2,96,256]{4,3,0,2,1:T(8,128)(2,1)S(1)}, bf16[2,2,2,96,256]{4,3,0,2,1:T(8,128)(2,1)S(1)}, u32[]{:S(2)}, u32[]{:S(2)}) collective-permute-start(bf16[2,2,2,96,256]{4,3,0,2,1:T(8,128)(2,1)S(1)} %dynamic-slice_bitcast_fusion.3), channel_id=1, source_target_pairs={{0,1},{1,0},{2,3},{3,2},{4,5},{5,4},{6,7},{7,6},{8,9},{9,8},{10,11... | collective-permute-start | bytes 1179656 | tf_op jit(solution)/shard_map/ppermute | solution.py:363
  178.6 12.1 %collective-permute-start.39 = (bf16[2,2,2,96,256]{4,3,0,2,1:T(8,128)(2,1)S(1)}, bf16[2,2,2,96,256]{4,3,0,2,1:T(8,128)(2,1)S(1)}, u32[]{:S(2)}, u32[]{:S(2)}) collective-permute-start(bf16[2,2,2,96,256]{4,3,0,2,1:T(8,128)(2,1)S(1)} %dynamic-slice_bitcast_fusion.2), channel_id=1, source_target_pairs={{0,4},{2,6},{4,0},{6,2},{8,12},{10,14},{12,8},{14,10},{16,20},{18,... | collective-permute-start | bytes 1179656 | tf_op jit(solution)/shard_map/ppermute | solution.py:363
  180.3 12.3 %collective-permute-start.43 = (bf16[2,2,2,96,256]{4,3,0,1,2:T(8,128)(2,1)S(1)}, bf16[2,2,2,96,256]{4,3,0,1,2:T(8,128)(2,1)S(1)}, u32[]{:S(2)}, u32[]{:S(2)}) collective-permute-start(bf16[2,2,2,96,256]{4,3,0,1,2:T(8,128)(2,1)S(1)} %dynamic-slice_bitcast_fusion.1), channel_id=1, source_target_pairs={{0,8},{2,10},{4,12},{6,14},{8,0},{10,2},{12,4},{14,6},{16,24},{18,... | collective-permute-start | bytes 1179656 | tf_op jit(solution)/shard_map/ppermute | solution.py:363
  184.7 12.3 %collective-permute-start.22 = (bf16[2,2,2,24,1024]{4,3,0,2,1:T(8,128)(2,1)S(1)}, bf16[2,2,2,24,1024]{4,3,0,2,1:T(8,128)(2,1)S(1)}, u32[]{:S(2)}, u32[]{:S(2)}) collective-permute-start(bf16[2,2,2,24,1024]{4,3,0,2,1:T(8,128)(2,1)S(1)} %dynamic-slice_bitcast_fusion.6), channel_id=1, source_target_pairs={{0,1},{1,0},{2,3},{3,2},{4,5},{5,4},{6,7},{7,6},{8,9},{9,8},{10,11... | collective-permute-start | bytes 1179656 | tf_op jit(solution)/shard_map/ppermute | solution.py:363
  184.9 14.2 %collective-permute-start.26 = (bf16[2,2,2,24,1024]{4,3,0,2,1:T(8,128)(2,1)S(1)}, bf16[2,2,2,24,1024]{4,3,0,2,1:T(8,128)(2,1)S(1)}, u32[]{:S(2)}, u32[]{:S(2)}) collective-permute-start(bf16[2,2,2,24,1024]{4,3,0,2,1:T(8,128)(2,1)S(1)} %dynamic-slice_bitcast_fusion.5), channel_id=1, source_target_pairs={{0,4},{2,6},{4,0},{6,2},{8,12},{10,14},{12,8},{14,10},{16,20},{18,... | collective-permute-start | bytes 1179656 | tf_op jit(solution)/shard_map/ppermute | solution.py:363
  188.5 12.3 %collective-permute-start.30 = (bf16[2,2,2,24,1024]{4,3,0,1,2:T(8,128)(2,1)S(1)}, bf16[2,2,2,24,1024]{4,3,0,1,2:T(8,128)(2,1)S(1)}, u32[]{:S(2)}, u32[]{:S(2)}) collective-permute-start(bf16[2,2,2,24,1024]{4,3,0,1,2:T(8,128)(2,1)S(1)} %dynamic-slice_bitcast_fusion.4), channel_id=1, source_target_pairs={{0,8},{2,10},{4,12},{6,14},{8,0},{10,2},{12,4},{14,6},{16,24},{18,... | collective-permute-start | bytes 1179656 | tf_op jit(solution)/shard_map/ppermute | solution.py:363
  190.7 17.9 %collective-permute-start.13 = (bf16[2,2,2,24,1152]{4,3,0,1,2:T(8,128)(2,1)S(1)}, bf16[2,2,2,24,1152]{4,3,0,1,2:T(8,128)(2,1)S(1)}, u32[]{:S(2)}, u32[]{:S(2)}) collective-permute-start(bf16[2,2,2,24,1152]{4,3,0,1,2:T(8,128)(2,1)S(1)} %bitcast.244), channel_id=1, source_target_pairs={{0,1},{1,0},{2,3},{3,2},{4,5},{5,4},{6,7},{7,6},{8,9},{9,8},{10,11... | collective-permute-start | bytes 1327112 | tf_op jit(solution)/shard_map/ppermute | solution.py:363
  192.5 17.5 %collective-permute-start.17 = (bf16[2,2,2,24,1152]{4,3,0,2,1:T(8,128)(2,1)S(1)}, bf16[2,2,2,24,1152]{4,3,0,2,1:T(8,128)(2,1)S(1)}, u32[]{:S(2)}, u32[]{:S(2)}) collective-permute-start(bf16[2,2,2,24,1152]{4,3,0,2,1:T(8,128)(2,1)S(1)} %dynamic-slice_bitcast_fusion), channel_id=1, source_target_pairs={{0,4},{2,6},{4,0},{6,2},{8,12},{10,14},{12,8},{14,10},{16,20},{18,... | collective-permute-start | bytes 1327112 | tf_op jit(solution)/shard_map/ppermute | solution.py:363
  197.0 10.9 %collective-permute-start.9 = (bf16[2,2,2,24,896]{4,3,0,1,2:T(8,128)(2,1)S(1)}, bf16[2,2,2,24,896]{4,3,0,1,2:T(8,128)(2,1)S(1)}, u32[]{:S(2)}, u32[]{:S(2)}) collective-permute-start(bf16[2,2,2,24,896]{4,3,0,1,2:T(8,128)(2,1)S(1)} %dynamic-slice_bitcast_fusion.7), channel_id=1, source_target_pairs={{0,8},{2,10},{4,12},{6,14},{8,0},{10,2},{12,4},{14,6},{16,24},{18,... | collective-permute-start | bytes 1032200 | tf_op jit(solution)/shard_map/ppermute | solution.py:363
  199.1 13.7 %collective-permute-start.36 = (bf16[2,2,96,256]{3,2,0,1:T(8,128)(2,1)S(1)}, bf16[2,2,96,256]{3,2,0,1:T(8,128)(2,1)S(1)}, u32[]{:S(2)}, u32[]{:S(2)}) collective-permute-start(bf16[2,2,96,256]{3,2,0,1:T(8,128)(2,1)S(1)} %dynamic-slice_bitcast_fusion.12), channel_id=1, source_target_pairs={{0,4},{2,6},{4,0},{6,2},{8,12},{10,14},{12,8},{14,10},{16,20},{18,... | collective-permute-start | bytes 589832 | tf_op jit(solution)/shard_map/ppermute | solution.py:363
  200.8 12.1 %collective-permute-start.40 = (bf16[2,2,96,256]{3,2,0,1:T(8,128)(2,1)S(1)}, bf16[2,2,96,256]{3,2,0,1:T(8,128)(2,1)S(1)}, u32[]{:S(2)}, u32[]{:S(2)}) collective-permute-start(bf16[2,2,96,256]{3,2,0,1:T(8,128)(2,1)S(1)} %dynamic-slice_bitcast_fusion.11), channel_id=1, source_target_pairs={{0,8},{2,10},{4,12},{6,14},{8,0},{10,2},{12,4},{14,6},{16,24},{18,... | collective-permute-start | bytes 589832 | tf_op jit(solution)/shard_map/ppermute | solution.py:363
  207.9 7.4 %collective-permute-start.44 = (bf16[2,2,96,256]{3,2,0,1:T(8,128)(2,1)S(1)}, bf16[2,2,96,256]{3,2,0,1:T(8,128)(2,1)S(1)}, u32[]{:S(2)}, u32[]{:S(2)}) collective-permute-start(bf16[2,2,96,256]{3,2,0,1:T(8,128)(2,1)S(1)} %dynamic-slice_bitcast_fusion.10), channel_id=1, source_target_pairs={{0,1},{1,0},{2,3},{3,2},{4,5},{5,4},{6,7},{7,6},{8,9},{9,8},{10,11... | collective-permute-start | bytes 589832 | tf_op jit(solution)/shard_map/ppermute | solution.py:363
  208.6 8.2 %collective-permute-start.23 = (bf16[2,2,24,1024]{3,2,0,1:T(8,128)(2,1)S(1)}, bf16[2,2,24,1024]{3,2,0,1:T(8,128)(2,1)S(1)}, u32[]{:S(2)}, u32[]{:S(2)}) collective-permute-start(bf16[2,2,24,1024]{3,2,0,1:T(8,128)(2,1)S(1)} %dynamic-slice_bitcast_fusion.15), channel_id=1, source_target_pairs={{0,4},{2,6},{4,0},{6,2},{8,12},{10,14},{12,8},{14,10},{16,20},{18,... | collective-permute-start | bytes 589832 | tf_op jit(solution)/shard_map/ppermute | solution.py:363
  210.1 8.5 %collective-permute-start.27 = (bf16[2,2,24,1024]{3,2,0,1:T(8,128)(2,1)S(1)}, bf16[2,2,24,1024]{3,2,0,1:T(8,128)(2,1)S(1)}, u32[]{:S(2)}, u32[]{:S(2)}) collective-permute-start(bf16[2,2,24,1024]{3,2,0,1:T(8,128)(2,1)S(1)} %dynamic-slice_bitcast_fusion.14), channel_id=1, source_target_pairs={{0,8},{2,10},{4,12},{6,14},{8,0},{10,2},{12,4},{14,6},{16,24},{18,... | collective-permute-start | bytes 589832 | tf_op jit(solution)/shard_map/ppermute | solution.py:363
  212.8 7.8 %collective-permute-start.31 = (bf16[2,2,24,1024]{3,2,0,1:T(8,128)(2,1)S(1)}, bf16[2,2,24,1024]{3,2,0,1:T(8,128)(2,1)S(1)}, u32[]{:S(2)}, u32[]{:S(2)}) collective-permute-start(bf16[2,2,24,1024]{3,2,0,1:T(8,128)(2,1)S(1)} %dynamic-slice_bitcast_fusion.13), channel_id=1, source_target_pairs={{0,1},{1,0},{2,3},{3,2},{4,5},{5,4},{6,7},{7,6},{8,9},{9,8},{10,11... | collective-permute-start | bytes 589832 | tf_op jit(solution)/shard_map/ppermute | solution.py:363
  213.0 9.6 %collective-permute-start.10 = (bf16[2,2,24,896]{3,2,0,1:T(8,128)(2,1)S(1)}, bf16[2,2,24,896]{3,2,0,1:T(8,128)(2,1)S(1)}, u32[]{:S(2)}, u32[]{:S(2)}) collective-permute-start(bf16[2,2,24,896]{3,2,0,1:T(8,128)(2,1)S(1)} %dynamic-slice_bitcast_fusion.16), channel_id=1, source_target_pairs={{0,1},{1,0},{2,3},{3,2},{4,5},{5,4},{6,7},{7,6},{8,9},{9,8},{10,11... | collective-permute-start | bytes 516104 | tf_op jit(solution)/shard_map/ppermute | solution.py:363
  215.3 45.1 %collective-permute-start.14 = (bf16[2,2,24,1152]{3,2,0,1:T(8,128)(2,1)S(1)}, bf16[2,2,24,1152]{3,2,0,1:T(8,128)(2,1)S(1)}, u32[]{:S(2)}, u32[]{:S(2)}) collective-permute-start(bf16[2,2,24,1152]{3,2,0,1:T(8,128)(2,1)S(1)} %dynamic-slice_bitcast_fusion.9), channel_id=1, source_target_pairs={{0,4},{2,6},{4,0},{6,2},{8,12},{10,14},{12,8},{14,10},{16,20},{18,... | collective-permute-start | bytes 663560 | tf_op jit(solution)/shard_map/ppermute | solution.py:363
  216.8 45.6 %collective-permute-start.18 = (bf16[2,2,24,1152]{3,2,0,1:T(8,128)(2,1)S(1)}, bf16[2,2,24,1152]{3,2,0,1:T(8,128)(2,1)S(1)}, u32[]{:S(2)}, u32[]{:S(2)}) collective-permute-start(bf16[2,2,24,1152]{3,2,0,1:T(8,128)(2,1)S(1)} %dynamic-slice_bitcast_fusion.8), channel_id=1, source_target_pairs={{0,8},{2,10},{4,12},{6,14},{8,0},{10,2},{12,4},{14,6},{16,24},{18,... | collective-permute-start | bytes 663560 | tf_op jit(solution)/shard_map/ppermute | solution.py:363
  231.4 21.8 %collective-permute-start.38 = (bf16[96,256]{1,0:T(8,128)(2,1)S(1)}, bf16[96,256]{1,0:T(8,128)(2,1)S(1)}, u32[]{:S(2)}, u32[]{:S(2)}) collective-permute-start(bf16[96,256]{1,0:T(8,128)(2,1)S(1)} %dynamic-slice_bitcast_fusion.30), channel_id=1, source_target_pairs={{0,16},{2,18},{4,20},{6,22},{8,24},{10,26},{12,28},{14,30},{16,0},... | collective-permute-start | bytes 147464 | tf_op jit(solution)/shard_map/ppermute | solution.py:363
  233.8 22.3 %collective-permute-start.42 = (bf16[96,256]{1,0:T(8,128)(2,1)S(1)}, bf16[96,256]{1,0:T(8,128)(2,1)S(1)}, u32[]{:S(2)}, u32[]{:S(2)}) collective-permute-start(bf16[96,256]{1,0:T(8,128)(2,1)S(1)} %dynamic-slice_bitcast_fusion.29), channel_id=1, source_target_pairs={{0,16},{2,18},{4,20},{6,22},{8,24},{10,26},{12,28},{14,30},{16,0},... | collective-permute-start | bytes 147464 | tf_op jit(solution)/shard_map/ppermute | solution.py:363
  240.9 6.5 %collective-permute-start.29 = (bf16[24,1024]{1,0:T(8,128)(2,1)S(1)}, bf16[24,1024]{1,0:T(8,128)(2,1)S(1)}, u32[]{:S(2)}, u32[]{:S(2)}) collective-permute-start(bf16[24,1024]{1,0:T(8,128)(2,1)S(1)} %dynamic-slice_bitcast_fusion.32), channel_id=1, source_target_pairs={{0,16},{2,18},{4,20},{6,22},{8,24},{10,26},{12,28},{14,30},{16,0},... | collective-permute-start | bytes 147464 | tf_op jit(solution)/shard_map/ppermute | solution.py:363
  (31 other events, 317.0 us)

commit v2 on v1

--- a/solution.py
+++ b/solution.py
@@ -111,6 +111,7 @@
     hbias,
     wd,
     dbias,
+    order,
     result,
     grad_hidden,
     wh_grad,
@@ -118,6 +119,7 @@
     hb_grad,
     vectors,
     normal,
+    ordered,
     gdown,
     total,
     gnormal,
@@ -130,7 +132,9 @@
     @pl.when(chunk == 0)
     def _():
         normed, _ = norm_parts(hidden[...])
-        normal[...] = (normed * gain[...] + shift[...]).astype(BF16)
+        made = (normed * gain[...] + shift[...]).astype(BF16)
+        normal[...] = made
+        ordered[...] = dot(made, order[...]).astype(BF16)
         gdown[...] = (cot[...].astype(F32) * live).astype(BF16)
         total[...] = hidden[...] + dbias[...]
         gnormal[...] = jnp.zeros_like(gnormal)
@@ -139,10 +143,20 @@
     active, slope = gelu_parts(before)
     active = active.astype(BF16)
     total[...] += dot(active, wd[...])
-    wd_grad[...] = dot(active, gdown[...], 0, 0).astype(BF16)
+    fresh = dot(active, gdown[...], 0, 0)
+    if wd_grad.ndim == 2:
+        wd_grad[...] = fresh.astype(BF16)
+    else:
+        size = fresh.shape[0] // 4
+        base = 2 * pairs
+        for core in range(2):
+            for mod in range(2):
+                start = (2 * core + mod) * size
+                piece = fresh[start : start + size].reshape(size // 8, 8, fresh.shape[1])
+                wd_grad[lens[base + core], 0, 0, lens[base + 2 + mod], 0] = piece.astype(BF16)
     gbefore = (dot(gdown[...], wd[...], 1, 1) * slope).astype(BF16)
     gnormal[...] += dot(gbefore, wh[...], 1, 1)
-    wh_grad[...] = dot(normal[...], gbefore, 0, 0).astype(BF16)
+    wh_grad[...] = dot(ordered[...], gbefore, 0, 0).reshape(wh_grad.shape).astype(BF16)
     hb_grad[...] = jnp.sum(gbefore.astype(F32), axis=0, keepdims=True)
 
     @pl.when(chunk == count - 1)
@@ -172,6 +186,7 @@
     ghidden,
     wqkv,
     wout,
+    order,
     input_grad,
     weight_grad,
     vectors,
@@ -182,9 +197,14 @@
     every = pairs * rows
     gattended = ghidden[...].astype(BF16)
     gmixed[...] = dot(gattended, wout[...], 1, 1).astype(BF16).reshape(pairs, rows, width)
-    weight_grad[:, 3 * width : 4 * width] = dot(
-        mixed[...].reshape(every, width), gattended, 0, 0
-    ).astype(BF16)
+    ordered = dot(mixed[...].reshape(every, width), order[...]).astype(BF16)
+
+    def put(first, last, value):
+        target = (slice(None),) * (len(weight_grad.shape) - 1) + (slice(first, last),)
+        value = value.reshape(weight_grad.shape[:-1] + (last - first,))
+        weight_grad[target] = value.astype(BF16)
+
+    put(3 * width, 4 * width, dot(ordered, gattended, 0, 0))
     first = lax.broadcasted_iota(jnp.int32, (rows, 128), 1) < HEAD_DIM
     index = lax.broadcasted_iota(jnp.int32, (rows, 1), 0)
     groups = width // 128
@@ -227,12 +247,13 @@
     tokens = seq[...].reshape(every, width).astype(F32)
     normed, factor = norm_parts(tokens)
     normal = (normed * gain[...] + shift[...]).astype(BF16)
+    ordered = dot(normal, order[...]).astype(BF16)
     gnormal = jnp.zeros((every, width), F32)
     for part in range(3):
         cols = slice(part * width, (part + 1) * width)
         piece = gproj[:, :, cols].reshape(every, width)
         gnormal += dot(piece, wqkv[:, cols], 1, 1)
-        weight_grad[:, cols] = dot(normal, piece, 0, 0).astype(BF16)
+        put(part * width, (part + 1) * width, dot(ordered, piece, 0, 0))
         if part == 0:
             vectors[2:3, :] = jnp.sum(piece.astype(F32), axis=0, keepdims=True)
         if part == 2:
@@ -275,26 +296,40 @@
     )(lens, seq, gain, shift, wqkv, qkv_bias, wout, out_bias)
 
 
-def run_feed(lens, hidden, cot, gain, shift, wh, hbias, wd, dbias, pairs, slots, chunks):
+def run_feed(lens, hidden, cot, gain, shift, wh, hbias, wd, dbias, order, pairs, slots, chunks, relative):
     every, width = hidden.shape
     ff = wh.shape[1]
     size = ff // chunks
-    fixed = lambda dims: pl.BlockSpec(dims, lambda c: (0, 0))
-    columns = lambda r: pl.BlockSpec((r, size), lambda c: (0, c))
-    rows = pl.BlockSpec((size, width), lambda c: (c, 0))
+    base = 2 * pairs + 4
+    fixed = lambda dims: pl.BlockSpec(dims, lambda c, s: (0, 0))
+    columns = lambda r: pl.BlockSpec((r, size), lambda c, s: (0, s[base + c]))
+    rows = pl.BlockSpec((size, width), lambda c, s: (s[base + c], 0))
+    if relative:
+        part = size // 4 // 8
+        wd_shape = shape((2, 2, 2, 2, 2, part, 8, width), BF16)
+        wd_spec = pl.BlockSpec(
+            (2, 1, 1, 2, 1, part, 8, width),
+            lambda c, s: (0, c % 2, c // 2 % 2, 0, c // 4, 0, 0, 0),
+        )
+        wh_shape = shape((width // 8, 8, ff), BF16)
+        wh_spec = pl.BlockSpec((width // 8, 8, size), lambda c, s: (0, 0, s[base + c]))
+    else:
+        wd_shape, wd_spec = shape((ff, width), BF16), rows
+        wh_shape, wh_spec = shape((width, ff), BF16), columns(width)
     return pl.pallas_call(
         functools.partial(feed_kernel, pairs, slots),
-        grid=(chunks,),
         out_shape=[
             shape((every, width), BF16),
             shape((every, width), F32),
-            shape((width, ff), BF16),
-            shape((ff, width), BF16),
+            wh_shape,
+            wd_shape,
             shape((1, ff), F32),
             shape((8, width), F32),
         ],
+        grid_spec=pltpu.PrefetchScalarGridSpec(
+        num_scalar_prefetch=1,
+        grid=(chunks,),
         in_specs=[
-            smem_spec(),
             fixed((every, width)),
             fixed((every, width)),
             fixed((1, width)),
@@ -303,21 +338,24 @@
             columns(1),
             rows,
             fixed((1, width)),
+            fixed((width, width)),
         ],
         out_specs=[
             fixed((every, width)),
             fixed((every, width)),
-            columns(width),
-            rows,
+            wh_spec,
+            wd_spec,
             columns(1),
             fixed((8, width)),
         ],
         scratch_shapes=[
             pltpu.VMEM((every, width), BF16),
             pltpu.VMEM((every, width), BF16),
+            pltpu.VMEM((every, width), BF16),
             pltpu.VMEM((every, width), F32),
             pltpu.VMEM((every, width), F32),
         ],
+        ),
         compiler_params=pltpu.CompilerParams(vmem_limit_bytes=VMEM_LIMIT),
         cost_estimate=pl.CostEstimate(
             flops=12 * every * width * ff,
@@ -325,20 +363,20 @@
             transcendentals=2 * every * ff,
         ),
         name="feed_forward",
-    )(lens, hidden, cot, gain, shift, wh, hbias, wd, dbias)
-
-
-def run_backward(lens, seq, gain, shift, q, k, v, mixed, ghidden, wqkv, wout, slots):
+    )(lens, hidden, cot, gain, shift, wh, hbias, wd, dbias, order)
+
+
+def run_backward(lens, seq, gain, shift, q, k, v, mixed, ghidden, wqkv, wout, order, slots, relative):
     pairs, rows, width = seq.shape
     every = pairs * rows
     return pl.pallas_call(
         functools.partial(backward_kernel, slots),
         out_shape=[
             shape((pairs, rows, width), BF16),
-            shape((width, 4 * width), BF16),
+            shape((width // 8, 8, 4 * width) if relative else (width, 4 * width), BF16),
             shape((8, width), F32),
         ],
-        in_specs=[smem_spec()] + [whole_spec()] * 10,
+        in_specs=[smem_spec()] + [whole_spec()] * 11,
         out_specs=[whole_spec()] * 3,
         scratch_shapes=[
             pltpu.VMEM((pairs, rows, width), BF16),
@@ -351,7 +389,145 @@
             transcendentals=every * rows * HEADS,
         ),
         name="attention_backward",
-    )(lens, seq, gain, shift, q, k, v, mixed, ghidden, wqkv, wout)
+    )(lens, seq, gain, shift, q, k, v, mixed, ghidden, wqkv, wout, order)
+
+
+BITS = ("core", "y", "z0", "x", "z1")
+ORDERS = (("core", "y", "z0", "x", "z1"), ("core", "z0", "y", "x", "z1"))
+
+
+def partner(bit):
+    if bit == "x":
+        return {"mod": 1 - lax.axis_index("mod")}
+    size = {"core": 1, "y": 2, "z0": 4, "z1": 8}[bit]
+    me = lax.axis_index("pairs")
+    return {"pairs": me + size - 2 * size * (me // size % 2)}
+
+
+def narrowed(ref, names, bit, value):
+    dim = names.index(bit)
+    index = (slice(None),) * dim + (value,)
+    return ref.at[index], names[:dim] + names[dim + 1 :]
+
+
+def piece_shapes(rows8, cols):
+    return [(2,) * (4 - step) + (rows8, 8, cols) for step in range(5)]
+
+
+def add_into(target, source):
+    lead = target.shape[:-3]
+    count = 1
+    for size in lead:
+        count *= size
+
+    def body(it, carry):
+        index = []
+        left = it
+        for size in reversed(lead):
+            index.insert(0, left % size)
+            left = left // size
+        index = tuple(index)
+        target[index] = (target[index].astype(F32) + source[index].astype(F32)).astype(BF16)
+        return carry
+
+    if count == 1:
+        body(0, 0)
+    else:
+        lax.fori_loop(0, count, body, 0)
+
+
+def scatter_kernel(plan, counts, *refs):
+    sources = refs[: counts[0]]
+    outs = refs[counts[0] : 2 * counts[0]]
+    rest = refs[2 * counts[0] :]
+    bufs, (send_sem, recv_sem, load_sem) = rest[:-3], rest[-3:]
+    barrier = pltpu.get_barrier_semaphore()
+    for bit in BITS:
+        pl.semaphore_signal(barrier, inc=1, device_id=partner(bit), device_id_type=pl.DeviceIdType.MESH)
+    pl.semaphore_wait(barrier, len(BITS))
+    copies = {}
+    loads = {}
+
+    def send(unit, step, ref):
+        bit = ORDERS[plan[unit][1]][step]
+        copy = pltpu.make_async_remote_copy(
+            src_ref=ref,
+            dst_ref=bufs[6 * unit + 1 + step],
+            send_sem=send_sem.at[5 * unit + step],
+            recv_sem=recv_sem.at[5 * unit + step],
+            device_id=partner(bit),
+            device_id_type=pl.DeviceIdType.MESH,
+        )
+        copy.start()
+        copies[unit, step] = copy
+
+    def begin(unit):
+        bucket, _, first, last = plan[unit]
+        every = (slice(None),) * 6
+        send(unit, 0, sources[bucket].at[(1,) + every + (slice(first, last),)])
+        loads[unit] = pltpu.make_async_copy(
+            sources[bucket].at[(0,) + every + (slice(first, last),)], bufs[6 * unit], load_sem.at[unit]
+        )
+        loads[unit].start()
+
+    held = {}
+
+    def advance(unit, step):
+        bucket, turn, first, last = plan[unit]
+        order = ORDERS[turn]
+        if step == 0:
+            loads[unit].wait()
+            held[unit] = (bufs[6 * unit], tuple(b for b in BITS if b != "core"))
+        copies[unit, step].wait_recv()
+        ref, names = held[unit]
+        arrived = bufs[6 * unit + 1 + step]
+        if step == 4:
+            total = ref[...].astype(F32) + arrived[...].astype(F32)
+            outs[bucket][:, :, first:last] = total
+            return
+        add_into(ref, arrived)
+        bit = order[step + 1]
+        sent, _ = narrowed(ref, names, bit, 1)
+        send(unit, step + 1, sent)
+        held[unit] = narrowed(ref, names, bit, 0)
+
+    units = len(plan)
+    for unit in range(units):
+        begin(unit)
+    for step in range(5):
+        for unit in range(units):
+            advance(unit, step)
+    for copy in copies.values():
+        copy.wait_send()
+
+
+def run_scatter(arrays, cuts):
+    plan, shapes = [], []
+    for index, array in enumerate(arrays):
+        cols, rows8 = array.shape[-1], array.shape[-3]
+        edges = [cols * place // cuts[index] // 128 * 128 for place in range(cuts[index])] + [cols]
+        for place in range(cuts[index]):
+            first, last = edges[place], edges[place + 1]
+            plan.append((index, place % 2, first, last))
+            arrivals = piece_shapes(rows8, last - first)
+            shapes += [arrivals[0]] + arrivals
+    units = len(plan)
+    return pl.pallas_call(
+        functools.partial(scatter_kernel, plan, (len(arrays),)),
+        out_shape=[shape(a.shape[-3:], F32) for a in arrays],
+        in_specs=[pl.BlockSpec(memory_space=pl.ANY)] * len(arrays),
+        out_specs=[whole_spec()] * len(arrays),
+        scratch_shapes=[pltpu.VMEM(dims, BF16) for dims in shapes]
+        + [
+            pltpu.SemaphoreType.DMA((5 * units,)),
+            pltpu.SemaphoreType.DMA((5 * units,)),
+            pltpu.SemaphoreType.DMA((units,)),
+        ],
+        compiler_params=pltpu.CompilerParams(
+            collective_id=1, has_side_effects=True, vmem_limit_bytes=VMEM_LIMIT
+        ),
+        name="scatter",
+    )(*arrays)
 
 
 def pair_bits():
@@ -449,6 +625,24 @@
         return jnp.where(is_text, texts, patches)[None]
 
     row = lambda vector: vector.reshape(1, -1)
+    chunks = 8
+    relative = lax.axis_size("pairs") == 16
+    chip = lax.axis_index("pairs") // 2
+    core = lax.axis_index("pairs") % 2
+    steps = jnp.arange(chunks, dtype=jnp.int32)
+    if relative:
+        extra = jnp.concatenate([jnp.stack([core, 1 - core, mod, 1 - mod]), steps ^ chip])
+        place = jnp.arange(width, dtype=jnp.int32)
+        block = place // (width // 32)
+        bit = lambda shift: (block >> shift) & 1
+        owner = (bit(0) << 4) + (bit(2) << 3) + (bit(3) << 2) + (bit(4) << 1) + bit(1)
+        owner = owner ^ (lax.axis_index("pairs") * 2 + mod)
+        source = owner * (width // 32) + place % (width // 32)
+    else:
+        extra = jnp.concatenate([jnp.zeros(4, jnp.int32), steps])
+        source = jnp.arange(width, dtype=jnp.int32)
+    order = (jnp.arange(width, dtype=jnp.int32)[:, None] == source[None, :]).astype(BF16)
+    lens = jnp.concatenate([lens, extra.astype(jnp.int32)])
     seq = gathered(inputs)
     cot = gathered(cotangent)
     qkv_bias = row(jnp.concatenate([query_bias, jnp.zeros_like(query_bias), value_bias]))
@@ -465,21 +659,43 @@
         row(hidden_bias),
         down_weight,
         row(down_bias),
+        order,
         half,
         slots,
-        8,
+        chunks,
+        relative,
     )
     block_out = returned(result.reshape(half, rows, width))
-    wd_out = scattered(wd_grad)
-    wh_out = scattered(wh_grad)
     input_rows, qkvo_grad, vec1 = run_backward(
-        lens, seq, row(norm1_gain), row(norm1_bias), q, k, v, mixed, ghidden, qkv_weight, out_weight, slots
+        lens,
+        seq,
+        row(norm1_gain),
+        row(norm1_bias),
+        q,
+        k,
+        v,
+        mixed,
+        ghidden,
+        qkv_weight,
+        out_weight,
+        order,
+        slots,
+        relative,
     )
     input_grad = returned(input_rows)
     strip = jnp.concatenate([vec1[:4], vec2[:4]], axis=0).T
     strip = jnp.concatenate([strip, hb_grad.reshape(width, -1)], axis=1).astype(BF16)
     strip = jnp.pad(strip, ((0, 0), (0, 128 - strip.shape[1])))
-    qkvo_out = scattered(jnp.concatenate([qkvo_grad, strip], axis=1))
+    if relative:
+        strip = dot(order, strip, 0, 0).astype(BF16).reshape(width // 8, 8, 128)
+        qkvo_grad = jnp.concatenate([qkvo_grad, strip], axis=2)
+        split = lambda array: array.reshape((2,) * 5 + (array.shape[0] // 32,) + array.shape[1:])
+        wd_out, wh_out, qkvo_out = run_scatter([wd_grad, split(wh_grad), split(qkvo_grad)], (2, 4, 4))
+        flat = lambda array: array.reshape(-1, array.shape[-1])
+        wd_out, wh_out, qkvo_out = flat(wd_out), flat(wh_out), flat(qkvo_out)
+    else:
+        wd_out, wh_out = scattered(wd_grad), scattered(wh_grad)
+        qkvo_out = scattered(jnp.concatenate([qkvo_grad, strip], axis=1))
     vec_out = qkvo_out[:, 4 * width :]
     return (
         block_out,

time: 275 us -> 256 us (0.931)
  Pallas kernels: 76 us -> 171 us
  waiting for transfers between devices: 83.4 us -> 26.8 us
  starting transfers between devices: 64.4 us -> 17.5 us
  local copies, waits for them, and re-layouts: 29.5 us -> 23.9 us
  other arithmetic: 19.3 us -> 14.1 us
    pallas_call x1 -> x2, Pallas kernels: 32 us -> 125 us  [the longest x1 91.1 us: run_scatter(): pl.pallas_call(functools.partial(scatter_kernel, plan, (len(arrays),)), o...]
    ppermute x39 -> x0, starting transfers between devices: 46.9 us -> none  [swapped(): return lax.ppermute(array, axis, [(i, i ^ 1 << bit) for i in range(size)])]
    ppermute x39 -> x0, waiting for transfers between devices: 40.5 us -> none  [swapped(): return lax.ppermute(array, axis, [(i, i ^ 1 << bit) for i in range(size)])]
    ppermute x2, waiting for transfers between devices: 13.9 us -> 0.01 us  [returned(): far_patches = lax.ppermute(patches, 'mod', [(0, 1)])]
    dynamic_slice x7 -> x0, local copies, waits for them, and re-layouts: 8.47 us -> none  [the longest x4 5.09 us: half_sum(): kept = lax.dynamic_index_in_dim(array, mine, dim, keepdims=False)]
    convert_element_type x30 -> x1, other arithmetic: 7.38 us -> 1.43 us  [on_device(): (jnp.arange(width, dtype=jnp.int32)[:, None] == source[None, :]).astype(B...]
  transfers between devices with their start and end apart: 47 -> 8, of which waited for: 24 -> 3; matrix products, arithmetic and copies ran while one was open for 13% -> 10% of each run, Pallas kernels for 0% -> 36%
where the time goes in v2:
time: 256 us; the launch traced here: 255 us
  Pallas kernels  171 us (67%)
  waiting for transfers between devices  26.8 us (10%)
  local copies, waits for them, and re-layouts  23.9 us (9%)
  starting transfers between devices  17.5 us (7%)
  other arithmetic  14.1 us (6%)
    pallas_call x1, Pallas kernels, run_scatter(): pl.pallas_call(functools.partial(scatter_kernel, plan, (len(arrays),)), o...  91.1 us
    pallas_call x1, Pallas kernels, run_feed(): pl.pallas_call(functools.partial(feed_kernel, pairs, slots), out_shape=[s...  34.2 us
    pallas_call x1, Pallas kernels, run_backward(): pl.pallas_call(functools.partial(backward_kernel, slots), out_shape=[shap...  28.9 us
    ppermute x2, waiting for transfers between devices, gathered(): patches = lax.ppermute(local[:half], 'mod', [(1, 0)])  24.7 us
    pallas_call x1, Pallas kernels, run_forward(): pl.pallas_call(functools.partial(forward_kernel, slots), out_shape=[seq_s...  17.1 us
    ppermute x2, starting transfers between devices, gathered(): texts = lax.ppermute(local[half:, :TEXT], 'mod', [(0, 1)])  6.3 us
    ppermute x2, starting transfers between devices, returned(): far_patches = lax.ppermute(patches, 'mod', [(0, 1)])  5.95 us
  transfers between devices with their start and end apart: 8, of which 3 were waited for; matrix products, arithmetic and copies ran while one was open for 10% of the time, Pallas kernels for 36%

profile of v2, /device:TPU:0, one launch (start us, length us, event | category | flops | bytes accessed | tf_op | source)
XLA Modules:
  0.0 255.3 jit_solution(9136293057806939757)
XLA Ops:
  0.7 1.0 slice.129
  1.7 4.9 %collective-permute-start.1 = (bf16[2,40,768]{2,1,0:T(8,128)(2,1)S(1)}, bf16[2,40,768]{2,1,0:T(8,128)(2,1)S(1)}, u32[]{:S(2)}, u32[]{:S(2)}) collective-permute-start(bf16[2,40,768]{2,1,0:T(8,128)(2,1)S(1)} %slice.129), channel_id=1, source_target_pairs={{0,1},{2,3},{4,5},{6,7},{8,9},{10,11},{12,13},{14,15},{16,17},{18,... | collective-permute-start | bytes 368648 | tf_op jit(solution)/shard_map/ppermute | solution.py:612
  6.6 0.9 slice.131
  7.6 1.4 collective-permute-start.3
  9.0 2.0 slice_bitcast_fusion
  11.1 1.4 collective-permute-start.2
  12.5 0.9 slice_bitcast_fusion.1
  13.4 1.3 collective-permute-start
  14.7 1.4 fusion.4.order
  21.3 11.5 %collective-permute-done.2 = bf16[2,240,768]{2,1,0:T(8,128)(2,1)} collective-permute-done((bf16[2,240,768]{2,1,0:T(8,128)(2,1)}, bf16[2,240,768]{2,1,0:T(8,128)(2,1)}, u32[]{:S(2)}, u32[]{:S(2)}) %collective-permute-start.2) | collective-permute-done | bytes 737312 | tf_op jit(solution)/shard_map/ppermute | solution.py:611
  32.8 1.2 bitcast_select_fusion
  34.0 13.2 %collective-permute-done = bf16[2,240,768]{2,1,0:T(8,128)(2,1)} collective-permute-done((bf16[2,240,768]{2,1,0:T(8,128)(2,1)}, bf16[2,240,768]{2,1,0:T(8,128)(2,1)}, u32[]{:S(2)}, u32[]{:S(2)}) %collective-permute-start) | collective-permute-done | bytes 737312 | tf_op jit(solution)/shard_map/ppermute | solution.py:611
  47.1 1.2 bitcast_select_fusion.1
  48.3 1.6 maximum_maximum_fusion.1
  50.0 17.1 %attention_forward.1 = (bf16[2,288,768]{2,1,0:T(8,128)(2,1)}, bf16[2,288,768]{2,1,0:T(8,128)(2,1)}, bf16[2,288,768]{2,1,0:T(8,128)(2,1)}, bf16[2,288,768]{2,1,0:T(8,128)(2,1)}, f32[576,768]{1,0:T(8,128)}) custom-call(s32[16]{0:T(128)} %concatenate.40.lens, bf16[2,288,768]{2,1,0:T(8,128)(2,1)} %get-tuple-element.58.seq, f32[1,768]{1,0:T(1,128)} %reshape.132.gain, ...), custom_call_target="tpu_custom_call" | custom-call | flops 3737124864 | bytes 12582912 | tf_op jit(solution)/shard_map/attention_forward/pallas_call | solution.py:284
  67.1 34.2 %feed_forward.1 = (bf16[576,768]{1,0:T(8,128)(2,1)}, f32[576,768]{1,0:T(8,128)}, bf16[96,8,3072]{2,1,0:T(8,128)(2,1)}, bf16[2,2,2,2,2,12,8,768]{7,6,5,4,3,2,1,0:...) custom-call(s32[16]{0:T(128)} %concatenate.40.lens, f32[576,768]{1,0:T(8,128)} %get-tuple-element.32.hidden, ...), custom_call_target="tpu_custom_call" | custom-call | flops 16307453952 | bytes 25165824 | tf_op jit(solution)/shard_map/feed_forward/pallas_call | solution.py:319
  101.3 0.9 slice.132
  102.3 1.2 slice.133
  104.9 28.9 %attention_backward.1 = (bf16[2,288,768]{2,1,0:T(8,128)(2,1)}, bf16[96,8,3072]{2,1,0:T(8,128)(2,1)}, f32[8,768]{1,0:T(8,128)}) custom-call(s32[16]{0:T(128)} %concatenate.40.lens, bf16[2,288,768]{2,1,0:T(8,128)(2,1)} %get-tuple-element.58.seq, f32[1,768]{1,0:T(1,128)} %reshape.132.gain, f32[1,768]{1,0:T(1,128)} %reshape.133.shift, ...), custom_call_target="tpu_custom_call" | custom-call | flops 7983857664 | bytes 20971520 | tf_op jit(solution)/shard_map/attention_backward/pallas_call | solution.py:372
  134.6 1.2 slice.114
  135.7 1.3 collective-permute-start.4
  137.6 4.6 %collective-permute-start.5 = (bf16[2,240,768]{2,1,0:T(8,128)(2,1)S(1)}, bf16[2,240,768]{2,1,0:T(8,128)(2,1)S(1)}, u32[]{:S(2)}, u32[]{:S(2)}) collective-permute-start(bf16[2,240,768]{2,1,0:T(8,128)(2,1)S(1)} %slice.133), channel_id=1, source_target_pairs={{0,1},{2,3},{4,5},{6,7},{8,9},{10,11},{12,13},{14,15},{16,17},{18,... | collective-permute-start | bytes 2211848 | tf_op jit(solution)/shard_map/ppermute | solution.py:620
  142.2 1.3 collective-permute-start.7
  144.1 5.1 %pad_maximum_fusion.refs_2_ = bf16[2,2,2,2,2,3,8,3200]{7,6,5,4,3,2,1,0:T(8,128)(2,1)} fusion(bf16[2,2,2,2,2,3,8,128]{7,6,5,4,3,2,1,0:T(8,128)(2,1)S(1)} %bitcast.46, bf16[2,2,2,2,2,3,8,3072]{7,6,5,4,3,2,1,0:T(8,128)(2,1)} %bitcast.32), kind=kLoop, calls=%fused_computation | loop fusion | flops 9830400 | bytes 9830400 | tf_op jit(solution)/shard_map/concatenate | solution.py:691
  150.1 91.1 %scatter.1 = (f32[12,8,768]{2,1,0:T(8,128)}, f32[3,8,3072]{2,1,0:T(8,128)}, f32[3,8,3200]{2,1,0:T(8,128)}) custom-call(bf16[2,2,2,2,2,12,8,768]{7,6,5,4,3,2,1,0:T(8,128)(2,1)} %get-tuple-element.40.refs_0_, bf16[2,2,2,2,2,3,8,3072]{7,6,5,4,3,2,1,0:T(8,128)(2,1)} %bitcast.31, bf16[2,2,2,2,2,3,8,3200]{7,6,5,4,3,2,1,0:T(8,128)(2,1)} %pad_maximum_fusion.refs_2_), custom_call_target="tpu_custom_call" | custom-call | tf_op jit(solution)/shard_map/scatter/pallas_call | solution.py:515
  242.1 1.5 slice.141
  243.6 1.6 slice.138
  245.2 1.3 collective-permute-start.6
  247.1 1.8 slice_reduce_fusion
  248.9 1.4 fusion.7
  250.3 2.1 collective-permute-done.6
  252.4 1.4 fusion.10
  (64 shorter events, 12.2 us)
Async XLA Ops:
  0.6 11.8 %copy-start.1 = (bf16[1,4,240,768]{3,2,1,0:T(8,128)(2,1)S(1)}, bf16[1,4,240,768]{3,2,1,0:T(8,128)(2,1)}, u32[]{:S(2)}) copy-start(bf16[1,4,240,768]{3,2,1,0:T(8,128)(2,1)} %param.17) | copy-start | bytes 4423684
  1.7 19.5 %collective-permute-start.1 = (bf16[2,40,768]{2,1,0:T(8,128)(2,1)S(1)}, bf16[2,40,768]{2,1,0:T(8,128)(2,1)S(1)}, u32[]{:S(2)}, u32[]{:S(2)}) collective-permute-start(bf16[2,40,768]{2,1,0:T(8,128)(2,1)S(1)} %slice.129), channel_id=1, source_target_pairs={{0,1},{2,3},{4,5},{6,7},{8,9},{10,11},{12,13},{14,15},{16,17},{18,... | collective-permute-start | bytes 368648 | tf_op jit(solution)/shard_map/ppermute | solution.py:612
  7.5 8.7 %copy-start.10 = (f32[768]{0:T(1024)S(1)}, f32[768]{0:T(1024)}, u32[]{:S(2)}) copy-start(f32[768]{0:T(1024)} %param.25) | copy-start | bytes 9220
  7.5 8.7 %copy-start.11 = (f32[768]{0:T(1024)S(1)}, f32[768]{0:T(1024)}, u32[]{:S(2)}) copy-start(f32[768]{0:T(1024)} %param.24) | copy-start | bytes 9220
  7.5 8.7 %copy-start.12 = (s32[4]{0:T(128)S(1)}, s32[4]{0:T(128)}, u32[]{:S(2)}) copy-start(s32[4]{0:T(128)} %param.20) | copy-start | bytes 52
  7.5 8.7 %copy-start.13 = (s32[4]{0:T(128)S(1)}, s32[4]{0:T(128)}, u32[]{:S(2)}) copy-start(s32[4]{0:T(128)} %param.19) | copy-start | bytes 52
  7.5 8.9 %copy-start.4 = (f32[768]{0:T(1024)S(1)}, f32[768]{0:T(1024)}, u32[]{:S(2)}) copy-start(f32[768]{0:T(1024)} %param.21) | copy-start | bytes 9220
  7.5 9.4 %copy-start.5 = (f32[768]{0:T(1024)S(1)}, f32[768]{0:T(1024)}, u32[]{:S(2)}) copy-start(f32[768]{0:T(1024)} %param.22) | copy-start | bytes 9220
  7.5 10.0 %copy-start.6 = (f32[768]{0:T(1024)S(1)}, f32[768]{0:T(1024)}, u32[]{:S(2)}) copy-start(f32[768]{0:T(1024)} %param.27) | copy-start | bytes 9220
  7.6 10.6 %copy-start.7 = (f32[768]{0:T(1024)S(1)}, f32[768]{0:T(1024)}, u32[]{:S(2)}) copy-start(f32[768]{0:T(1024)} %param.28) | copy-start | bytes 9220
  7.6 11.2 %copy-start.8 = (f32[768]{0:T(1024)S(1)}, f32[768]{0:T(1024)}, u32[]{:S(2)}) copy-start(f32[768]{0:T(1024)} %param.29) | copy-start | bytes 9220
  7.6 11.8 %copy-start.9 = (f32[768]{0:T(1024)S(1)}, f32[768]{0:T(1024)}, u32[]{:S(2)}) copy-start(f32[768]{0:T(1024)} %param.33) | copy-start | bytes 9220
  7.6 13.6 %collective-permute-start.3 = (bf16[2,40,768]{2,1,0:T(8,128)(2,1)S(1)}, bf16[2,40,768]{2,1,0:T(8,128)(2,1)S(1)}, u32[]{:S(2)}, u32[]{:S(2)}) collective-permute-start(bf16[2,40,768]{2,1,0:T(8,128)(2,1)S(1)} %slice.131), channel_id=1, source_target_pairs={{0,1},{2,3},{4,5},{6,7},{8,9},{10,11},{12,13},{14,15},{16,17},{18,... | collective-permute-start | bytes 368648 | tf_op jit(solution)/shard_map/ppermute | solution.py:612
  11.1 10.2 %copy-start = (bf16[1,4,240,768]{3,2,1,0:T(8,128)(2,1)S(1)}, bf16[1,4,240,768]{3,2,1,0:T(8,128)(2,1)}, u32[]{:S(2)}) copy-start(bf16[1,4,240,768]{3,2,1,0:T(8,128)(2,1)} %param.18) | copy-start | bytes 4423684
  11.1 21.7 %collective-permute-start.2 = (bf16[2,240,768]{2,1,0:T(8,128)(2,1)}, bf16[2,240,768]{2,1,0:T(8,128)(2,1)}, u32[]{:S(2)}, u32[]{:S(2)}) collective-permute-start(bf16[2,240,768]{2,1,0:T(8,128)(2,1)} %slice_bitcast_fusion), channel_id=1, source_target_pairs={{1,0},{3,2},{5,4},{7,6},{9,8},{11,10},{13,12},{15,14},{17,16},{19,... | collective-permute-start | bytes 2211848 | tf_op jit(solution)/shard_map/ppermute | solution.py:611
  13.4 33.7 %collective-permute-start = (bf16[2,240,768]{2,1,0:T(8,128)(2,1)}, bf16[2,240,768]{2,1,0:T(8,128)(2,1)}, u32[]{:S(2)}, u32[]{:S(2)}) collective-permute-start(bf16[2,240,768]{2,1,0:T(8,128)(2,1)} %slice_bitcast_fusion.1), channel_id=1, source_target_pairs={{1,0},{3,2},{5,4},{7,6},{9,8},{11,10},{13,12},{15,14},{17,16},{19,... | collective-permute-start | bytes 2211848 | tf_op jit(solution)/shard_map/ppermute | solution.py:611
  135.7 113.2 %collective-permute-start.4 = (bf16[2,40,768]{2,1,0:T(8,128)(2,1)S(1)}, bf16[2,40,768]{2,1,0:T(8,128)(2,1)S(1)}, u32[]{:S(2)}, u32[]{:S(2)}) collective-permute-start(bf16[2,40,768]{2,1,0:T(8,128)(2,1)S(1)} %slice.132), channel_id=1, source_target_pairs={{1,0},{3,2},{5,4},{7,6},{9,8},{11,10},{13,12},{15,14},{17,16},{19,... | collective-permute-start | bytes 368648 | tf_op jit(solution)/shard_map/ppermute | solution.py:621
  137.6 111.3 %collective-permute-start.5 = (bf16[2,240,768]{2,1,0:T(8,128)(2,1)S(1)}, bf16[2,240,768]{2,1,0:T(8,128)(2,1)S(1)}, u32[]{:S(2)}, u32[]{:S(2)}) collective-permute-start(bf16[2,240,768]{2,1,0:T(8,128)(2,1)S(1)} %slice.133), channel_id=1, source_target_pairs={{0,1},{2,3},{4,5},{6,7},{8,9},{10,11},{12,13},{14,15},{16,17},{18,... | collective-permute-start | bytes 2211848 | tf_op jit(solution)/shard_map/ppermute | solution.py:620
  142.2 110.2 %collective-permute-start.7 = (bf16[2,240,768]{2,1,0:T(8,128)(2,1)S(1)}, bf16[2,240,768]{2,1,0:T(8,128)(2,1)S(1)}, u32[]{:S(2)}, u32[]{:S(2)}) collective-permute-start(bf16[2,240,768]{2,1,0:T(8,128)(2,1)S(1)} %slice.114), channel_id=1, source_target_pairs={{0,1},{2,3},{4,5},{6,7},{8,9},{10,11},{12,13},{14,15},{16,17},{18,... | collective-permute-start | bytes 2211848 | tf_op jit(solution)/shard_map/ppermute | solution.py:620
  245.2 7.2 %collective-permute-start.6 = (bf16[2,40,768]{2,1,0:T(8,128)(2,1)S(1)}, bf16[2,40,768]{2,1,0:T(8,128)(2,1)S(1)}, u32[]{:S(2)}, u32[]{:S(2)}) collective-permute-start(bf16[2,40,768]{2,1,0:T(8,128)(2,1)S(1)} %slice.113), channel_id=1, source_target_pairs={{1,0},{3,2},{5,4},{7,6},{9,8},{11,10},{13,12},{15,14},{17,16},{19,... | collective-permute-start | bytes 368648 | tf_op jit(solution)/shard_map/ppermute | solution.py:621
  250.3 3.5 %copy-start.3 = (f32[3,8,3072]{2,1,0:T(8,128)S(1)}, f32[3,8,3072]{2,1,0:T(8,128)}, u32[]{:S(2)}) copy-start(f32[3,8,3072]{2,1,0:T(8,128)} %get-tuple-element.47) | copy-start | bytes 884740
  250.3 4.2 %copy-start.2 = (f32[12,8,768]{2,1,0:T(8,128)S(1)}, f32[12,8,768]{2,1,0:T(8,128)}, u32[]{:S(2)}) copy-start(f32[12,8,768]{2,1,0:T(8,128)} %get-tuple-element.48) | copy-start | bytes 884740

commit v3 on v1

--- a/solution.py
+++ b/solution.py
@@ -1,4 +1,5 @@
 import functools
+import types
 
 import jax
 import jax.numpy as jnp
@@ -52,8 +53,43 @@
     return jnp.concatenate(parts, axis=0)
 
 
+def mix_heads(pair, group, text_count, patch_count, slots, q_in, k_in, v_in, mixed):
+    rows = q_in.shape[1]
+    first = lax.broadcasted_iota(jnp.int32, (rows, 128), 1) < HEAD_DIM
+    column = lax.broadcasted_iota(jnp.int32, (1, rows), 1)
+    off = pl.multiple_of(group * 128, 128)
+    live = live_slots(column, text_count, patch_count, slots)
+    q2 = q_in[pair, :, pl.ds(off, 128)]
+    k2 = k_in[pair, :, pl.ds(off, 128)]
+    v2 = v_in[pair, :, pl.ds(off, 128)]
+    halves = []
+    for half in range(2):
+        keep = first if half == 0 else ~first
+        qm = jnp.where(keep, q2, jnp.zeros_like(q2))
+        scores = jnp.where(live, dot(qm, k2, 1, 1), MASKED)
+        highest = jnp.max(scores, axis=-1, keepdims=True)
+        shifted = jnp.exp(scores - highest)
+        total = jnp.sum(shifted, axis=-1, keepdims=True)
+        halves.append(dot(shifted.astype(BF16), v2) / total)
+    mixed[pair, :, pl.ds(off, 128)] = jnp.where(first, halves[0], halves[1]).astype(BF16)
+
+
 def forward_kernel(
-    slots, lens, seq, gain, shift, wqkv, qkv_bias, wout, out_bias, q_out, k_out, v_out, mixed, hidden
+    slots,
+    lens,
+    seq,
+    gain,
+    shift,
+    wqkv,
+    qkv_bias,
+    wout,
+    out_bias,
+    q_out,
+    k_out,
+    v_out,
+    hidden,
+    mixed_out,
+    mixed,
 ):
     pairs, rows, width = seq.shape
     tokens = seq[...].reshape(pairs * rows, width).astype(F32)
@@ -65,31 +101,16 @@
         if part == 0:
             made = made * 0.125
         ref[...] = made.astype(BF16).reshape(pairs, rows, width)
-    first = lax.broadcasted_iota(jnp.int32, (rows, 128), 1) < HEAD_DIM
-    column = lax.broadcasted_iota(jnp.int32, (1, rows), 1)
     groups = width // 128
 
     def step(it, carry):
         pair = it // groups
-        off = pl.multiple_of((it % groups) * 128, 128)
-        live = live_slots(column, lens[pair], lens[pairs + pair], slots)
-        q2 = q_out[pair, :, pl.ds(off, 128)]
-        k2 = k_out[pair, :, pl.ds(off, 128)]
-        v2 = v_out[pair, :, pl.ds(off, 128)]
-        halves = []
-        for half in range(2):
-            keep = first if half == 0 else ~first
-            qm = jnp.where(keep, q2, jnp.zeros_like(q2))
-            scores = jnp.where(live, dot(qm, k2, 1, 1), MASKED)
-            highest = jnp.max(scores, axis=-1, keepdims=True)
-            shifted = jnp.exp(scores - highest)
-            total = jnp.sum(shifted, axis=-1, keepdims=True)
-            halves.append(dot(shifted.astype(BF16), v2) / total)
-        mixed[pair, :, pl.ds(off, 128)] = jnp.where(first, halves[0], halves[1]).astype(BF16)
+        mix_heads(pair, it % groups, lens[pair], lens[pairs + pair], slots, q_out, k_out, v_out, mixed)
         return carry
 
     lax.fori_loop(0, pairs * groups, step, 0)
     rows_mixed = mixed[...].reshape(pairs * rows, width)
+    mixed_out[...] = mixed[...]
     hidden[...] = tokens + dot(rows_mixed, wout[...]) + out_bias[...]
 
 
@@ -111,6 +132,7 @@
     hbias,
     wd,
     dbias,
+    order,
     result,
     grad_hidden,
     wh_grad,
@@ -118,6 +140,7 @@
     hb_grad,
     vectors,
     normal,
+    ordered,
     gdown,
     total,
     gnormal,
@@ -130,7 +153,9 @@
     @pl.when(chunk == 0)
     def _():
         normed, _ = norm_parts(hidden[...])
-        normal[...] = (normed * gain[...] + shift[...]).astype(BF16)
+        made = (normed * gain[...] + shift[...]).astype(BF16)
+        normal[...] = made
+        ordered[...] = dot(made, order[...]).astype(BF16)
         gdown[...] = (cot[...].astype(F32) * live).astype(BF16)
         total[...] = hidden[...] + dbias[...]
         gnormal[...] = jnp.zeros_like(gnormal)
@@ -139,10 +164,20 @@
     active, slope = gelu_parts(before)
     active = active.astype(BF16)
     total[...] += dot(active, wd[...])
-    wd_grad[...] = dot(active, gdown[...], 0, 0).astype(BF16)
+    fresh = dot(active, gdown[...], 0, 0)
+    if wd_grad.ndim == 2:
+        wd_grad[...] = fresh.astype(BF16)
+    else:
+        size = fresh.shape[0] // 4
+        base = 2 * pairs
+        for core in range(2):
+            for mod in range(2):
+                start = (2 * core + mod) * size
+                piece = fresh[start : start + size].reshape(size // 8, 8, fresh.shape[1])
+                wd_grad[lens[base + core], 0, 0, lens[base + 2 + mod], 0] = piece.astype(BF16)
     gbefore = (dot(gdown[...], wd[...], 1, 1) * slope).astype(BF16)
     gnormal[...] += dot(gbefore, wh[...], 1, 1)
-    wh_grad[...] = dot(normal[...], gbefore, 0, 0).astype(BF16)
+    wh_grad[...] = dot(ordered[...], gbefore, 0, 0).reshape(wh_grad.shape).astype(BF16)
     hb_grad[...] = jnp.sum(gbefore.astype(F32), axis=0, keepdims=True)
 
     @pl.when(chunk == count - 1)
@@ -172,6 +207,7 @@
     ghidden,
     wqkv,
     wout,
+    order,
     input_grad,
     weight_grad,
     vectors,
@@ -182,9 +218,14 @@
     every = pairs * rows
     gattended = ghidden[...].astype(BF16)
     gmixed[...] = dot(gattended, wout[...], 1, 1).astype(BF16).reshape(pairs, rows, width)
-    weight_grad[:, 3 * width : 4 * width] = dot(
-        mixed[...].reshape(every, width), gattended, 0, 0
-    ).astype(BF16)
+    ordered = dot(mixed[...].reshape(every, width), order[...]).astype(BF16)
+
+    def put(first, last, value):
+        target = (slice(None),) * (len(weight_grad.shape) - 1) + (slice(first, last),)
+        value = value.reshape(weight_grad.shape[:-1] + (last - first,))
+        weight_grad[target] = value.astype(BF16)
+
+    put(3 * width, 4 * width, dot(ordered, gattended, 0, 0))
     first = lax.broadcasted_iota(jnp.int32, (rows, 128), 1) < HEAD_DIM
     index = lax.broadcasted_iota(jnp.int32, (rows, 1), 0)
     groups = width // 128
@@ -227,12 +268,13 @@
     tokens = seq[...].reshape(every, width).astype(F32)
     normed, factor = norm_parts(tokens)
     normal = (normed * gain[...] + shift[...]).astype(BF16)
+    ordered = dot(normal, order[...]).astype(BF16)
     gnormal = jnp.zeros((every, width), F32)
     for part in range(3):
         cols = slice(part * width, (part + 1) * width)
         piece = gproj[:, :, cols].reshape(every, width)
         gnormal += dot(piece, wqkv[:, cols], 1, 1)
-        weight_grad[:, cols] = dot(normal, piece, 0, 0).astype(BF16)
+        put(part * width, (part + 1) * width, dot(ordered, piece, 0, 0))
         if part == 0:
             vectors[2:3, :] = jnp.sum(piece.astype(F32), axis=0, keepdims=True)
         if part == 2:
@@ -258,43 +300,53 @@
 
 def run_forward(lens, seq, gain, shift, wqkv, qkv_bias, wout, out_bias, slots):
     pairs, rows, width = seq.shape
-    seq_shape = shape((pairs, rows, width), BF16)
     every = pairs * rows
+    cube = shape((pairs, rows, width), BF16)
     return pl.pallas_call(
         functools.partial(forward_kernel, slots),
-        out_shape=[seq_shape] * 4 + [shape((every, width), F32)],
+        out_shape=[cube, cube, cube, shape((every, width), F32), cube],
         in_specs=[smem_spec()] + [whole_spec()] * 7,
         out_specs=[whole_spec()] * 5,
+        scratch_shapes=[pltpu.VMEM((pairs, rows, width), BF16)],
         compiler_params=pltpu.CompilerParams(vmem_limit_bytes=VMEM_LIMIT),
-        cost_estimate=pl.CostEstimate(
-            flops=2 * every * width * width * 4 + 8 * every * rows * width,
-            bytes_accessed=12 * 2**20,
-            transcendentals=every * rows * HEADS,
-        ),
         name="attention_forward",
     )(lens, seq, gain, shift, wqkv, qkv_bias, wout, out_bias)
 
 
-def run_feed(lens, hidden, cot, gain, shift, wh, hbias, wd, dbias, pairs, slots, chunks):
+def run_feed(lens, hidden, cot, gain, shift, wh, hbias, wd, dbias, order, pairs, slots, chunks, relative):
     every, width = hidden.shape
     ff = wh.shape[1]
     size = ff // chunks
-    fixed = lambda dims: pl.BlockSpec(dims, lambda c: (0, 0))
-    columns = lambda r: pl.BlockSpec((r, size), lambda c: (0, c))
-    rows = pl.BlockSpec((size, width), lambda c: (c, 0))
+    base = 2 * pairs + 4
+    fixed = lambda dims: pl.BlockSpec(dims, lambda c, s: (0, 0))
+    columns = lambda r: pl.BlockSpec((r, size), lambda c, s: (0, s[base + c]))
+    rows = pl.BlockSpec((size, width), lambda c, s: (s[base + c], 0))
+    if relative:
+        part = size // 4 // 8
+        wd_shape = shape((2, 2, 2, 2, 2, part, 8, width), BF16)
+        wd_spec = pl.BlockSpec(
+            (2, 1, 1, 2, 1, part, 8, width),
+            lambda c, s: (0, c % 2, c // 2 % 2, 0, c // 4, 0, 0, 0),
+        )
+        wh_shape = shape((width // 8, 8, ff), BF16)
+        wh_spec = pl.BlockSpec((width // 8, 8, size), lambda c, s: (0, 0, s[base + c]))
+    else:
+        wd_shape, wd_spec = shape((ff, width), BF16), rows
+        wh_shape, wh_spec = shape((width, ff), BF16), columns(width)
     return pl.pallas_call(
         functools.partial(feed_kernel, pairs, slots),
-        grid=(chunks,),
         out_shape=[
             shape((every, width), BF16),
             shape((every, width), F32),
-            shape((width, ff), BF16),
-            shape((ff, width), BF16),
+            wh_shape,
+            wd_shape,
             shape((1, ff), F32),
             shape((8, width), F32),
         ],
+        grid_spec=pltpu.PrefetchScalarGridSpec(
+        num_scalar_prefetch=1,
+        grid=(chunks,),
         in_specs=[
-            smem_spec(),
             fixed((every, width)),
             fixed((every, width)),
             fixed((1, width)),
@@ -303,21 +355,24 @@
             columns(1),
             rows,
             fixed((1, width)),
+            fixed((width, width)),
         ],
         out_specs=[
             fixed((every, width)),
             fixed((every, width)),
-            columns(width),
-            rows,
+            wh_spec,
+            wd_spec,
             columns(1),
             fixed((8, width)),
         ],
         scratch_shapes=[
             pltpu.VMEM((every, width), BF16),
             pltpu.VMEM((every, width), BF16),
+            pltpu.VMEM((every, width), BF16),
             pltpu.VMEM((every, width), F32),
             pltpu.VMEM((every, width), F32),
         ],
+        ),
         compiler_params=pltpu.CompilerParams(vmem_limit_bytes=VMEM_LIMIT),
         cost_estimate=pl.CostEstimate(
             flops=12 * every * width * ff,
@@ -325,20 +380,20 @@
             transcendentals=2 * every * ff,
         ),
         name="feed_forward",
-    )(lens, hidden, cot, gain, shift, wh, hbias, wd, dbias)
-
-
-def run_backward(lens, seq, gain, shift, q, k, v, mixed, ghidden, wqkv, wout, slots):
+    )(lens, hidden, cot, gain, shift, wh, hbias, wd, dbias, order)
+
+
+def run_backward(lens, seq, gain, shift, q, k, v, mixed, ghidden, wqkv, wout, order, slots, relative):
     pairs, rows, width = seq.shape
     every = pairs * rows
     return pl.pallas_call(
         functools.partial(backward_kernel, slots),
         out_shape=[
             shape((pairs, rows, width), BF16),
-            shape((width, 4 * width), BF16),
+            shape((width // 8, 8, 4 * width) if relative else (width, 4 * width), BF16),
             shape((8, width), F32),
         ],
-        in_specs=[smem_spec()] + [whole_spec()] * 10,
+        in_specs=[smem_spec()] + [whole_spec()] * 11,
         out_specs=[whole_spec()] * 3,
         scratch_shapes=[
             pltpu.VMEM((pairs, rows, width), BF16),
@@ -351,7 +406,790 @@
             transcendentals=every * rows * HEADS,
         ),
         name="attention_backward",
-    )(lens, seq, gain, shift, q, k, v, mixed, ghidden, wqkv, wout)
+    )(lens, seq, gain, shift, q, k, v, mixed, ghidden, wqkv, wout, order)
+
+
+BITS = ("core", "y", "z0", "x", "z1")
+ORDERS = (("core", "y", "z0", "x", "z1"), ("core", "z0", "y", "x", "z1"))
+
+
+def partner(bit):
+    if bit == "x":
+        return {"mod": 1 - lax.axis_index("mod")}
+    size = {"core": 1, "y": 2, "z0": 4, "z1": 8}[bit]
+    me = lax.axis_index("pairs")
+    return {"pairs": me + size - 2 * size * (me // size % 2)}
+
+
+def narrowed(ref, names, bit, value):
+    dim = names.index(bit)
+    index = (slice(None),) * dim + (value,)
+    return ref.at[index], names[:dim] + names[dim + 1 :]
+
+
+def flip(value, bit):
+    return value + bit - 2 * value * bit
+
+
+def place():
+    pairs = lax.axis_index("pairs")
+    return {
+        "core": pairs % 2,
+        "y": pairs // 2 % 2,
+        "z0": pairs // 4 % 2,
+        "z1": pairs // 8,
+        "x": lax.axis_index("mod"),
+    }
+
+
+def hop(bit, source, target, sems, index, there=None):
+    return pltpu.make_async_remote_copy(
+        src_ref=source,
+        dst_ref=target,
+        send_sem=sems[0].at[index],
+        recv_sem=sems[1].at[index if there is None else there],
+        device_id=partner(bit),
+        device_id_type=pl.DeviceIdType.MESH,
+    )
+
+
+def lead_index(it, lead):
+    index = []
+    for size in reversed(lead):
+        index.insert(0, it % size)
+        it = it // size
+    return tuple(index)
+
+
+def accumulate(target, source):
+    lead = target.shape[:-3]
+    count = 1
+    for size in lead:
+        count *= size
+    if count == 1:
+        at = (0,) * len(lead)
+        target[at] = target[at] + source[at]
+        return
+
+    def body(it, carry):
+        at = lead_index(it, lead)
+        target[at] = target[at] + source[at]
+        return carry
+
+    lax.fori_loop(0, count, body, 0)
+
+
+class Unit:
+    def __init__(self, own, arrivals, order, sems, base, finish):
+        self.own, self.arrivals, self.order = own, arrivals, order
+        self.sems, self.base, self.finish = sems, base, finish
+        self.peers = {}
+
+    def views(self, step):
+        ref, names = self.own, list(BITS)
+        for bit in self.order[:step]:
+            ref, names = narrowed(ref, names, bit, 0)
+        sent, _ = narrowed(ref, names, self.order[step], 1)
+        kept, _ = narrowed(ref, names, self.order[step], 0)
+        return sent, kept
+
+    def copy(self, step):
+        bit = self.order[step]
+        sent, _ = self.views(step)
+        peer = self.peers.get(bit, self)
+        return hop(bit, sent, peer.arrivals[step], self.sems, self.base + step, peer.base + step)
+
+    def arrival(self, step):
+        sent, _ = self.views(step)
+        return hop(self.order[step], sent, self.arrivals[step], self.sems, self.base + step)
+
+    def start(self):
+        self.copy(0).start()
+
+    def advance(self, step):
+        self.arrival(step).wait_recv()
+        _, kept = self.views(step)
+        if step == 4:
+            self.finish(kept[...].astype(F32) + self.arrivals[4][...].astype(F32))
+            return
+        accumulate(kept, self.arrivals[step])
+        self.copy(step + 1).start()
+
+    def drain(self):
+        for step in range(5):
+            self.copy(step).wait_send()
+
+
+def counts(here, pairs, text_len, patch_count):
+    base = here["x"] * pairs
+    return [text_len[base + pair] for pair in range(pairs)] + [patch_count[base + pair] for pair in range(pairs)]
+
+
+def opening_kernel(pairs, slots, names, *refs):
+    r = types.SimpleNamespace(**dict(zip(names, refs)))
+    rows, width = r.seq.shape[1:]
+    every, tail = pairs * rows, rows - slots
+    here = place()
+    lens = counts(here, pairs, r.text_len, r.patch_count)
+    sems = (r.send_sem, r.recv_sem)
+    barrier = pltpu.get_barrier_semaphore()
+    pl.semaphore_signal(barrier, inc=1, device_id=partner("x"), device_id_type=pl.DeviceIdType.MESH)
+
+    def moves(which, pair):
+        source, target = ((r.inputs, r.seq), (r.cotangent, r.cot))[which]
+        index = which * pairs + pair
+        patches, texts = target.at[pair, pl.ds(0, slots)], target.at[pair, pl.ds(slots, tail)]
+        near = lambda src, dst: pltpu.make_async_copy(src, dst, r.load_sem.at[index])
+        return (
+            hop("x", source.at[0, pair], patches, sems, index),
+            hop("x", source.at[0, pairs + pair, pl.ds(0, tail)], texts, sems, index),
+            near(source.at[0, pairs + pair], patches),
+            near(source.at[0, pair, pl.ds(0, tail)], texts),
+        )
+
+    every_move = [(which, pair) for which in range(2) for pair in range(pairs)]
+    weights = [
+        pltpu.make_async_copy(source, target, r.load_sem.at[2 * pairs + index])
+        for index, (source, target) in enumerate(((r.wqkv_in, r.wqkv), (r.wout_in, r.wout)))
+    ]
+    pl.semaphore_wait(barrier, 1)
+
+    @pl.when(here["x"] == 1)
+    def _():
+        for move in every_move:
+            moves(*move)[0].start()
+        for move in every_move:
+            moves(*move)[2].start()
+
+    @pl.when(here["x"] == 0)
+    def _():
+        for move in every_move:
+            moves(*move)[1].start()
+        for move in every_move:
+            moves(*move)[3].start()
+
+    for copy in weights:
+        copy.start()
+
+    def arrived(which, pair):
+        @pl.when(here["x"] == 1)
+        def _():
+            moves(which, pair)[1].wait_recv()
+            moves(which, pair)[2].wait()
+
+        @pl.when(here["x"] == 0)
+        def _():
+            moves(which, pair)[0].wait_recv()
+            moves(which, pair)[3].wait()
+
+    place_at = lax.broadcasted_iota(jnp.int32, (width, 1), 0)
+    feature = lax.broadcasted_iota(jnp.int32, (width, width), 1)
+    unit = width // 32
+    block = place_at // unit
+    bit = lambda shift: (block >> shift) & 1
+    owner = (bit(0) << 4) + (bit(2) << 3) + (bit(3) << 2) + (bit(4) << 1) + bit(1)
+    owner = owner ^ (lax.axis_index("pairs") * 2 + here["x"])
+    source = owner * unit + (place_at - block * unit)
+    r.order[...] = (source == feature).astype(F32).astype(BF16)
+    vec = lambda index: r.vecs[index : index + 1, :]
+    for copy in weights:
+        copy.wait()
+    for pair in range(pairs):
+        arrived(0, pair)
+        tokens = r.seq[pair].astype(F32)
+        normed, _ = norm_parts(tokens)
+        normal = (normed * vec(0) + vec(1)).astype(BF16)
+        r.normal[pair] = normal
+        for part, ref in enumerate((r.q_out, r.k_out, r.v_out)):
+            made = dot(normal, r.wqkv[:, part * width : (part + 1) * width])
+            if part == 0:
+                made = (made + vec(2)) * 0.125
+            if part == 2:
+                made = made + vec(3)
+            ref[pair] = made.astype(BF16)
+
+        def step(group, carry):
+            mix_heads(pair, group, lens[pair], lens[pairs + pair], slots, r.q_out, r.k_out, r.v_out, r.mixed)
+            return carry
+
+        lax.fori_loop(0, width // 128, step, 0)
+        made = r.seq[pair].astype(F32) + dot(r.mixed[pair], r.wout[...]) + vec(4)
+        r.hidden[pair * rows : (pair + 1) * rows, :] = made
+    stores = [
+        pltpu.make_async_copy(r.seq, r.seq_out, r.store_sem.at[0]),
+        pltpu.make_async_copy(r.cot, r.cot_out, r.store_sem.at[1]),
+    ]
+    stores[0].start()
+    r.mixed_out[...] = dot(r.order[...], r.mixed[...].reshape(every, width), 1, 1).astype(BF16)
+    r.normal_out[...] = dot(r.order[...], r.normal[...].reshape(every, width), 1, 1).astype(BF16)
+    for pair in range(pairs):
+        arrived(1, pair)
+    stores[1].start()
+
+    @pl.when(here["x"] == 1)
+    def _():
+        for move in every_move:
+            moves(*move)[0].wait_send()
+
+    @pl.when(here["x"] == 0)
+    def _():
+        for move in every_move:
+            moves(*move)[1].wait_send()
+
+    for copy in stores:
+        copy.wait()
+
+
+def run_opening(text_len, patch_count, inputs, cotangent, vecs, wqkv, wout):
+    _, group, slots, width = inputs.shape
+    pairs = group // 2
+    rows = padded(TEXT + slots)
+    every = pairs * rows
+    hbm = pl.BlockSpec(memory_space=pl.ANY)
+    operands = dict(
+        text_len=(text_len, smem_spec()),
+        patch_count=(patch_count, smem_spec()),
+        inputs=(inputs, hbm),
+        cotangent=(cotangent, hbm),
+        vecs=(vecs, whole_spec()),
+        wqkv_in=(wqkv, hbm),
+        wout_in=(wout, hbm),
+    )
+    cube = shape((pairs, rows, width), BF16)
+    tall = shape((width, every), BF16)
+    outs = dict(
+        q_out=(cube, whole_spec()),
+        k_out=(cube, whole_spec()),
+        v_out=(cube, whole_spec()),
+        hidden=(shape((every, width), F32), whole_spec()),
+        mixed_out=(tall, whole_spec()),
+        normal_out=(tall, whole_spec()),
+        seq_out=(cube, hbm),
+        cot_out=(cube, hbm),
+        order=(shape((width, width), BF16), whole_spec()),
+    )
+    held = pltpu.VMEM((pairs, rows, width), BF16)
+    scratch = dict(
+        seq=held,
+        cot=held,
+        mixed=held,
+        normal=held,
+        wqkv=pltpu.VMEM(wqkv.shape, BF16),
+        wout=pltpu.VMEM(wout.shape, BF16),
+        send_sem=pltpu.SemaphoreType.DMA((2 * pairs,)),
+        recv_sem=pltpu.SemaphoreType.DMA((2 * pairs,)),
+        load_sem=pltpu.SemaphoreType.DMA((2 * pairs + 2,)),
+        store_sem=pltpu.SemaphoreType.DMA((2,)),
+    )
+    names = list(operands) + list(outs) + list(scratch)
+    return pl.pallas_call(
+        functools.partial(opening_kernel, pairs, slots, names),
+        out_shape=[kind for kind, _ in outs.values()],
+        in_specs=[spec for _, spec in operands.values()],
+        out_specs=[spec for _, spec in outs.values()],
+        scratch_shapes=list(scratch.values()),
+        compiler_params=pltpu.CompilerParams(collective_id=2, has_side_effects=True, vmem_limit_bytes=VMEM_LIMIT),
+        name="opening",
+    )(*[value for value, _ in operands.values()])
+
+
+def fused_kernel(pairs, slots, names, *refs):
+    r = types.SimpleNamespace(**dict(zip(names, refs)))
+    rows, width = r.seq.shape[1:]
+    every = pairs * rows
+    tail = rows - slots
+    here = place()
+    lens = counts(here, pairs, r.text_len, r.patch_count)
+    vec_in = lambda index: r.vecs[index : index + 1, :]
+    sems = (r.send_sem, r.recv_sem)
+    barrier = pltpu.get_barrier_semaphore()
+    for bit in BITS:
+        pl.semaphore_signal(barrier, inc=1, device_id=partner(bit), device_id_type=pl.DeviceIdType.MESH)
+
+    def load(name, target, index):
+        return pltpu.make_async_copy(getattr(r, name), getattr(r, target), r.load_sem.at[index])
+
+    early = [load("hidden_in", "hidden", 0), load("order_in", "order", 1), load("cot_in", "cot", 2)]
+    late = [
+        load("mixed_in", "mixed_t", 3),
+        load("normal_in", "normal_t", 4),
+        load("seq_in", "seq", 5),
+        load("q_in", "q", 6),
+        load("k_in", "k", 7),
+        load("v_in", "v", 8),
+    ]
+
+    def block_of(t):
+        z1, z0 = 1 - t // 2, 1 - t % 2
+        return flip(z0, here["z0"]) + 2 * flip(z1, here["z1"])
+
+    def weight_loads(t, slot):
+        start = pl.multiple_of(block_of(t) * width, width)
+        return (
+            pltpu.make_async_copy(r.wh.at[:, pl.ds(start, width)], r.wbuf.at[slot], r.w_sem.at[slot]),
+            pltpu.make_async_copy(r.wd.at[pl.ds(start, width), :], r.wbuf.at[2 + slot], r.w_sem.at[2 + slot]),
+        )
+
+    early[0].start()
+    early[1].start()
+    for copy in weight_loads(0, 0):
+        copy.start()
+    early[2].start()
+    early[0].wait()
+    live = live_rows(lens, pairs, rows, slots)
+    normed, _ = norm_parts(r.hidden[...])
+    made = (normed * vec_in(5) + vec_in(6)).astype(BF16)
+    r.normal2[...] = made
+    early[1].wait()
+    r.normal2_t[...] = dot(r.order[...], made, 1, 1).astype(BF16)
+    r.total[...] = r.hidden[...] + vec_in(7)
+    r.gnormal[...] = jnp.zeros_like(r.gnormal)
+    early[2].wait()
+    r.gdown[...] = (r.cot[...].reshape(every, width).astype(F32) * live).astype(BF16)
+    r.unit_h[...] = jnp.zeros_like(r.unit_h)
+    for copy in late:
+        copy.start()
+    r.zeros[...] = jnp.zeros_like(r.zeros)
+    pl.semaphore_wait(barrier, len(BITS))
+
+    def blanks():
+        return [
+            pltpu.make_async_copy(r.zeros, out.at[0, pair, pl.ds(tail, slots - tail)], r.zero_sem.at[2 * pair + index])
+            for index, out in enumerate((r.block_out, r.input_grad))
+            for pair in range(2 * pairs)
+        ]
+
+    @pl.when(here["x"] == 0)
+    def _():
+        for copy in blanks():
+            copy.start()
+
+    arrivals = lambda name, index: [getattr(r, name + str(step)).at[index] for step in range(5)]
+    tasks = {}
+
+    def at(tick, action):
+        tasks.setdefault(tick, []).append(action)
+
+    a_core = lambda t, y: hop("core", r.a_own.at[t, 1, y], r.a_core.at[t, y], sems, 2 * t + y)
+    a_y = lambda t: hop("y", r.a_own.at[t, 0, 1], r.a_y.at[t], sems, 8 + t)
+    a_z0 = lambda k: hop("z0", r.a_own.at[2 * k, 0, 0], r.a_z0.at[k], sems, 12 + k)
+    a_x = lambda k: hop("x", r.a_own.at[2 * k + 1, 0, 0, 1], r.a_x.at[k], sems, 14 + k)
+    a_z1 = lambda: hop("z1", r.a_own.at[1, 0, 0, 0], r.a_z1.at[0], sems, 16)
+
+    def a_first(t):
+        a_core(t, 1).wait_recv()
+        accumulate(r.a_own.at[t, 0, 1], r.a_core.at[t, 1])
+        a_y(t).start()
+        a_core(t, 0).wait_recv()
+        accumulate(r.a_own.at[t, 0, 0], r.a_core.at[t, 0])
+
+    def a_second(t):
+        k = t // 2
+        a_y(t).wait_recv()
+        accumulate(r.a_own.at[t, 0, 0], r.a_y.at[t])
+        if t % 2 == 0:
+            a_z0(k).start()
+        else:
+            a_z0(k).wait_recv()
+            accumulate(r.a_own.at[t, 0, 0], r.a_z0.at[k])
+            a_x(k).start()
+
+    def a_third(k):
+        a_x(k).wait_recv()
+        accumulate(r.a_own.at[2 * k + 1, 0, 0, pl.ds(0, 1)], r.a_x.at[pl.ds(k, 1)])
+        if k == 0:
+            a_z1().start()
+
+    def a_last():
+        a_z1().wait_recv()
+        r.out_a[...] = r.a_own[3, 0, 0, 0].astype(F32) + r.a_z1[0].astype(F32)
+
+    for t in range(4):
+        at(2 * t + 2, functools.partial(a_first, t))
+        at(2 * t + 4, functools.partial(a_second, t))
+    at(8, functools.partial(a_third, 0))
+    at(12, functools.partial(a_third, 1))
+    at(14, a_last)
+
+    def b_finish(t):
+        def finish(value):
+            r.out_b[:, :, pl.ds(pl.multiple_of(block_of(t) * width, width), width)] = value
+
+        return finish
+
+    def c_finish(g):
+        def finish(value):
+            for part in range(3):
+                cols = slice(part * width + 128 * g, part * width + 128 * g + 128)
+                r.out_c[:, :, cols] = value[:, :, 128 * part : 128 * part + 128]
+
+        return finish
+
+    def o_finish(value):
+        r.out_o[...] = value
+
+    def plain(name):
+        def finish(value):
+            getattr(r, name)[...] = value
+
+        return finish
+
+    units = {}
+    for t in range(4):
+        units["b", t] = Unit(r.b_own.at[t], arrivals("b", t), ORDERS[1], sems, 20 + 5 * t, b_finish(t))
+    for t in range(4):
+        units["b", t].peers = {"z0": units["b", t ^ 1], "z1": units["b", t ^ 2]}
+    groups = width // 128
+    for g in range(groups):
+        units["c", g] = Unit(r.c_own.at[g], arrivals("c", g), ORDERS[g % 2], sems, 40 + 5 * g, c_finish(g))
+    units["o", 0] = Unit(r.o_own, arrivals("o", 0), ORDERS[0], sems, 70, o_finish)
+    units["h", 0] = Unit(r.unit_h, arrivals("h", 0), ORDERS[1], sems, 75, plain("out_h"))
+    units["v", 0] = Unit(r.unit_v, arrivals("v", 0), ORDERS[0], sems, 80, plain("out_v"))
+    plans = {
+        ("b", 0): [2, 6, 8, 10, 15],
+        ("b", 1): [4, 6, 8, 10, 15],
+        ("b", 2): [6, 11, 13, 14, 16],
+        ("b", 3): [8, 11, 13, 14, 16],
+    }
+    plans["o", 0] = [9, 13, 15, 16, 17]
+    plans["h", 0] = [9, 10, 11, 12, 13]
+    for g in range(groups):
+        plans["c", g] = [11 + 2 * g, 13 + 2 * g, 14 + 2 * g, 15 + 2 * g, 16 + 2 * g]
+    for key, ticks in plans.items():
+        for step, tick in enumerate(ticks):
+            at(tick, functools.partial(units[key].advance, step))
+
+    def run_tasks(ticks, now):
+        for tick in ticks:
+            if tick in tasks:
+
+                @pl.when(now == tick)
+                def _(tick=tick):
+                    for action in tasks[tick]:
+                        action()
+
+    size = width // 2
+
+    def feed_step(t, carry):
+        slot = t % 2
+        for copy in weight_loads(t, slot):
+            copy.wait()
+
+        @pl.when(t < 3)
+        def _():
+            for copy in weight_loads(t + 1, 1 - slot):
+                copy.start()
+
+        for sub in range(2):
+            run_tasks([2 * k + sub for k in range(4)], 2 * t + sub)
+            y = 1 - sub
+            part = flip(y, here["y"])
+            start = pl.multiple_of(part * size, size)
+            wh = r.wbuf[slot, :, pl.ds(start, size)]
+            wd = r.wbuf[2 + slot, pl.ds(start, size), :]
+            before = dot(r.normal2[...], wh) + r.vecs[pl.ds(8 + block_of(t), 1), pl.ds(start, size)]
+            active, slope = gelu_parts(before)
+            active = active.astype(BF16)
+            r.total[...] += dot(active, wd)
+            fresh = dot(active, r.gdown[...], 0, 0)
+            quarter = size // 4
+            for core in range(2):
+                for mod in range(2):
+                    first = (2 * core + mod) * quarter
+                    piece = fresh[first : first + quarter].reshape(quarter // 8, 8, width)
+                    r.a_own[t, flip(core, here["core"]), y, flip(mod, here["x"])] = piece.astype(BF16)
+            a_core(t, y).start()
+            gbefore = (dot(r.gdown[...], wd, 1, 1) * slope).astype(BF16)
+            r.gnormal[...] += dot(gbefore, wh, 1, 1)
+            fresh = dot(r.normal2_t[...], gbefore)
+            fresh = fresh.reshape((2,) * 5 + (width // 256, 8, size)).astype(BF16)
+            r.b_own[t, :, :, :, :, :, :, :, pl.ds(start, size)] = fresh
+            sums = jnp.sum(gbefore.astype(F32), axis=0, keepdims=True)
+            z1, z0 = 1 - t // 2, 1 - t % 2
+            for core in range(2):
+                for mod in range(2):
+                    first = (2 * core + mod) * quarter
+                    r.unit_h[
+                        flip(core, here["core"]), y, z0, flip(mod, here["x"]), z1, 0, 0:1, 0:quarter
+                    ] = sums[:, first : first + quarter]
+        hop("core", r.b_own.at[t, 1], r.b0.at[t], sems, 20 + 5 * t).start()
+        return carry
+
+    lax.fori_loop(0, 4, feed_step, 0)
+
+    wout_load = pltpu.make_async_copy(r.wout, r.wbuf.at[3], r.w_sem.at[3])
+    wout_load.start()
+    wqkv_loads = [
+        pltpu.make_async_copy(
+            r.wqkv.at[:, pl.ds(part * width, width)], r.wbuf.at[part], r.w_sem.at[part]
+        )
+        for part in range(3)
+    ]
+    for copy in wqkv_loads:
+        copy.start()
+    units["h", 0].start()
+    r.result[...] = (r.total[...] * live).astype(BF16).reshape(pairs, rows, width)
+
+    def give(source, target, index):
+        near = lambda src, dst: pltpu.make_async_copy(src, dst, r.give_sem.at[index])
+        first_pairs, last_pairs = pl.ds(0, pairs), pl.ds(pairs, pairs)
+        patches, texts = source.at[:, pl.ds(0, slots)], source.at[:, pl.ds(slots, tail)]
+        return (
+            hop("x", patches, target.at[0, first_pairs], sems, 85 + index),
+            hop("x", texts, target.at[0, last_pairs, pl.ds(0, tail)], sems, 85 + index),
+            near(patches, target.at[0, last_pairs]),
+            near(texts, target.at[0, first_pairs, pl.ds(0, tail)]),
+        )
+
+    def give_start(copies):
+        for which in range(2):
+
+            @pl.when(here["x"] == which)
+            def _():
+                copies[which].start()
+                copies[3 - which].start()
+
+    def give_wait(copies):
+        for which in range(2):
+
+            @pl.when(here["x"] == which)
+            def _():
+                copies[1 - which].wait_recv()
+                copies[which].wait_send()
+                copies[3 - which].wait()
+
+    result_copies = give(r.result, r.block_out, 0)
+    give_start(result_copies)
+    normed, factor = norm_parts(r.hidden[...])
+    gnorm = r.gnormal[...]
+    down = r.gdown[...].astype(F32)
+    vec = [
+        jnp.sum(gnorm * normed, axis=0, keepdims=True),
+        jnp.sum(gnorm, axis=0, keepdims=True),
+        jnp.sum(down, axis=0, keepdims=True),
+    ]
+    made = down + norm_back(gnorm, normed, factor, vec_in(5))
+    gattended = made.astype(BF16)
+    vec.append(jnp.sum(gattended.astype(F32), axis=0, keepdims=True))
+    for index, value in enumerate(vec):
+        r.vec[4 + index : 5 + index, :] = value
+    r.gnormal[...] = made
+    wout_load.wait()
+    r.gmixed[...] = dot(gattended, r.wbuf[3], 1, 1).astype(BF16).reshape(pairs, rows, width)
+    for copy in late:
+        copy.wait()
+    fresh = dot(r.mixed_t[...], gattended)
+    r.o_own[...] = fresh.reshape((2,) * 5 + (width // 256, 8, width)).astype(BF16)
+    units["o", 0].start()
+
+    first = lax.broadcasted_iota(jnp.int32, (rows, 128), 1) < HEAD_DIM
+    index = lax.broadcasted_iota(jnp.int32, (rows, 1), 0)
+
+    def head_step(g, carry):
+        base = g * 128
+        off = pl.multiple_of(base, 128)
+        for pair in range(pairs):
+            run_tasks([8 + 2 * k + pair for k in range(groups)], 8 + 2 * g + pair)
+            keys_live = live_slots(index, lens[pair], lens[pairs + pair], slots)
+            q2 = r.q[pair, :, pl.ds(off, 128)]
+            k2 = r.k[pair, :, pl.ds(off, 128)]
+            v2 = r.v[pair, :, pl.ds(off, 128)]
+            g2 = r.gmixed[pair, :, pl.ds(off, 128)]
+            gq = gk = gv = None
+            for half in range(2):
+                keep = first if half == 0 else ~first
+                zero = jnp.zeros_like(q2)
+                qm = jnp.where(keep, q2, zero)
+                km = jnp.where(keep, k2, zero)
+                gm = jnp.where(keep, g2, zero)
+                scores = jnp.where(keys_live, dot(k2, qm, 1, 1), MASKED)
+                highest = jnp.max(scores, axis=0, keepdims=True)
+                shifted = jnp.exp(scores - highest)
+                probs = shifted * (1.0 / jnp.sum(shifted, axis=0, keepdims=True))
+                gprobs = dot(v2, gm, 1, 1)
+                row_dot = jnp.sum(probs * gprobs, axis=0, keepdims=True)
+                gscores = (probs * (gprobs - row_dot)).astype(BF16)
+                new_v = dot(probs.astype(BF16), gm)
+                new_k = dot(gscores, qm)
+                new_q = dot(gscores, km, 0, 0)
+                gq = new_q if gq is None else gq + new_q
+                gk = new_k if gk is None else gk + new_k
+                gv = new_v if gv is None else gv + new_v
+            r.gproj[pair, :, pl.ds(off, 128)] = (gq * 0.125).astype(BF16)
+            r.gproj[pair, :, pl.ds(pl.multiple_of(base + width, 128), 128)] = gk.astype(BF16)
+            r.gproj[pair, :, pl.ds(pl.multiple_of(base + 2 * width, 128), 128)] = gv.astype(BF16)
+        pieces = [
+            r.gproj[:, :, pl.ds(pl.multiple_of(base + part * width, 128), 128)].reshape(every, 128)
+            for part in range(3)
+        ]
+        fresh = dot(r.normal_t[...], jnp.concatenate(pieces, axis=1))
+        r.c_own[g] = fresh.reshape((2,) * 5 + (width // 256, 8, 384)).astype(BF16)
+        hop("core", r.c_own.at[g, 1], r.c0.at[g], sems, 40 + 5 * g).start()
+        return carry
+
+    lax.fori_loop(0, groups, head_step, 0)
+
+    def run_now(tick):
+        for action in tasks.get(tick, []):
+            action()
+
+    tokens = r.seq[...].reshape(every, width).astype(F32)
+    normed, factor = norm_parts(tokens)
+    gnormal = jnp.zeros((every, width), F32)
+    for part in range(3):
+        run_now(20 + part)
+        piece = r.gproj[:, :, part * width : (part + 1) * width].reshape(every, width)
+        wqkv_loads[part].wait()
+        gnormal += dot(piece, r.wbuf[part], 1, 1)
+        if part == 0:
+            r.vec[2:3, :] = jnp.sum(piece.astype(F32), axis=0, keepdims=True)
+        if part == 2:
+            r.vec[3:4, :] = jnp.sum(piece.astype(F32), axis=0, keepdims=True)
+    run_now(23)
+    r.vec[0:1, :] = jnp.sum(gnormal * normed, axis=0, keepdims=True)
+    r.vec[1:2, :] = jnp.sum(gnormal, axis=0, keepdims=True)
+    made = r.gnormal[...] + norm_back(gnormal, normed, factor, vec_in(0))
+    r.grad_rows[...] = (made * live).astype(BF16).reshape(pairs, rows, width)
+    grad_copies = give(r.grad_rows, r.input_grad, 1)
+    give_start(grad_copies)
+    run_now(24)
+    rest = r.vec[...]
+    ordered = jnp.zeros_like(rest)
+    for _ in range(3):
+        high = rest.astype(BF16)
+        ordered += dot(high, r.order[...], 1, 1)
+        rest = rest - high.astype(F32)
+    r.unit_v[...] = jnp.zeros_like(r.unit_v)
+    unit = width // 32
+    for block in range(32):
+        bits = tuple(block >> shift & 1 for shift in (4, 3, 2, 1, 0))
+        r.unit_v[bits + (0, slice(None), slice(0, unit))] = ordered[:, block * unit : (block + 1) * unit]
+    units["v", 0].start()
+    run_now(25)
+    run_now(26)
+    for step in range(5):
+        units["v", 0].advance(step)
+    give_wait(result_copies)
+    give_wait(grad_copies)
+
+    @pl.when(here["x"] == 0)
+    def _():
+        for copy in blanks():
+            copy.wait()
+
+    for t in range(4):
+        a_core(t, 0).wait_send()
+        a_core(t, 1).wait_send()
+        a_y(t).wait_send()
+    for k in range(2):
+        a_z0(k).wait_send()
+        a_x(k).wait_send()
+    a_z1().wait_send()
+    for unit in units.values():
+        unit.drain()
+
+
+def run_fused(text_len, patch_count, vecs, hidden, cot, wh, wd, order, wqkv, wout, seq, q, k, v, mixed_t, normal_t, slots):
+    pairs, rows, width = seq.shape
+    every = pairs * rows
+    wide = (2,) * 5
+    eight = width // 256
+    groups = width // 128
+
+    def arrivals(name, count, tail, kind):
+        return {name + str(step): pltpu.VMEM((count,) + (2,) * (4 - step) + tail, kind) for step in range(5)}
+
+    flat = lambda kind: pltpu.VMEM((every, width), kind)
+    cube = pltpu.VMEM((pairs, rows, width), BF16)
+    tall = pltpu.VMEM((width, every), BF16)
+    block = (width // 64, 8, width)
+    scratch = dict(
+        cot=cube,
+        result=cube,
+        grad_rows=cube,
+        zeros=pltpu.VMEM((slots - (rows - slots), width), BF16),
+        give_sem=pltpu.SemaphoreType.DMA((2,)),
+        zero_sem=pltpu.SemaphoreType.DMA((4 * pairs,)),
+        hidden=flat(F32),
+        gdown=flat(BF16),
+        seq=cube,
+        q=cube,
+        k=cube,
+        v=cube,
+        mixed_t=tall,
+        normal_t=tall,
+        wbuf=pltpu.VMEM((4, width, width), BF16),
+        order=pltpu.VMEM((width, width), BF16),
+        normal2=flat(BF16),
+        normal2_t=tall,
+        total=flat(F32),
+        gnormal=flat(F32),
+        gmixed=cube,
+        gproj=pltpu.VMEM((pairs, rows, 3 * width), BF16),
+        vec=pltpu.VMEM((8, width), F32),
+        a_own=pltpu.VMEM((4, 2, 2, 2) + block, BF16),
+        a_core=pltpu.VMEM((4, 2, 2) + block, BF16),
+        a_y=pltpu.VMEM((4, 2) + block, BF16),
+        a_z0=pltpu.VMEM((2, 2) + block, BF16),
+        a_x=pltpu.VMEM((2,) + block, BF16),
+        a_z1=pltpu.VMEM((1,) + block, BF16),
+        b_own=pltpu.VMEM((4,) + wide + (eight, 8, width), BF16),
+        **arrivals("b", 4, (eight, 8, width), BF16),
+        c_own=pltpu.VMEM((groups,) + wide + (eight, 8, 384), BF16),
+        **arrivals("c", groups, (eight, 8, 384), BF16),
+        o_own=pltpu.VMEM(wide + (eight, 8, width), BF16),
+        **arrivals("o", 1, (eight, 8, width), BF16),
+        unit_h=pltpu.VMEM(wide + (1, 8, 128), F32),
+        **arrivals("h", 1, (1, 8, 128), F32),
+        unit_v=pltpu.VMEM(wide + (1, 8, 128), F32),
+        **arrivals("v", 1, (1, 8, 128), F32),
+        send_sem=pltpu.SemaphoreType.DMA((87,)),
+        recv_sem=pltpu.SemaphoreType.DMA((87,)),
+        load_sem=pltpu.SemaphoreType.DMA((9,)),
+        w_sem=pltpu.SemaphoreType.DMA((4,)),
+    )
+    hbm = pl.BlockSpec(memory_space=pl.ANY)
+    operands = dict(
+        text_len=(text_len, smem_spec()),
+        patch_count=(patch_count, smem_spec()),
+        vecs=(vecs, whole_spec()),
+        hidden_in=(hidden, hbm),
+        cot_in=(cot, hbm),
+        wh=(wh, hbm),
+        wd=(wd, hbm),
+        order_in=(order, hbm),
+        wqkv=(wqkv, hbm),
+        wout=(wout, hbm),
+        seq_in=(seq, hbm),
+        q_in=(q, hbm),
+        k_in=(k, hbm),
+        v_in=(v, hbm),
+        mixed_in=(mixed_t, hbm),
+        normal_in=(normal_t, hbm),
+    )
+    final = shape((1, 2 * pairs, slots, width), BF16)
+    outs = dict(
+        block_out=(final, hbm),
+        input_grad=(final, hbm),
+        out_a=(shape(block, F32), whole_spec()),
+        out_b=(shape((eight, 8, 4 * width), F32), whole_spec()),
+        out_c=(shape((eight, 8, 3 * width), F32), whole_spec()),
+        out_o=(shape((eight, 8, width), F32), whole_spec()),
+        out_h=(shape((1, 8, 128), F32), whole_spec()),
+        out_v=(shape((1, 8, 128), F32), whole_spec()),
+    )
+    names = list(operands) + list(outs) + list(scratch)
+    return pl.pallas_call(
+        functools.partial(fused_kernel, pairs, slots, names),
+        out_shape=[kind for kind, _ in outs.values()],
+        in_specs=[spec for _, spec in operands.values()],
+        out_specs=[spec for _, spec in outs.values()],
+        scratch_shapes=list(scratch.values()),
+        compiler_params=pltpu.CompilerParams(
+            collective_id=1, has_side_effects=True, vmem_limit_bytes=67043328
+        ),
+        name="fused",
+    )(*[value for value, _ in operands.values()])
 
 
 def pair_bits():
@@ -440,61 +1278,115 @@
         return jnp.concatenate([patches, texts, blank], axis=1)
 
     def returned(array):
+        far_patches = lax.ppermute(array[:, :slots], "mod", [(0, 1)])
+        far_texts = lax.ppermute(array[:, slots : slots + TEXT], "mod", [(1, 0)])
+        return assembled(array, far_patches, far_texts)
+
+    def assembled(array, far_patches, far_texts):
         patches, texts = array[:, :slots], array[:, slots : slots + TEXT]
-        far_patches = lax.ppermute(patches, "mod", [(0, 1)])
-        far_texts = lax.ppermute(texts, "mod", [(1, 0)])
         texts = jnp.concatenate([texts, far_texts], axis=0)
         texts = jnp.pad(texts, ((0, 0), (0, slots - TEXT), (0, 0)))
         patches = jnp.concatenate([far_patches, patches], axis=0)
         return jnp.where(is_text, texts, patches)[None]
 
     row = lambda vector: vector.reshape(1, -1)
-    seq = gathered(inputs)
-    cot = gathered(cotangent)
-    qkv_bias = row(jnp.concatenate([query_bias, jnp.zeros_like(query_bias), value_bias]))
-    q, k, v, mixed, hidden = run_forward(
-        lens, seq, row(norm1_gain), row(norm1_bias), qkv_weight, qkv_bias, out_weight, row(out_bias), slots
-    )
-    result, ghidden, wh_grad, wd_grad, hb_grad, vec2 = run_feed(
-        lens,
-        hidden,
-        cot.reshape(half * rows, width),
-        row(norm2_gain),
-        row(norm2_bias),
-        hidden_weight,
-        row(hidden_bias),
-        down_weight,
-        row(down_bias),
-        half,
-        slots,
-        8,
-    )
-    block_out = returned(result.reshape(half, rows, width))
-    wd_out = scattered(wd_grad)
-    wh_out = scattered(wh_grad)
-    input_rows, qkvo_grad, vec1 = run_backward(
-        lens, seq, row(norm1_gain), row(norm1_bias), q, k, v, mixed, ghidden, qkv_weight, out_weight, slots
-    )
-    input_grad = returned(input_rows)
-    strip = jnp.concatenate([vec1[:4], vec2[:4]], axis=0).T
-    strip = jnp.concatenate([strip, hb_grad.reshape(width, -1)], axis=1).astype(BF16)
-    strip = jnp.pad(strip, ((0, 0), (0, 128 - strip.shape[1])))
-    qkvo_out = scattered(jnp.concatenate([qkvo_grad, strip], axis=1))
-    vec_out = qkvo_out[:, 4 * width :]
+    if lax.axis_size("pairs") == 16:
+        parts = [norm1_gain, norm1_bias, query_bias, value_bias, out_bias, norm2_gain, norm2_bias, down_bias, hidden_bias]
+        vecs = jnp.concatenate(parts).reshape(-1, width)
+        made = run_opening(text_len, patch_count, inputs, cotangent, vecs, qkv_weight, out_weight)
+        q, k, v, hidden, mixed, normal, seq, cot, order = made
+        made = run_fused(
+            text_len,
+            patch_count,
+            vecs,
+            hidden,
+            cot,
+            hidden_weight,
+            down_weight,
+            order,
+            qkv_weight,
+            out_weight,
+            seq,
+            q,
+            k,
+            v,
+            mixed,
+            normal,
+            slots,
+        )
+        block_out, input_grad, wd_out, wh_out, qkv_out, wo_out, hb_out, vec_out = made
+        flat = lambda array: array.reshape(-1, array.shape[-1])
+        wd_out, wh_out, qkv_out, wo_out = flat(wd_out), flat(wh_out), flat(qkv_out), flat(wo_out)
+        vec_out = vec_out[0, :, : width // 32].T
+        hb_out = hb_out[0, 0, : hidden_bias.shape[0] // 32]
+    else:
+        seq = gathered(inputs)
+        cot = gathered(cotangent).reshape(half * rows, width)
+        qkv_bias = row(jnp.concatenate([query_bias, jnp.zeros_like(query_bias), value_bias]))
+        feature = jnp.arange(width, dtype=jnp.int32)
+        order = (feature[:, None] == feature[None, :]).astype(BF16)
+        q, k, v, hidden, mixed = run_forward(
+            lens, seq, row(norm1_gain), row(norm1_bias), qkv_weight, qkv_bias, out_weight, row(out_bias), slots
+        )
+        chunks = 8
+        steps = jnp.arange(chunks, dtype=jnp.int32)
+        lens = jnp.concatenate([lens, jnp.zeros(4, jnp.int32), steps])
+        result, ghidden, wh_grad, wd_grad, hb_grad, vec2 = run_feed(
+            lens,
+            hidden,
+            cot,
+            row(norm2_gain),
+            row(norm2_bias),
+            hidden_weight,
+            row(hidden_bias),
+            down_weight,
+            row(down_bias),
+            order,
+            half,
+            slots,
+            chunks,
+            False,
+        )
+        block_out = returned(result.reshape(half, rows, width))
+        input_rows, qkvo_grad, vec1 = run_backward(
+            lens,
+            seq,
+            row(norm1_gain),
+            row(norm1_bias),
+            q,
+            k,
+            v,
+            mixed,
+            ghidden,
+            qkv_weight,
+            out_weight,
+            order,
+            slots,
+            False,
+        )
+        input_grad = returned(input_rows)
+        strip = jnp.concatenate([vec1[:4], vec2[:4]], axis=0).T
+        strip = jnp.concatenate([strip, hb_grad.reshape(width, -1)], axis=1).astype(BF16)
+        strip = jnp.pad(strip, ((0, 0), (0, 128 - strip.shape[1])))
+        wd_out, wh_out = scattered(wd_grad), scattered(wh_grad)
+        qkvo_out = scattered(jnp.concatenate([qkvo_grad, strip], axis=1))
+        vec_out = qkvo_out[:, 4 * width :]
+        qkv_out, wo_out = qkvo_out[:, : 3 * width], qkvo_out[:, 3 * width : 4 * width]
+        hb_out = vec_out[:, 8 : 8 + hidden_bias.shape[0] // width].reshape(-1)
     return (
         block_out,
         input_grad,
         vec_out[:, 0],
         vec_out[:, 1],
-        qkvo_out[:, : 3 * width],
+        qkv_out,
         vec_out[:, 2],
         vec_out[:, 3],
-        qkvo_out[:, 3 * width : 4 * width],
+        wo_out,
         vec_out[:, 7],
         vec_out[:, 4],
         vec_out[:, 5],
         wh_out,
-        vec_out[:, 8 : 8 + hidden_bias.shape[0] // width].reshape(-1),
+        hb_out,
         wd_out,
         vec_out[:, 6],
     )

time: 275 us -> 204 us (0.74)
  Pallas kernels: 76 us -> 187 us
  waiting for transfers between devices: 83.4 us -> 0 us
  starting transfers between devices: 64.4 us -> 0 us
  other arithmetic: 19.3 us -> 0.01 us
  local copies, waits for them, and re-layouts: 29.5 us -> 15.9 us
    pallas_call x3 -> x2, Pallas kernels: 76 us -> 187 us  [the longest x1 147 us: run_fused(): pl.pallas_call(functools.partial(fused_kernel, pairs, slots, names), out_...]
    ppermute x47 -> x0, waiting for transfers between devices: 83.4 us -> none  [the longest x39 40.5 us: swapped(): return lax.ppermute(array, axis, [(i, i ^ 1 << bit) for i in range(size)])]
    ppermute x47 -> x0, starting transfers between devices: 64.4 us -> none  [the longest x39 46.9 us: swapped(): return lax.ppermute(array, axis, [(i, i ^ 1 << bit) for i in range(size)])]
    slice x17 -> x0, local copies, waits for them, and re-layouts: 14 us -> none  [the longest x4 4.17 us: returned(): patches, texts = (array[:, :slots], array[:, slots:slots + TEXT])]
    unnamed x34 -> x24, local copies, waits for them, and re-layouts: 0.29 us -> 12.1 us
    dynamic_slice x8 -> x0, local copies, waits for them, and re-layouts: 8.54 us -> none  [the longest x4 5.09 us: half_sum(): kept = lax.dynamic_index_in_dim(array, mine, dim, keepdims=False)]
    convert_element_type x30 -> x0, other arithmetic: 7.38 us -> none  [half_sum(): total.astype(BF16)]
    concatenate x7 -> x0, other arithmetic: 6.5 us -> none  [the longest x1 2.69 us: on_device(): qkvo_out = scattered(jnp.concatenate([qkvo_grad, strip], axis=1))]
  transfers between devices with their start and end apart: 47 -> 0, of which waited for: 24 -> 0; matrix products, arithmetic and copies ran while one was open for 13% -> 0% of each run, Pallas kernels for 0% -> 0%
where the time goes in v3:
time: 204 us
  Pallas kernels  187 us (92%)
  local copies, waits for them, and re-layouts  15.9 us (8%)
    pallas_call x1, Pallas kernels, run_fused(): pl.pallas_call(functools.partial(fused_kernel, pairs, slots, names), out_...  147 us
    pallas_call x1, Pallas kernels, run_opening(): pl.pallas_call(functools.partial(opening_kernel, pairs, slots, names), ou...  40.4 us
    unnamed x24, local copies, waits for them, and re-layouts  12.1 us

profile of v3, /device:TPU:0, one launch (start us, length us, event | category | flops | bytes accessed | tf_op | source)
XLA Modules:
  0.0 203.8 jit_solution(5168218186869799193)
XLA Ops:
  0.7 0.7 constant_dynamic-update-slice_fusion.8
  1.3 0.7 constant_dynamic-update-slice_fusion.7
  2.0 0.7 constant_dynamic-update-slice_fusion.6
  2.7 0.7 constant_dynamic-update-slice_fusion.5
  3.4 0.7 constant_dynamic-update-slice_fusion.4
  4.1 0.7 constant_dynamic-update-slice_fusion.3
  4.8 0.7 constant_dynamic-update-slice_fusion.2
  5.5 0.7 constant_dynamic-update-slice_fusion.1
  6.2 0.7 constant_dynamic-update-slice_fusion
  6.9 0.6 reshape.45.refs_4_.refs_2_
  7.5 40.4 %opening.1 = (bf16[2,288,768]{2,1,0:T(8,128)(2,1)}, bf16[2,288,768]{2,1,0:T(8,128)(2,1)}, bf16[2,288,768]{2,1,0:T(8,128)(2,1)}, f32[576,768]{1,0:T(8,128)}, bf16...) custom-call(s32[4]{0:T(128)} %refs_0_.3, ...), custom_call_target="tpu_custom_call" | custom-call | tf_op jit(solution)/shard_map/opening/pallas_call | solution.py:685
  47.9 146.9 %fused.1 = (bf16[1,4,240,768]{3,2,1,0:T(8,128)(2,1)}, bf16[1,4,240,768]{3,2,1,0:T(8,128)(2,1)}, f32[12,8,768]{2,1,0:T(8,128)}, f32[3,8,3072]{2,1,0:T(8,128)}, f3...) custom-call(s32[4]{0:T(128)} %refs_0_.3, s32[4]{0:T(128)} %refs_1_.3, ...), custom_call_target="tpu_custom_call" | custom-call | tf_op jit(solution)/shard_map/fused/pallas_call | solution.py:1182
  194.8 1.2 slice_bitcast_fusion.2
  196.0 0.7 slice_bitcast_fusion
  196.7 0.5 slice_bitcast_fusion.1
  197.2 0.0 copy-start
  197.2 2.7 %copy.47 = bf16[1,4,240,768]{3,2,1,0:T(8,128)(2,1)} copy(bf16[1,4,240,768]{3,2,1,0:T(8,128)(2,1)} %get-tuple-element.72) | data formatting | bytes 2949120
  199.9 0.0 copy-done
  199.9 0.0 copy-start.3
  199.9 0.0 copy-start.4
  199.9 0.0 copy-start.2
  199.9 0.0 copy-start.1
  199.9 1.1 copy.48
  201.1 0.0 copy-done.3
  201.1 0.7 copy.49
  201.7 0.0 copy-done.4
  201.7 0.6 copy.50
  202.4 0.0 copy-done.2
  202.4 0.7 copy.51
  203.1 0.0 copy-done.1
  203.1 0.7 copy.52
  (1 shorter events, 0.0 us)
Async XLA Ops:
  197.2 2.7 %copy-start = (bf16[1,4,240,768]{3,2,1,0:T(8,128)(2,1)S(1)}, bf16[1,4,240,768]{3,2,1,0:T(8,128)(2,1)}, u32[]{:S(2)}) copy-start(bf16[1,4,240,768]{3,2,1,0:T(8,128)(2,1)} %get-tuple-element.73) | copy-start | bytes 4423684
  199.9 1.1 copy-start.3
  199.9 1.8 copy-start.4
  199.9 2.5 %copy-start.2 = (f32[3,8,3072]{2,1,0:T(8,128)S(1)}, f32[3,8,3072]{2,1,0:T(8,128)}, u32[]{:S(2)}) copy-start(f32[3,8,3072]{2,1,0:T(8,128)} %get-tuple-element.46) | copy-start | bytes 884740
  199.9 3.2 %copy-start.1 = (f32[12,8,768]{2,1,0:T(8,128)S(1)}, f32[12,8,768]{2,1,0:T(8,128)}, u32[]{:S(2)}) copy-start(f32[12,8,768]{2,1,0:T(8,128)} %get-tuple-element.48) | copy-start | bytes 884740

commit v4 on v3

--- a/solution.py
+++ b/solution.py
@@ -693,6 +693,48 @@
     )(*[value for value, _ in operands.values()])
 
 
+A, B, C, O, H, V, R = range(7)
+PLAN = {
+    3: [(A, 0, 0)],
+    4: [(B, 0, 0)],
+    5: [(A, 0, 1)],
+    6: [(B, 1, 0)],
+    7: [(A, 0, 2), (A, 1, 0)],
+    8: [(B, 2, 0), (B, 2, 1), (A, 1, 1)],
+    10: [(B, 3, 0), (B, 3, 1)],
+    11: [(A, 1, 2), (A, 2, 0), (B, 3, 2), (B, 4, 0)],
+    12: [(A, 2, 1), (B, 0, 1), (B, 2, 2)],
+    13: [(A, 0, 3), (B, 1, 1), (B, 3, 3), (B, 5, 0)],
+    14: [(B, 2, 3), (A, 2, 2), (A, 3, 0)],
+    15: [(B, 1, 2)],
+    16: [(B, 0, 2), (B, 1, 3), (B, 6, 0), (B, 6, 1), (A, 3, 1), (R, 0, 0)],
+    17: [(B, 7, 0), (B, 7, 1), (H, 0, 0), (B, 0, 3), (R, 0, 1)],
+    18: [(A, 3, 2), (B, 7, 2)],
+    19: [(B, 6, 2)],
+    20: [(B, 4, 1)],
+    21: [(O, 0, 0), (R, 0, 2)],
+    22: [(A, 1, 3), (B, 5, 1), (B, 7, 3), (H, 0, 1), (A, 0, 4), (B, 7, 4), (B, 5, 2), (B, 6, 3), (B, 6, 4), (R, 0, 3)],
+    23: [(R, 0, 4)],
+    24: [(B, 5, 3), (B, 2, 4), (B, 3, 4), (B, 5, 4), (R, 0, 5)],
+    25: [(O, 0, 1), (R, 0, 6)],
+    26: [(B, 4, 2), (H, 0, 2), (B, 1, 4), (R, 0, 7)],
+    27: [(C, 0, 0), (R, 0, 8)],
+    28: [(O, 0, 2), (C, 1, 0), (B, 4, 3), (H, 0, 3), (B, 4, 4), (R, 0, 9)],
+    29: [(C, 2, 0), (R, 1, 0)],
+    30: [(C, 0, 1), (O, 0, 3), (C, 3, 0), (B, 0, 4), (H, 0, 4), (R, 1, 1)],
+    31: [(C, 1, 1), (C, 4, 0), (R, 1, 2)],
+    32: [(C, 0, 2), (C, 2, 1), (C, 5, 0), (O, 0, 4), (R, 1, 3)],
+}
+TAIL = [
+    (C, 1, 2), (V, 0, 0), (C, 3, 1), (R, 1, 4), (C, 0, 3), (C, 2, 2),
+    (C, 4, 1), (R, 2, 0), (C, 1, 3), (C, 3, 2), (C, 5, 1), (R, 2, 1),
+    (C, 2, 3), (V, 0, 1), (C, 0, 4), (C, 4, 2), (R, 2, 2), (C, 3, 3),
+    (C, 5, 2), (V, 0, 2), (C, 1, 4), (C, 4, 3), (R, 2, 3), (C, 2, 4),
+    (C, 5, 3), (R, 2, 4), (V, 0, 3), (C, 3, 4), (C, 4, 4), (C, 5, 4),
+    (V, 0, 4),
+]
+
+
 def fused_kernel(pairs, slots, names, *refs):
     r = types.SimpleNamespace(**dict(zip(names, refs)))
     rows, width = r.seq.shape[1:]
@@ -765,10 +807,6 @@
             copy.start()
 
     arrivals = lambda name, index: [getattr(r, name + str(step)).at[index] for step in range(5)]
-    tasks = {}
-
-    def at(tick, action):
-        tasks.setdefault(tick, []).append(action)
 
     a_core = lambda t, y: hop("core", r.a_own.at[t, 1, y], r.a_core.at[t, y], sems, 2 * t + y)
     a_y = lambda t: hop("y", r.a_own.at[t, 0, 1], r.a_y.at[t], sems, 8 + t)
@@ -776,12 +814,11 @@
     a_x = lambda k: hop("x", r.a_own.at[2 * k + 1, 0, 0, 1], r.a_x.at[k], sems, 14 + k)
     a_z1 = lambda: hop("z1", r.a_own.at[1, 0, 0, 0], r.a_z1.at[0], sems, 16)
 
-    def a_first(t):
-        a_core(t, 1).wait_recv()
-        accumulate(r.a_own.at[t, 0, 1], r.a_core.at[t, 1])
-        a_y(t).start()
-        a_core(t, 0).wait_recv()
-        accumulate(r.a_own.at[t, 0, 0], r.a_core.at[t, 0])
+    def a_core_sum(t, y):
+        a_core(t, y).wait_recv()
+        accumulate(r.a_own.at[t, 0, y], r.a_core.at[t, y])
+        if y == 1:
+            a_y(t).start()
 
     def a_second(t):
         k = t // 2
@@ -804,16 +841,14 @@
         a_z1().wait_recv()
         r.out_a[...] = r.a_own[3, 0, 0, 0].astype(F32) + r.a_z1[0].astype(F32)
 
-    for t in range(4):
-        at(2 * t + 2, functools.partial(a_first, t))
-        at(2 * t + 4, functools.partial(a_second, t))
-    at(8, functools.partial(a_third, 0))
-    at(12, functools.partial(a_third, 1))
-    at(14, a_last)
-
-    def b_finish(t):
+    size = width // 2
+
+    def b_columns(u):
+        return block_of(u // 2) * width + flip(1 - u % 2, here["y"]) * size
+
+    def b_finish(u):
         def finish(value):
-            r.out_b[:, :, pl.ds(pl.multiple_of(block_of(t) * width, width), width)] = value
+            r.out_b[:, :, pl.ds(pl.multiple_of(b_columns(u), 128), size)] = value
 
         return finish
 
@@ -825,50 +860,92 @@
 
         return finish
 
-    def o_finish(value):
-        r.out_o[...] = value
-
-    def plain(name):
+    def plain(target):
         def finish(value):
-            getattr(r, name)[...] = value
+            target[...] = value
 
         return finish
 
     units = {}
-    for t in range(4):
-        units["b", t] = Unit(r.b_own.at[t], arrivals("b", t), ORDERS[1], sems, 20 + 5 * t, b_finish(t))
-    for t in range(4):
-        units["b", t].peers = {"z0": units["b", t ^ 1], "z1": units["b", t ^ 2]}
+    for u in range(8):
+        units[B, u] = Unit(r.b_own.at[u], arrivals("b", u), ORDERS[1], sems, 20 + 5 * u, b_finish(u))
+    for u in range(8):
+        units[B, u].peers = {"y": units[B, u ^ 1], "z0": units[B, u ^ 2], "z1": units[B, u ^ 4]}
     groups = width // 128
     for g in range(groups):
-        units["c", g] = Unit(r.c_own.at[g], arrivals("c", g), ORDERS[g % 2], sems, 40 + 5 * g, c_finish(g))
-    units["o", 0] = Unit(r.o_own, arrivals("o", 0), ORDERS[0], sems, 70, o_finish)
-    units["h", 0] = Unit(r.unit_h, arrivals("h", 0), ORDERS[1], sems, 75, plain("out_h"))
-    units["v", 0] = Unit(r.unit_v, arrivals("v", 0), ORDERS[0], sems, 80, plain("out_v"))
-    plans = {
-        ("b", 0): [2, 6, 8, 10, 15],
-        ("b", 1): [4, 6, 8, 10, 15],
-        ("b", 2): [6, 11, 13, 14, 16],
-        ("b", 3): [8, 11, 13, 14, 16],
-    }
-    plans["o", 0] = [9, 13, 15, 16, 17]
-    plans["h", 0] = [9, 10, 11, 12, 13]
-    for g in range(groups):
-        plans["c", g] = [11 + 2 * g, 13 + 2 * g, 14 + 2 * g, 15 + 2 * g, 16 + 2 * g]
-    for key, ticks in plans.items():
-        for step, tick in enumerate(ticks):
-            at(tick, functools.partial(units[key].advance, step))
+        units[C, g] = Unit(r.c_own.at[g], arrivals("c", g), ORDERS[(g + 1) % 2], sems, 60 + 5 * g, c_finish(g))
+    units[O, 0] = Unit(r.o_own, arrivals("o", 0), ORDERS[0], sems, 90, plain(r.out_o))
+    units[H, 0] = Unit(r.unit_h, arrivals("h", 0), ORDERS[1], sems, 95, plain(r.out_h))
+    units[V, 0] = Unit(r.unit_v, arrivals("v", 0), ORDERS[0], sems, 100, plain(r.out_v))
+
+    def give(source, target, pair, index):
+        near = lambda src, dst: pltpu.make_async_copy(src, dst, r.give_sem.at[index])
+        part = lambda first, count: hop(
+            "x", source.at[pair, pl.ds(first, count)], target.at[0, pair, pl.ds(first, count)], sems, 105 + index
+        )
+        patches, texts = source.at[pair, pl.ds(0, slots)], source.at[pair, pl.ds(slots, tail)]
+        far_texts = hop("x", texts, target.at[0, pairs + pair, pl.ds(0, tail)], sems, 105 + index)
+        near_texts = lambda: near(texts, target.at[0, pair, pl.ds(0, tail)])
+        near_patches = lambda: near(patches, target.at[0, pairs + pair])
+        return part, far_texts, near_texts, near_patches
+
+    gives = [give(r.result, r.block_out, pair, pair) for pair in range(pairs)]
+    gives += [give(r.grad_rows, r.input_grad, pair, pairs + pair) for pair in range(pairs)]
+
+    def give_start(index):
+        _, far_texts, near_texts, near_patches = gives[index]
+
+        @pl.when(here["x"] == 0)
+        def _():
+            near_texts().start()
+
+        @pl.when(here["x"] == 1)
+        def _():
+            far_texts.start()
+            near_patches().start()
+
+    def give_part(index, piece):
+        @pl.when(here["x"] == 0)
+        def _():
+            gives[index][0](tail * piece, tail).start()
+
+    def give_wait(index):
+        part, far_texts, near_texts, near_patches = gives[index]
+
+        @pl.when(here["x"] == 0)
+        def _():
+            far_texts.wait_recv()
+            part(0, slots).wait_send()
+            near_texts().wait()
+
+        @pl.when(here["x"] == 1)
+        def _():
+            part(0, slots).wait_recv()
+            far_texts.wait_send()
+            near_patches().wait()
+
+    def act(kind, piece, step):
+        if kind == R:
+            pieces = slots // tail
+            give_part(step // pieces if piece == 0 else pairs + piece - 1, step % pieces)
+        elif kind != A:
+            units[kind, piece].advance(step)
+        elif step < 2:
+            a_core_sum(piece, 1 - step)
+        else:
+            (a_second, a_third, lambda _: a_last())[step - 2](piece)
+
+    def run_now(tick):
+        for item in PLAN.get(tick, []):
+            act(*item)
 
     def run_tasks(ticks, now):
         for tick in ticks:
-            if tick in tasks:
+            if tick in PLAN:
 
                 @pl.when(now == tick)
                 def _(tick=tick):
-                    for action in tasks[tick]:
-                        action()
-
-    size = width // 2
+                    run_now(tick)
 
     def feed_step(t, carry):
         slot = t % 2
@@ -881,7 +958,7 @@
                 copy.start()
 
         for sub in range(2):
-            run_tasks([2 * k + sub for k in range(4)], 2 * t + sub)
+            run_tasks([4 * k + 2 * sub for k in range(4)], 4 * t + 2 * sub)
             y = 1 - sub
             part = flip(y, here["y"])
             start = pl.multiple_of(part * size, size)
@@ -899,11 +976,14 @@
                     piece = fresh[first : first + quarter].reshape(quarter // 8, 8, width)
                     r.a_own[t, flip(core, here["core"]), y, flip(mod, here["x"])] = piece.astype(BF16)
             a_core(t, y).start()
+            run_tasks([4 * k + 2 * sub + 1 for k in range(4)], 4 * t + 2 * sub + 1)
             gbefore = (dot(r.gdown[...], wd, 1, 1) * slope).astype(BF16)
             r.gnormal[...] += dot(gbefore, wh, 1, 1)
             fresh = dot(r.normal2_t[...], gbefore)
             fresh = fresh.reshape((2,) * 5 + (width // 256, 8, size)).astype(BF16)
-            r.b_own[t, :, :, :, :, :, :, :, pl.ds(start, size)] = fresh
+            unit = 2 * t + sub
+            r.b_own[unit] = fresh
+            hop("core", r.b_own.at[unit, 1], r.b0.at[unit], sems, 20 + 5 * unit).start()
             sums = jnp.sum(gbefore.astype(F32), axis=0, keepdims=True)
             z1, z0 = 1 - t // 2, 1 - t % 2
             for core in range(2):
@@ -912,7 +992,6 @@
                     r.unit_h[
                         flip(core, here["core"]), y, z0, flip(mod, here["x"]), z1, 0, 0:1, 0:quarter
                     ] = sums[:, first : first + quarter]
-        hop("core", r.b_own.at[t, 1], r.b0.at[t], sems, 20 + 5 * t).start()
         return carry
 
     lax.fori_loop(0, 4, feed_step, 0)
@@ -927,39 +1006,12 @@
     ]
     for copy in wqkv_loads:
         copy.start()
-    units["h", 0].start()
+    units[H, 0].start()
     r.result[...] = (r.total[...] * live).astype(BF16).reshape(pairs, rows, width)
 
-    def give(source, target, index):
-        near = lambda src, dst: pltpu.make_async_copy(src, dst, r.give_sem.at[index])
-        first_pairs, last_pairs = pl.ds(0, pairs), pl.ds(pairs, pairs)
-        patches, texts = source.at[:, pl.ds(0, slots)], source.at[:, pl.ds(slots, tail)]
-        return (
-            hop("x", patches, target.at[0, first_pairs], sems, 85 + index),
-            hop("x", texts, target.at[0, last_pairs, pl.ds(0, tail)], sems, 85 + index),
-            near(patches, target.at[0, last_pairs]),
-            near(texts, target.at[0, first_pairs, pl.ds(0, tail)]),
-        )
-
-    def give_start(copies):
-        for which in range(2):
-
-            @pl.when(here["x"] == which)
-            def _():
-                copies[which].start()
-                copies[3 - which].start()
-
-    def give_wait(copies):
-        for which in range(2):
-
-            @pl.when(here["x"] == which)
-            def _():
-                copies[1 - which].wait_recv()
-                copies[which].wait_send()
-                copies[3 - which].wait()
-
-    result_copies = give(r.result, r.block_out, 0)
-    give_start(result_copies)
+    for pair in range(pairs):
+        give_start(pair)
+    run_now(16)
     normed, factor = norm_parts(r.hidden[...])
     gnorm = r.gnormal[...]
     down = r.gdown[...].astype(F32)
@@ -974,85 +1026,102 @@
     for index, value in enumerate(vec):
         r.vec[4 + index : 5 + index, :] = value
     r.gnormal[...] = made
+    run_now(17)
     wout_load.wait()
     r.gmixed[...] = dot(gattended, r.wbuf[3], 1, 1).astype(BF16).reshape(pairs, rows, width)
     for copy in late:
         copy.wait()
     fresh = dot(r.mixed_t[...], gattended)
     r.o_own[...] = fresh.reshape((2,) * 5 + (width // 256, 8, width)).astype(BF16)
-    units["o", 0].start()
+    units[O, 0].start()
+    for copy in wqkv_loads:
+        copy.wait()
 
     first = lax.broadcasted_iota(jnp.int32, (rows, 128), 1) < HEAD_DIM
     index = lax.broadcasted_iota(jnp.int32, (rows, 1), 0)
 
-    def head_step(g, carry):
+    def project_back(pair):
+        made = jnp.zeros((rows, width), F32)
+        sums = []
+        for part in range(3):
+            piece = r.gproj[pair, :, part * width : (part + 1) * width]
+            made += dot(piece, r.wbuf[part], 1, 1)
+            sums.append(jnp.sum(piece.astype(F32), axis=0, keepdims=True))
+        return made, sums
+
+    def finish_pair(pair, grad, sums):
+        normed, factor = norm_parts(r.seq[pair].astype(F32))
+        sums = [
+            jnp.sum(grad * normed, axis=0, keepdims=True),
+            jnp.sum(grad, axis=0, keepdims=True),
+            sums[0],
+            sums[2],
+        ]
+        for index, value in enumerate(sums):
+            r.vec[index : index + 1, :] = value if pair == 0 else r.vec[index : index + 1, :] + value
+        span = slice(pair * rows, (pair + 1) * rows)
+        made = r.gnormal[span, :] + norm_back(grad, normed, factor, vec_in(0))
+        r.grad_rows[pair] = (made * live[span]).astype(BF16)
+        give_start(pairs + pair)
+
+    def head_step(it, carry):
+        pair, g = it // groups, it % groups
         base = g * 128
         off = pl.multiple_of(base, 128)
-        for pair in range(pairs):
-            run_tasks([8 + 2 * k + pair for k in range(groups)], 8 + 2 * g + pair)
-            keys_live = live_slots(index, lens[pair], lens[pairs + pair], slots)
-            q2 = r.q[pair, :, pl.ds(off, 128)]
-            k2 = r.k[pair, :, pl.ds(off, 128)]
-            v2 = r.v[pair, :, pl.ds(off, 128)]
-            g2 = r.gmixed[pair, :, pl.ds(off, 128)]
-            gq = gk = gv = None
-            for half in range(2):
-                keep = first if half == 0 else ~first
-                zero = jnp.zeros_like(q2)
-                qm = jnp.where(keep, q2, zero)
-                km = jnp.where(keep, k2, zero)
-                gm = jnp.where(keep, g2, zero)
-                scores = jnp.where(keys_live, dot(k2, qm, 1, 1), MASKED)
-                highest = jnp.max(scores, axis=0, keepdims=True)
-                shifted = jnp.exp(scores - highest)
-                probs = shifted * (1.0 / jnp.sum(shifted, axis=0, keepdims=True))
-                gprobs = dot(v2, gm, 1, 1)
-                row_dot = jnp.sum(probs * gprobs, axis=0, keepdims=True)
-                gscores = (probs * (gprobs - row_dot)).astype(BF16)
-                new_v = dot(probs.astype(BF16), gm)
-                new_k = dot(gscores, qm)
-                new_q = dot(gscores, km, 0, 0)
-                gq = new_q if gq is None else gq + new_q
-                gk = new_k if gk is None else gk + new_k
-                gv = new_v if gv is None else gv + new_v
-            r.gproj[pair, :, pl.ds(off, 128)] = (gq * 0.125).astype(BF16)
-            r.gproj[pair, :, pl.ds(pl.multiple_of(base + width, 128), 128)] = gk.astype(BF16)
-            r.gproj[pair, :, pl.ds(pl.multiple_of(base + 2 * width, 128), 128)] = gv.astype(BF16)
-        pieces = [
-            r.gproj[:, :, pl.ds(pl.multiple_of(base + part * width, 128), 128)].reshape(every, 128)
-            for part in range(3)
-        ]
-        fresh = dot(r.normal_t[...], jnp.concatenate(pieces, axis=1))
-        r.c_own[g] = fresh.reshape((2,) * 5 + (width // 256, 8, 384)).astype(BF16)
-        hop("core", r.c_own.at[g, 1], r.c0.at[g], sems, 40 + 5 * g).start()
+
+        @pl.when(it == groups)
+        def _():
+            finish_pair(0, *project_back(0))
+
+        run_tasks([18 + k for k in range(pairs * groups)], 18 + it)
+        at_pair = here["x"] * pairs + pair
+        keys_live = live_slots(index, r.text_len[at_pair], r.patch_count[at_pair], slots)
+        q2 = r.q[pair, :, pl.ds(off, 128)]
+        k2 = r.k[pair, :, pl.ds(off, 128)]
+        v2 = r.v[pair, :, pl.ds(off, 128)]
+        g2 = r.gmixed[pair, :, pl.ds(off, 128)]
+        gq = gk = gv = None
+        for half in range(2):
+            keep = first if half == 0 else ~first
+            zero = jnp.zeros_like(q2)
+            qm = jnp.where(keep, q2, zero)
+            km = jnp.where(keep, k2, zero)
+            gm = jnp.where(keep, g2, zero)
+            scores = jnp.where(keys_live, dot(k2, qm, 1, 1), MASKED)
+            highest = jnp.max(scores, axis=0, keepdims=True)
+            shifted = jnp.exp(scores - highest)
+            probs = shifted * (1.0 / jnp.sum(shifted, axis=0, keepdims=True))
+            gprobs = dot(v2, gm, 1, 1)
+            row_dot = jnp.sum(probs * gprobs, axis=0, keepdims=True)
+            gscores = (probs * (gprobs - row_dot)).astype(BF16)
+            new_v = dot(probs.astype(BF16), gm)
+            new_k = dot(gscores, qm)
+            new_q = dot(gscores, km, 0, 0)
+            gq = new_q if gq is None else gq + new_q
+            gk = new_k if gk is None else gk + new_k
+            gv = new_v if gv is None else gv + new_v
+        r.gproj[pair, :, pl.ds(off, 128)] = (gq * 0.125).astype(BF16)
+        r.gproj[pair, :, pl.ds(pl.multiple_of(base + width, 128), 128)] = gk.astype(BF16)
+        r.gproj[pair, :, pl.ds(pl.multiple_of(base + 2 * width, 128), 128)] = gv.astype(BF16)
+
+        @pl.when(it >= (pairs - 1) * groups)
+        def _():
+            pieces = [
+                r.gproj[:, :, pl.ds(pl.multiple_of(base + part * width, 128), 128)].reshape(every, 128)
+                for part in range(3)
+            ]
+            fresh = dot(r.normal_t[...], jnp.concatenate(pieces, axis=1))
+            r.c_own[g] = fresh.reshape((2,) * 5 + (width // 256, 8, 384)).astype(BF16)
+            hop("core", r.c_own.at[g, 1], r.c0.at[g], sems, 60 + 5 * g).start()
+
         return carry
 
-    lax.fori_loop(0, groups, head_step, 0)
-
-    def run_now(tick):
-        for action in tasks.get(tick, []):
-            action()
-
-    tokens = r.seq[...].reshape(every, width).astype(F32)
-    normed, factor = norm_parts(tokens)
-    gnormal = jnp.zeros((every, width), F32)
-    for part in range(3):
-        run_now(20 + part)
-        piece = r.gproj[:, :, part * width : (part + 1) * width].reshape(every, width)
-        wqkv_loads[part].wait()
-        gnormal += dot(piece, r.wbuf[part], 1, 1)
-        if part == 0:
-            r.vec[2:3, :] = jnp.sum(piece.astype(F32), axis=0, keepdims=True)
-        if part == 2:
-            r.vec[3:4, :] = jnp.sum(piece.astype(F32), axis=0, keepdims=True)
-    run_now(23)
-    r.vec[0:1, :] = jnp.sum(gnormal * normed, axis=0, keepdims=True)
-    r.vec[1:2, :] = jnp.sum(gnormal, axis=0, keepdims=True)
-    made = r.gnormal[...] + norm_back(gnormal, normed, factor, vec_in(0))
-    r.grad_rows[...] = (made * live).astype(BF16).reshape(pairs, rows, width)
-    grad_copies = give(r.grad_rows, r.input_grad, 1)
-    give_start(grad_copies)
-    run_now(24)
+    lax.fori_loop(0, pairs * groups, head_step, 0)
+
+    run_now(30)
+    made, sums = project_back(1)
+    run_now(31)
+    finish_pair(1, made, sums)
     rest = r.vec[...]
     ordered = jnp.zeros_like(rest)
     for _ in range(3):
@@ -1064,13 +1133,12 @@
     for block in range(32):
         bits = tuple(block >> shift & 1 for shift in (4, 3, 2, 1, 0))
         r.unit_v[bits + (0, slice(None), slice(0, unit))] = ordered[:, block * unit : (block + 1) * unit]
-    units["v", 0].start()
-    run_now(25)
-    run_now(26)
-    for step in range(5):
-        units["v", 0].advance(step)
-    give_wait(result_copies)
-    give_wait(grad_copies)
+    units[V, 0].start()
+    run_now(32)
+    for item in TAIL:
+        act(*item)
+    for number in range(2 * pairs):
+        give_wait(number)
 
     @pl.when(here["x"] == 0)
     def _():
@@ -1108,7 +1176,7 @@
         result=cube,
         grad_rows=cube,
         zeros=pltpu.VMEM((slots - (rows - slots), width), BF16),
-        give_sem=pltpu.SemaphoreType.DMA((2,)),
+        give_sem=pltpu.SemaphoreType.DMA((2 * pairs,)),
         zero_sem=pltpu.SemaphoreType.DMA((4 * pairs,)),
         hidden=flat(F32),
         gdown=flat(BF16),
@@ -1133,8 +1201,8 @@
         a_z0=pltpu.VMEM((2, 2) + block, BF16),
         a_x=pltpu.VMEM((2,) + block, BF16),
         a_z1=pltpu.VMEM((1,) + block, BF16),
-        b_own=pltpu.VMEM((4,) + wide + (eight, 8, width), BF16),
-        **arrivals("b", 4, (eight, 8, width), BF16),
+        b_own=pltpu.VMEM((8,) + wide + (eight, 8, width // 2), BF16),
+        **arrivals("b", 8, (eight, 8, width // 2), BF16),
         c_own=pltpu.VMEM((groups,) + wide + (eight, 8, 384), BF16),
         **arrivals("c", groups, (eight, 8, 384), BF16),
         o_own=pltpu.VMEM(wide + (eight, 8, width), BF16),
@@ -1143,8 +1211,8 @@
         **arrivals("h", 1, (1, 8, 128), F32),
         unit_v=pltpu.VMEM(wide + (1, 8, 128), F32),
         **arrivals("v", 1, (1, 8, 128), F32),
-        send_sem=pltpu.SemaphoreType.DMA((87,)),
-        recv_sem=pltpu.SemaphoreType.DMA((87,)),
+        send_sem=pltpu.SemaphoreType.DMA((105 + 2 * pairs,)),
+        recv_sem=pltpu.SemaphoreType.DMA((105 + 2 * pairs,)),
         load_sem=pltpu.SemaphoreType.DMA((9,)),
         w_sem=pltpu.SemaphoreType.DMA((4,)),
     )

time: 204 us -> 161 us (0.79)
  Pallas kernels: 187 us -> 144 us
    pallas_call x1, Pallas kernels: 147 us -> 104 us  [run_fused(): pl.pallas_call(functools.partial(fused_kernel, pairs, slots, names), out_...]
where the time goes in v4:
time: 161 us
  Pallas kernels  144 us (89%)
  local copies, waits for them, and re-layouts  15.9 us (10%)
    pallas_call x1, Pallas kernels, run_fused(): pl.pallas_call(functools.partial(fused_kernel, pairs, slots, names), out_...  104 us
    pallas_call x1, Pallas kernels, run_opening(): pl.pallas_call(functools.partial(opening_kernel, pairs, slots, names), ou...  40.4 us
    unnamed x24, local copies, waits for them, and re-layouts  12.1 us

profile of v4, /device:TPU:0, one launch (start us, length us, event | category | flops | bytes accessed | tf_op | source)
XLA Modules:
  0.0 160.8 jit_solution(5739036859642886645)
XLA Ops:
  0.7 0.7 constant_dynamic-update-slice_fusion.8
  1.3 0.7 constant_dynamic-update-slice_fusion.7
  2.0 0.7 constant_dynamic-update-slice_fusion.6
  2.7 0.7 constant_dynamic-update-slice_fusion.5
  3.4 0.7 constant_dynamic-update-slice_fusion.4
  4.1 0.7 constant_dynamic-update-slice_fusion.3
  4.8 0.7 constant_dynamic-update-slice_fusion.2
  5.5 0.7 constant_dynamic-update-slice_fusion.1
  6.2 0.7 constant_dynamic-update-slice_fusion
  6.9 0.6 reshape.45.refs_4_.refs_2_
  7.5 40.4 %opening.1 = (bf16[2,288,768]{2,1,0:T(8,128)(2,1)}, bf16[2,288,768]{2,1,0:T(8,128)(2,1)}, bf16[2,288,768]{2,1,0:T(8,128)(2,1)}, f32[576,768]{1,0:T(8,128)}, bf16...) custom-call(s32[4]{0:T(128)} %refs_0_.3, ...), custom_call_target="tpu_custom_call" | custom-call | tf_op jit(solution)/shard_map/opening/pallas_call | solution.py:685
  47.9 103.8 %fused.1 = (bf16[1,4,240,768]{3,2,1,0:T(8,128)(2,1)}, bf16[1,4,240,768]{3,2,1,0:T(8,128)(2,1)}, f32[12,8,768]{2,1,0:T(8,128)}, f32[3,8,3072]{2,1,0:T(8,128)}, f3...) custom-call(s32[4]{0:T(128)} %refs_0_.3, s32[4]{0:T(128)} %refs_1_.3, ...), custom_call_target="tpu_custom_call" | custom-call | tf_op jit(solution)/shard_map/fused/pallas_call | solution.py:1250
  151.8 1.2 slice_bitcast_fusion.2
  153.0 0.7 slice_bitcast_fusion
  153.6 0.5 slice_bitcast_fusion.1
  154.2 0.0 copy-start
  154.2 2.7 %copy.47 = bf16[1,4,240,768]{3,2,1,0:T(8,128)(2,1)} copy(bf16[1,4,240,768]{3,2,1,0:T(8,128)(2,1)} %get-tuple-element.72) | data formatting | bytes 2949120
  156.9 0.0 copy-done
  156.9 0.0 copy-start.3
  156.9 0.0 copy-start.4
  156.9 0.0 copy-start.2
  156.9 0.0 copy-start.1
  156.9 1.1 copy.48
  158.0 0.0 copy-done.3
  158.0 0.7 copy.49
  158.7 0.0 copy-done.4
  158.7 0.6 copy.50
  159.3 0.0 copy-done.2
  159.3 0.7 copy.51
  160.1 0.0 copy-done.1
  160.1 0.7 copy.52
  (1 shorter events, 0.0 us)
Async XLA Ops:
  154.2 2.7 %copy-start = (bf16[1,4,240,768]{3,2,1,0:T(8,128)(2,1)S(1)}, bf16[1,4,240,768]{3,2,1,0:T(8,128)(2,1)}, u32[]{:S(2)}) copy-start(bf16[1,4,240,768]{3,2,1,0:T(8,128)(2,1)} %get-tuple-element.73) | copy-start | bytes 4423684
  156.9 1.1 copy-start.3
  156.9 1.8 %copy-start.4 = (f32[3,8,768]{2,1,0:T(8,128)S(1)}, f32[3,8,768]{2,1,0:T(8,128)}, u32[]{:S(2)}) copy-start(f32[3,8,768]{2,1,0:T(8,128)} %get-tuple-element.45) | copy-start | bytes 221188
  156.9 2.5 %copy-start.2 = (f32[3,8,3072]{2,1,0:T(8,128)S(1)}, f32[3,8,3072]{2,1,0:T(8,128)}, u32[]{:S(2)}) copy-start(f32[3,8,3072]{2,1,0:T(8,128)} %get-tuple-element.46) | copy-start | bytes 884740
  156.9 3.2 %copy-start.1 = (f32[12,8,768]{2,1,0:T(8,128)S(1)}, f32[12,8,768]{2,1,0:T(8,128)}, u32[]{:S(2)}) copy-start(f32[12,8,768]{2,1,0:T(8,128)} %get-tuple-element.48) | copy-start | bytes 884740

commit v5 on v4

--- a/solution.py
+++ b/solution.py
@@ -463,17 +463,23 @@
 
 def accumulate(target, source):
     lead = target.shape[:-3]
+    tiles = target.shape[-3] * target.shape[-2] * target.shape[-1] // 1024
+    while lead and tiles * lead[-1] <= 72:
+        tiles *= lead[-1]
+        lead = lead[:-1]
     count = 1
     for size in lead:
         count *= size
+
+    def add(at):
+        target[at] = target[at] + source[at]
+
     if count == 1:
-        at = (0,) * len(lead)
-        target[at] = target[at] + source[at]
+        add((0,) * len(lead) if lead else (Ellipsis,))
         return
 
     def body(it, carry):
-        at = lead_index(it, lead)
-        target[at] = target[at] + source[at]
+        add(lead_index(it, lead))
         return carry
 
     lax.fori_loop(0, count, body, 0)
@@ -591,6 +597,12 @@
     owner = owner ^ (lax.axis_index("pairs") * 2 + here["x"])
     source = owner * unit + (place_at - block * unit)
     r.order[...] = (source == feature).astype(F32).astype(BF16)
+    row = 0
+    for index in range(9):
+        part = getattr(r, str(index))
+        for first in range(0, part.shape[0], width):
+            r.vecs[row : row + 1, :] = part[first : first + width].reshape(1, width)
+            row += 1
     vec = lambda index: r.vecs[index : index + 1, :]
     for copy in weights:
         copy.wait()
@@ -622,6 +634,10 @@
     stores[0].start()
     r.mixed_out[...] = dot(r.order[...], r.mixed[...].reshape(every, width), 1, 1).astype(BF16)
     r.normal_out[...] = dot(r.order[...], r.normal[...].reshape(every, width), 1, 1).astype(BF16)
+    normed, _ = norm_parts(r.hidden[...])
+    made = (normed * vec(5) + vec(6)).astype(BF16)
+    r.normal2[...] = made
+    r.normal2_t[...] = dot(r.order[...], made, 1, 1).astype(BF16)
     for pair in range(pairs):
         arrived(1, pair)
     stores[1].start()
@@ -640,7 +656,7 @@
         copy.wait()
 
 
-def run_opening(text_len, patch_count, inputs, cotangent, vecs, wqkv, wout):
+def run_opening(text_len, patch_count, inputs, cotangent, parts, wqkv, wout):
     _, group, slots, width = inputs.shape
     pairs = group // 2
     rows = padded(TEXT + slots)
@@ -651,19 +667,23 @@
         patch_count=(patch_count, smem_spec()),
         inputs=(inputs, hbm),
         cotangent=(cotangent, hbm),
-        vecs=(vecs, whole_spec()),
         wqkv_in=(wqkv, hbm),
         wout_in=(wout, hbm),
     )
+    operands.update((index, (part, whole_spec())) for index, part in enumerate(parts))
+    count = sum(part.shape[0] for part in parts) // width
     cube = shape((pairs, rows, width), BF16)
     tall = shape((width, every), BF16)
     outs = dict(
+        vecs=(shape((count, width), F32), whole_spec()),
         q_out=(cube, whole_spec()),
         k_out=(cube, whole_spec()),
         v_out=(cube, whole_spec()),
         hidden=(shape((every, width), F32), whole_spec()),
         mixed_out=(tall, whole_spec()),
         normal_out=(tall, whole_spec()),
+        normal2=(shape((every, width), BF16), whole_spec()),
+        normal2_t=(tall, whole_spec()),
         seq_out=(cube, hbm),
         cot_out=(cube, hbm),
         order=(shape((width, width), BF16), whole_spec()),
@@ -681,7 +701,7 @@
         load_sem=pltpu.SemaphoreType.DMA((2 * pairs + 2,)),
         store_sem=pltpu.SemaphoreType.DMA((2,)),
     )
-    names = list(operands) + list(outs) + list(scratch)
+    names = [str(name) for name in (*operands, *outs, *scratch)]
     return pl.pallas_call(
         functools.partial(opening_kernel, pairs, slots, names),
         out_shape=[kind for kind, _ in outs.values()],
@@ -700,38 +720,38 @@
     5: [(A, 0, 1)],
     6: [(B, 1, 0)],
     7: [(A, 0, 2), (A, 1, 0)],
-    8: [(B, 2, 0), (B, 2, 1), (A, 1, 1)],
+    8: [(B, 2, 0), (B, 2, 1)],
+    9: [(A, 1, 1)],
     10: [(B, 3, 0), (B, 3, 1)],
-    11: [(A, 1, 2), (A, 2, 0), (B, 3, 2), (B, 4, 0)],
-    12: [(A, 2, 1), (B, 0, 1), (B, 2, 2)],
-    13: [(A, 0, 3), (B, 1, 1), (B, 3, 3), (B, 5, 0)],
-    14: [(B, 2, 3), (A, 2, 2), (A, 3, 0)],
-    15: [(B, 1, 2)],
-    16: [(B, 0, 2), (B, 1, 3), (B, 6, 0), (B, 6, 1), (A, 3, 1), (R, 0, 0)],
-    17: [(B, 7, 0), (B, 7, 1), (H, 0, 0), (B, 0, 3), (R, 0, 1)],
-    18: [(A, 3, 2), (B, 7, 2)],
-    19: [(B, 6, 2)],
-    20: [(B, 4, 1)],
-    21: [(O, 0, 0), (R, 0, 2)],
-    22: [(A, 1, 3), (B, 5, 1), (B, 7, 3), (H, 0, 1), (A, 0, 4), (B, 7, 4), (B, 5, 2), (B, 6, 3), (B, 6, 4), (R, 0, 3)],
-    23: [(R, 0, 4)],
-    24: [(B, 5, 3), (B, 2, 4), (B, 3, 4), (B, 5, 4), (R, 0, 5)],
+    11: [(A, 2, 0), (A, 1, 2)],
+    12: [(B, 2, 2), (B, 3, 2), (B, 4, 0)],
+    13: [(A, 2, 1), (B, 0, 1)],
+    14: [(A, 0, 3), (B, 1, 1), (B, 2, 3), (B, 3, 3), (B, 5, 0), (A, 3, 0)],
+    15: [(A, 2, 2), (B, 1, 2), (B, 6, 0), (B, 6, 1)],
+    16: [(A, 3, 1), (B, 0, 2), (B, 1, 3), (R, 0, 0)],
+    17: [(R, 0, 1)],
+    18: [(B, 0, 3), (B, 7, 0), (B, 7, 1), (H, 0, 0), (R, 0, 2)],
+    19: [(R, 0, 3)],
+    20: [(B, 7, 2)],
+    21: [(A, 3, 2), (O, 0, 0), (B, 6, 2)],
+    23: [(B, 4, 1), (B, 7, 3), (B, 7, 4), (R, 0, 4)],
+    24: [(A, 1, 3), (B, 5, 1), (B, 6, 3), (H, 0, 1), (A, 0, 4), (B, 3, 4), (B, 6, 4), (R, 0, 5)],
     25: [(O, 0, 1), (R, 0, 6)],
-    26: [(B, 4, 2), (H, 0, 2), (B, 1, 4), (R, 0, 7)],
-    27: [(C, 0, 0), (R, 0, 8)],
-    28: [(O, 0, 2), (C, 1, 0), (B, 4, 3), (H, 0, 3), (B, 4, 4), (R, 0, 9)],
-    29: [(C, 2, 0), (R, 1, 0)],
-    30: [(C, 0, 1), (O, 0, 3), (C, 3, 0), (B, 0, 4), (H, 0, 4), (R, 1, 1)],
-    31: [(C, 1, 1), (C, 4, 0), (R, 1, 2)],
-    32: [(C, 0, 2), (C, 2, 1), (C, 5, 0), (O, 0, 4), (R, 1, 3)],
+    26: [(B, 5, 2), (B, 2, 4), (R, 0, 7)],
+    27: [(C, 0, 0), (B, 4, 2), (H, 0, 2), (R, 0, 8)],
+    28: [(O, 0, 2), (C, 1, 0), (B, 5, 3), (B, 5, 4)],
+    29: [(C, 2, 0), (B, 4, 3), (H, 0, 3), (B, 4, 4), (R, 0, 9)],
+    30: [(C, 0, 1), (C, 3, 0), (B, 1, 4), (O, 0, 3), (R, 1, 0)],
+    31: [(C, 1, 1), (C, 4, 0), (B, 0, 4), (H, 0, 4), (R, 1, 1)],
+    32: [(C, 2, 1), (C, 5, 0), (C, 0, 2), (R, 1, 2)],
 }
 TAIL = [
-    (C, 1, 2), (V, 0, 0), (C, 3, 1), (R, 1, 4), (C, 0, 3), (C, 2, 2),
-    (C, 4, 1), (R, 2, 0), (C, 1, 3), (C, 3, 2), (C, 5, 1), (R, 2, 1),
-    (C, 2, 3), (V, 0, 1), (C, 0, 4), (C, 4, 2), (R, 2, 2), (C, 3, 3),
-    (C, 5, 2), (V, 0, 2), (C, 1, 4), (C, 4, 3), (R, 2, 3), (C, 2, 4),
-    (C, 5, 3), (R, 2, 4), (V, 0, 3), (C, 3, 4), (C, 4, 4), (C, 5, 4),
-    (V, 0, 4),
+    (C, 1, 2), (V, 0, 0), (C, 3, 1), (R, 1, 3), (C, 0, 3), (O, 0, 4),
+    (C, 2, 2), (C, 4, 1), (C, 1, 3), (R, 1, 4), (C, 3, 2), (C, 5, 1),
+    (R, 2, 0), (C, 2, 3), (V, 0, 1), (C, 0, 4), (C, 4, 2), (R, 2, 1),
+    (C, 3, 3), (C, 5, 2), (V, 0, 2), (C, 1, 4), (C, 4, 3), (R, 2, 2),
+    (C, 2, 4), (C, 5, 3), (R, 2, 3), (V, 0, 3), (C, 3, 4), (C, 4, 4),
+    (C, 5, 4), (R, 2, 4), (V, 0, 4),
 ]
 
 
@@ -751,7 +771,12 @@
     def load(name, target, index):
         return pltpu.make_async_copy(getattr(r, name), getattr(r, target), r.load_sem.at[index])
 
-    early = [load("hidden_in", "hidden", 0), load("order_in", "order", 1), load("cot_in", "cot", 2)]
+    early = [
+        load("normal2_in", "normal2", 0),
+        load("cot_in", "cot", 1),
+        load("normal2_t_in", "normal2_t", 2),
+        load("hidden_in", "hidden", 9),
+    ]
     late = [
         load("mixed_in", "mixed_t", 3),
         load("normal_in", "normal_t", 4),
@@ -759,6 +784,7 @@
         load("q_in", "q", 6),
         load("k_in", "k", 7),
         load("v_in", "v", 8),
+        load("order_in", "order", 10),
     ]
 
     def block_of(t):
@@ -773,38 +799,20 @@
         )
 
     early[0].start()
-    early[1].start()
     for copy in weight_loads(0, 0):
         copy.start()
-    early[2].start()
-    early[0].wait()
+    for copy in early[1:]:
+        copy.start()
+    r.gnormal[...] = jnp.zeros_like(r.gnormal)
     live = live_rows(lens, pairs, rows, slots)
-    normed, _ = norm_parts(r.hidden[...])
-    made = (normed * vec_in(5) + vec_in(6)).astype(BF16)
-    r.normal2[...] = made
-    early[1].wait()
-    r.normal2_t[...] = dot(r.order[...], made, 1, 1).astype(BF16)
+    for copy in early:
+        copy.wait()
     r.total[...] = r.hidden[...] + vec_in(7)
-    r.gnormal[...] = jnp.zeros_like(r.gnormal)
-    early[2].wait()
     r.gdown[...] = (r.cot[...].reshape(every, width).astype(F32) * live).astype(BF16)
     r.unit_h[...] = jnp.zeros_like(r.unit_h)
     for copy in late:
         copy.start()
-    r.zeros[...] = jnp.zeros_like(r.zeros)
     pl.semaphore_wait(barrier, len(BITS))
-
-    def blanks():
-        return [
-            pltpu.make_async_copy(r.zeros, out.at[0, pair, pl.ds(tail, slots - tail)], r.zero_sem.at[2 * pair + index])
-            for index, out in enumerate((r.block_out, r.input_grad))
-            for pair in range(2 * pairs)
-        ]
-
-    @pl.when(here["x"] == 0)
-    def _():
-        for copy in blanks():
-            copy.start()
 
     arrivals = lambda name, index: [getattr(r, name + str(step)).at[index] for step in range(5)]
 
@@ -875,8 +883,8 @@
     for g in range(groups):
         units[C, g] = Unit(r.c_own.at[g], arrivals("c", g), ORDERS[(g + 1) % 2], sems, 60 + 5 * g, c_finish(g))
     units[O, 0] = Unit(r.o_own, arrivals("o", 0), ORDERS[0], sems, 90, plain(r.out_o))
-    units[H, 0] = Unit(r.unit_h, arrivals("h", 0), ORDERS[1], sems, 95, plain(r.out_h))
-    units[V, 0] = Unit(r.unit_v, arrivals("v", 0), ORDERS[0], sems, 100, plain(r.out_v))
+    units[H, 0] = Unit(r.unit_h, arrivals("h", 0), ORDERS[1], sems, 95, plain(r.out_v.at[pl.ds(1, 1)]))
+    units[V, 0] = Unit(r.unit_v, arrivals("v", 0), ORDERS[0], sems, 100, plain(r.out_v.at[pl.ds(0, 1)]))
 
     def give(source, target, pair, index):
         near = lambda src, dst: pltpu.make_async_copy(src, dst, r.give_sem.at[index])
@@ -1139,12 +1147,6 @@
         act(*item)
     for number in range(2 * pairs):
         give_wait(number)
-
-    @pl.when(here["x"] == 0)
-    def _():
-        for copy in blanks():
-            copy.wait()
-
     for t in range(4):
         a_core(t, 0).wait_send()
         a_core(t, 1).wait_send()
@@ -1157,7 +1159,7 @@
         unit.drain()
 
 
-def run_fused(text_len, patch_count, vecs, hidden, cot, wh, wd, order, wqkv, wout, seq, q, k, v, mixed_t, normal_t, slots):
+def run_fused(text_len, patch_count, vecs, hidden, cot, wh, wd, order, wqkv, wout, seq, q, k, v, mixed_t, normal_t, normal2, normal2_t, slots):
     pairs, rows, width = seq.shape
     every = pairs * rows
     wide = (2,) * 5
@@ -1175,9 +1177,7 @@
         cot=cube,
         result=cube,
         grad_rows=cube,
-        zeros=pltpu.VMEM((slots - (rows - slots), width), BF16),
         give_sem=pltpu.SemaphoreType.DMA((2 * pairs,)),
-        zero_sem=pltpu.SemaphoreType.DMA((4 * pairs,)),
         hidden=flat(F32),
         gdown=flat(BF16),
         seq=cube,
@@ -1213,7 +1213,7 @@
         **arrivals("v", 1, (1, 8, 128), F32),
         send_sem=pltpu.SemaphoreType.DMA((105 + 2 * pairs,)),
         recv_sem=pltpu.SemaphoreType.DMA((105 + 2 * pairs,)),
-        load_sem=pltpu.SemaphoreType.DMA((9,)),
+        load_sem=pltpu.SemaphoreType.DMA((11,)),
         w_sem=pltpu.SemaphoreType.DMA((4,)),
     )
     hbm = pl.BlockSpec(memory_space=pl.ANY)
@@ -1234,6 +1234,8 @@
         v_in=(v, hbm),
         mixed_in=(mixed_t, hbm),
         normal_in=(normal_t, hbm),
+        normal2_in=(normal2, hbm),
+        normal2_t_in=(normal2_t, hbm),
     )
     final = shape((1, 2 * pairs, slots, width), BF16)
     outs = dict(
@@ -1243,8 +1245,7 @@
         out_b=(shape((eight, 8, 4 * width), F32), whole_spec()),
         out_c=(shape((eight, 8, 3 * width), F32), whole_spec()),
         out_o=(shape((eight, 8, width), F32), whole_spec()),
-        out_h=(shape((1, 8, 128), F32), whole_spec()),
-        out_v=(shape((1, 8, 128), F32), whole_spec()),
+        out_v=(shape((2, 8, 128), F32), whole_spec()),
     )
     names = list(operands) + list(outs) + list(scratch)
     return pl.pallas_call(
@@ -1360,9 +1361,8 @@
     row = lambda vector: vector.reshape(1, -1)
     if lax.axis_size("pairs") == 16:
         parts = [norm1_gain, norm1_bias, query_bias, value_bias, out_bias, norm2_gain, norm2_bias, down_bias, hidden_bias]
-        vecs = jnp.concatenate(parts).reshape(-1, width)
-        made = run_opening(text_len, patch_count, inputs, cotangent, vecs, qkv_weight, out_weight)
-        q, k, v, hidden, mixed, normal, seq, cot, order = made
+        made = run_opening(text_len, patch_count, inputs, cotangent, parts, qkv_weight, out_weight)
+        vecs, q, k, v, hidden, mixed, normal, normal2, normal2_t, seq, cot, order = made
         made = run_fused(
             text_len,
             patch_count,
@@ -1380,13 +1380,19 @@
             v,
             mixed,
             normal,
+            normal2,
+            normal2_t,
             slots,
         )
-        block_out, input_grad, wd_out, wh_out, qkv_out, wo_out, hb_out, vec_out = made
+        block_out, input_grad, wd_out, wh_out, qkv_out, wo_out, vectors = made
+        slot = lax.broadcasted_iota(jnp.int32, (1, 1, slots, 1), 2)
+        blank = is_text & (slot >= TEXT)
+        block_out = jnp.where(blank, jnp.zeros((), BF16), block_out)
+        input_grad = jnp.where(blank, jnp.zeros((), BF16), input_grad)
         flat = lambda array: array.reshape(-1, array.shape[-1])
         wd_out, wh_out, qkv_out, wo_out = flat(wd_out), flat(wh_out), flat(qkv_out), flat(wo_out)
-        vec_out = vec_out[0, :, : width // 32].T
-        hb_out = hb_out[0, 0, : hidden_bias.shape[0] // 32]
+        vec_out = [vectors[0, index, : width // 32] for index in range(8)]
+        hb_out = vectors[1, 0, : hidden_bias.shape[0] // 32]
     else:
         seq = gathered(inputs)
         cot = gathered(cotangent).reshape(half * rows, width)
@@ -1441,22 +1447,23 @@
         vec_out = qkvo_out[:, 4 * width :]
         qkv_out, wo_out = qkvo_out[:, : 3 * width], qkvo_out[:, 3 * width : 4 * width]
         hb_out = vec_out[:, 8 : 8 + hidden_bias.shape[0] // width].reshape(-1)
+        vec_out = [vec_out[:, index] for index in range(8)]
     return (
         block_out,
         input_grad,
-        vec_out[:, 0],
-        vec_out[:, 1],
+        vec_out[0],
+        vec_out[1],
         qkv_out,
-        vec_out[:, 2],
-        vec_out[:, 3],
+        vec_out[2],
+        vec_out[3],
         wo_out,
-        vec_out[:, 7],
-        vec_out[:, 4],
-        vec_out[:, 5],
+        vec_out[7],
+        vec_out[4],
+        vec_out[5],
         wh_out,
         hb_out,
         wd_out,
-        vec_out[:, 6],
+        vec_out[6],
     )
 
 

time: 161 us -> 148 us (0.919)
  local copies, waits for them, and re-layouts: 15.9 us -> 3.82 us
  Pallas kernels: 144 us -> 139 us
  other arithmetic: 0.01 us -> 3.78 us
    unnamed x24 -> x14, local copies, waits for them, and re-layouts: 12.1 us -> 2.77 us
    pallas_call x1, Pallas kernels: 104 us -> 97.9 us  [run_fused(): pl.pallas_call(functools.partial(fused_kernel, pairs, slots, names), out_...]
    select_n x0 -> x1, other arithmetic: none -> 3.78 us  [on_device(): input_grad = jnp.where(blank, jnp.zeros((), BF16), input_grad)]
where the time goes in v5:
time: 148 us; the launch traced here: 147 us
  Pallas kernels  139 us (94%)
  local copies, waits for them, and re-layouts  3.82 us (3%)
  other arithmetic  3.78 us (3%)
    pallas_call x1, Pallas kernels, run_fused(): pl.pallas_call(functools.partial(fused_kernel, pairs, slots, names), out_...  97.9 us
    pallas_call x1, Pallas kernels, run_opening(): pl.pallas_call(functools.partial(opening_kernel, pairs, slots, names), ou...  41.1 us
    select_n x1, other arithmetic, on_device(): input_grad = jnp.where(blank, jnp.zeros((), BF16), input_grad)  3.78 us

profile of v5, /device:TPU:0, one launch (start us, length us, event | category | flops | bytes accessed | tf_op | source)
XLA Modules:
  0.0 147.3 jit_solution(10737457510625959003)
XLA Ops:
  0.6 41.1 %opening.1 = (f32[12,768]{1,0:T(8,128)}, bf16[2,288,768]{2,1,0:T(8,128)(2,1)}, bf16[2,288,768]{2,1,0:T(8,128)(2,1)}, bf16[2,288,768]{2,1,0:T(8,128)(2,1)}, f32[5...) custom-call(s32[4]{0:T(128)} %refs_0_.3, ...), custom_call_target="tpu_custom_call" | custom-call | tf_op jit(solution)/shard_map/opening/pallas_call | solution.py:705
  41.7 97.9 %fused.1 = (bf16[1,4,240,768]{3,2,1,0:T(8,128)(2,1)}, bf16[1,4,240,768]{3,2,1,0:T(8,128)(2,1)}, f32[12,8,768]{2,1,0:T(8,128)}, f32[3,8,3072]{2,1,0:T(8,128)}, f3...) custom-call(s32[4]{0:T(128)} %refs_0_.3, s32[4]{0:T(128)} %refs_1_.3, ...), custom_call_target="tpu_custom_call" | custom-call | tf_op jit(solution)/shard_map/fused/pallas_call | solution.py:1251
  139.7 0.0 copy-start.4
  139.7 0.0 copy-start.2
  139.7 0.0 copy-start.3
  139.7 0.0 copy-start.1
  139.7 0.0 copy-start
  139.7 3.8 %broadcast_select_fusion = (bf16[1,4,240,768]{3,2,1,0:T(8,128)(2,1)}, bf16[1,4,240,768]{3,2,1,0:T(8,128)(2,1)}) fusion(bf16[1,4,240,768]{3,2,1,0:T(8,128)(2,1)} %get-tuple-element.47, pred[240]{0:T(512)(128)(4,1)S(1)} %compare_and_fusion, bf16[1,4,240,768]{3,2,1,0:T(8,128)(2,1)} %get-tuple-element.46), kind=kLoop, calls=%fused_computation | loop fusion | flops 1474560 | bytes 5898480 | tf_op jit(solution)/shard_map/jit(_where)/select_n | solution.py:1391
  143.5 0.0 copy-done.4
  143.5 0.5 slice_bitcast_fusion
  144.0 0.5 slice_bitcast_fusion.1
  144.6 0.0 copy-done.2
  144.6 0.7 copy.36
  145.2 0.0 copy-done.3
  145.2 0.6 copy.37
  145.9 0.0 copy-done.1
  145.9 0.7 copy.38
  146.6 0.0 copy-done
  146.6 0.7 copy.39
  (1 shorter events, 0.0 us)
Async XLA Ops:
  139.7 3.8 %copy-start.4 = (f32[2,8,128]{2,1,0:T(8,128)S(1)}, f32[2,8,128]{2,1,0:T(8,128)}, u32[]{:S(2)}) copy-start(f32[2,8,128]{2,1,0:T(8,128)} %get-tuple-element.48) | copy-start | bytes 24580
  139.7 4.9 %copy-start.2 = (f32[3,8,2304]{2,1,0:T(8,128)S(1)}, f32[3,8,2304]{2,1,0:T(8,128)}, u32[]{:S(2)}) copy-start(f32[3,8,2304]{2,1,0:T(8,128)} %get-tuple-element.49) | copy-start | bytes 663556
  139.7 5.6 %copy-start.3 = (f32[3,8,768]{2,1,0:T(8,128)S(1)}, f32[3,8,768]{2,1,0:T(8,128)}, u32[]{:S(2)}) copy-start(f32[3,8,768]{2,1,0:T(8,128)} %get-tuple-element.50) | copy-start | bytes 221188
  139.7 6.2 %copy-start.1 = (f32[3,8,3072]{2,1,0:T(8,128)S(1)}, f32[3,8,3072]{2,1,0:T(8,128)}, u32[]{:S(2)}) copy-start(f32[3,8,3072]{2,1,0:T(8,128)} %get-tuple-element.51) | copy-start | bytes 884740
  139.7 6.9 %copy-start = (f32[12,8,768]{2,1,0:T(8,128)S(1)}, f32[12,8,768]{2,1,0:T(8,128)}, u32[]{:S(2)}) copy-start(f32[12,8,768]{2,1,0:T(8,128)} %get-tuple-element.52) | copy-start | bytes 884740

commit v6 on v5

--- a/solution.py
+++ b/solution.py
@@ -526,6 +526,21 @@
             self.copy(step).wait_send()
 
 
+STORED = [
+    "q_out",
+    "k_out",
+    "v_out",
+    "hidden",
+    "seq",
+    "order",
+    "mixed_out",
+    "normal_out",
+    "normal2",
+    "normal2_t",
+    "cot",
+]
+
+
 def counts(here, pairs, text_len, patch_count):
     base = here["x"] * pairs
     return [text_len[base + pair] for pair in range(pairs)] + [patch_count[base + pair] for pair in range(pairs)]
@@ -628,19 +643,22 @@
         made = r.seq[pair].astype(F32) + dot(r.mixed[pair], r.wout[...]) + vec(4)
         r.hidden[pair * rows : (pair + 1) * rows, :] = made
     stores = [
-        pltpu.make_async_copy(r.seq, r.seq_out, r.store_sem.at[0]),
-        pltpu.make_async_copy(r.cot, r.cot_out, r.store_sem.at[1]),
+        pltpu.make_async_copy(getattr(r, name), getattr(r, str(20 + index)), r.store_sem.at[index])
+        for index, name in enumerate(STORED)
     ]
-    stores[0].start()
+    for copy in stores[:6]:
+        copy.start()
     r.mixed_out[...] = dot(r.order[...], r.mixed[...].reshape(every, width), 1, 1).astype(BF16)
     r.normal_out[...] = dot(r.order[...], r.normal[...].reshape(every, width), 1, 1).astype(BF16)
     normed, _ = norm_parts(r.hidden[...])
     made = (normed * vec(5) + vec(6)).astype(BF16)
     r.normal2[...] = made
     r.normal2_t[...] = dot(r.order[...], made, 1, 1).astype(BF16)
+    for copy in stores[6:10]:
+        copy.start()
     for pair in range(pairs):
         arrived(1, pair)
-    stores[1].start()
+    stores[10].start()
 
     @pl.when(here["x"] == 1)
     def _():
@@ -676,30 +694,33 @@
     tall = shape((width, every), BF16)
     outs = dict(
         vecs=(shape((count, width), F32), whole_spec()),
-        q_out=(cube, whole_spec()),
-        k_out=(cube, whole_spec()),
-        v_out=(cube, whole_spec()),
-        hidden=(shape((every, width), F32), whole_spec()),
-        mixed_out=(tall, whole_spec()),
-        normal_out=(tall, whole_spec()),
-        normal2=(shape((every, width), BF16), whole_spec()),
-        normal2_t=(tall, whole_spec()),
-        seq_out=(cube, hbm),
-        cot_out=(cube, hbm),
-        order=(shape((width, width), BF16), whole_spec()),
     )
+    long = shape((every, width), F32)
+    flat = shape((every, width), BF16)
+    square = shape((width, width), BF16)
+    kinds = [cube, cube, cube, long, cube, square, tall, tall, flat, tall, cube]
+    outs.update((20 + index, (kind, hbm)) for index, kind in enumerate(kinds))
     held = pltpu.VMEM((pairs, rows, width), BF16)
     scratch = dict(
         seq=held,
         cot=held,
         mixed=held,
         normal=held,
+        q_out=held,
+        k_out=held,
+        v_out=held,
+        hidden=pltpu.VMEM(long.shape, F32),
+        order=pltpu.VMEM(square.shape, BF16),
+        mixed_out=pltpu.VMEM(tall.shape, BF16),
+        normal_out=pltpu.VMEM(tall.shape, BF16),
+        normal2=pltpu.VMEM(flat.shape, BF16),
+        normal2_t=pltpu.VMEM(tall.shape, BF16),
         wqkv=pltpu.VMEM(wqkv.shape, BF16),
         wout=pltpu.VMEM(wout.shape, BF16),
         send_sem=pltpu.SemaphoreType.DMA((2 * pairs,)),
         recv_sem=pltpu.SemaphoreType.DMA((2 * pairs,)),
         load_sem=pltpu.SemaphoreType.DMA((2 * pairs + 2,)),
-        store_sem=pltpu.SemaphoreType.DMA((2,)),
+        store_sem=pltpu.SemaphoreType.DMA((len(kinds),)),
     )
     names = [str(name) for name in (*operands, *outs, *scratch)]
     return pl.pallas_call(
@@ -723,35 +744,35 @@
     8: [(B, 2, 0), (B, 2, 1)],
     9: [(A, 1, 1)],
     10: [(B, 3, 0), (B, 3, 1)],
-    11: [(A, 2, 0), (A, 1, 2)],
-    12: [(B, 2, 2), (B, 3, 2), (B, 4, 0)],
-    13: [(A, 2, 1), (B, 0, 1)],
-    14: [(A, 0, 3), (B, 1, 1), (B, 2, 3), (B, 3, 3), (B, 5, 0), (A, 3, 0)],
-    15: [(A, 2, 2), (B, 1, 2), (B, 6, 0), (B, 6, 1)],
+    11: [(A, 1, 2), (A, 2, 0), (B, 4, 0), (B, 3, 2)],
+    12: [(A, 2, 1), (B, 0, 1), (B, 2, 2)],
+    13: [(A, 0, 3)],
+    14: [(B, 1, 1), (B, 2, 3), (B, 3, 3), (B, 5, 0)],
+    15: [(A, 2, 2), (A, 3, 0), (B, 1, 2), (B, 6, 0), (B, 6, 1)],
     16: [(A, 3, 1), (B, 0, 2), (B, 1, 3), (R, 0, 0)],
     17: [(R, 0, 1)],
     18: [(B, 0, 3), (B, 7, 0), (B, 7, 1), (H, 0, 0), (R, 0, 2)],
     19: [(R, 0, 3)],
-    20: [(B, 7, 2)],
-    21: [(A, 3, 2), (O, 0, 0), (B, 6, 2)],
-    23: [(B, 4, 1), (B, 7, 3), (B, 7, 4), (R, 0, 4)],
-    24: [(A, 1, 3), (B, 5, 1), (B, 6, 3), (H, 0, 1), (A, 0, 4), (B, 3, 4), (B, 6, 4), (R, 0, 5)],
-    25: [(O, 0, 1), (R, 0, 6)],
-    26: [(B, 5, 2), (B, 2, 4), (R, 0, 7)],
-    27: [(C, 0, 0), (B, 4, 2), (H, 0, 2), (R, 0, 8)],
-    28: [(O, 0, 2), (C, 1, 0), (B, 5, 3), (B, 5, 4)],
-    29: [(C, 2, 0), (B, 4, 3), (H, 0, 3), (B, 4, 4), (R, 0, 9)],
-    30: [(C, 0, 1), (C, 3, 0), (B, 1, 4), (O, 0, 3), (R, 1, 0)],
-    31: [(C, 1, 1), (C, 4, 0), (B, 0, 4), (H, 0, 4), (R, 1, 1)],
-    32: [(C, 2, 1), (C, 5, 0), (C, 0, 2), (R, 1, 2)],
+    20: [(A, 3, 2), (O, 0, 0), (B, 7, 2)],
+    21: [(B, 6, 2)],
+    22: [(C, 0, 0), (B, 4, 1), (R, 0, 4)],
+    23: [(A, 1, 3), (A, 0, 4), (R, 0, 5)],
+    24: [(C, 1, 0), (B, 5, 1), (B, 6, 3), (B, 7, 3), (H, 0, 1), (B, 6, 4), (B, 7, 4), (R, 0, 6)],
+    25: [(O, 0, 1), (R, 0, 7)],
+    26: [(C, 0, 1), (C, 2, 0), (B, 5, 2), (B, 2, 4), (B, 3, 4), (R, 0, 8)],
+    27: [(O, 0, 2), (C, 1, 1), (B, 4, 2), (B, 5, 3), (H, 0, 2), (B, 5, 4)],
+    28: [(C, 0, 2), (R, 0, 9)],
+    29: [(O, 0, 3), (C, 2, 1), (B, 4, 3), (H, 0, 3), (B, 1, 4), (B, 4, 4), (C, 1, 2), (R, 1, 0)],
+    30: [(C, 0, 3), (C, 3, 0), (R, 1, 1)],
+    31: [(C, 1, 3), (C, 2, 2), (C, 4, 0), (B, 0, 4), (O, 0, 4), (H, 0, 4), (R, 1, 2)],
+    32: [(C, 5, 0), (C, 0, 4), (R, 1, 3)],
 }
 TAIL = [
-    (C, 1, 2), (V, 0, 0), (C, 3, 1), (R, 1, 3), (C, 0, 3), (O, 0, 4),
-    (C, 2, 2), (C, 4, 1), (C, 1, 3), (R, 1, 4), (C, 3, 2), (C, 5, 1),
-    (R, 2, 0), (C, 2, 3), (V, 0, 1), (C, 0, 4), (C, 4, 2), (R, 2, 1),
-    (C, 3, 3), (C, 5, 2), (V, 0, 2), (C, 1, 4), (C, 4, 3), (R, 2, 2),
-    (C, 2, 4), (C, 5, 3), (R, 2, 3), (V, 0, 3), (C, 3, 4), (C, 4, 4),
-    (C, 5, 4), (R, 2, 4), (V, 0, 4),
+    (C, 2, 3), (C, 3, 1), (R, 1, 4), (V, 0, 0), (C, 4, 1), (R, 2, 0),
+    (C, 1, 4), (C, 3, 2), (C, 5, 1), (V, 0, 1), (R, 2, 1), (C, 4, 2),
+    (V, 0, 2), (C, 2, 4), (C, 3, 3), (R, 2, 2), (C, 5, 2), (C, 4, 3),
+    (R, 2, 3), (V, 0, 3), (C, 5, 3), (R, 2, 4), (C, 3, 4), (C, 4, 4),
+    (V, 0, 4), (C, 5, 4),
 ]
 
 
@@ -881,7 +902,7 @@
         units[B, u].peers = {"y": units[B, u ^ 1], "z0": units[B, u ^ 2], "z1": units[B, u ^ 4]}
     groups = width // 128
     for g in range(groups):
-        units[C, g] = Unit(r.c_own.at[g], arrivals("c", g), ORDERS[(g + 1) % 2], sems, 60 + 5 * g, c_finish(g))
+        units[C, g] = Unit(r.c_own.at[g], arrivals("c", g), ORDERS[(1, 0, 1, 1, 0, 1)[g]], sems, 60 + 5 * g, c_finish(g))
     units[O, 0] = Unit(r.o_own, arrivals("o", 0), ORDERS[0], sems, 90, plain(r.out_o))
     units[H, 0] = Unit(r.unit_h, arrivals("h", 0), ORDERS[1], sems, 95, plain(r.out_v.at[pl.ds(1, 1)]))
     units[V, 0] = Unit(r.unit_v, arrivals("v", 0), ORDERS[0], sems, 100, plain(r.out_v.at[pl.ds(0, 1)]))
@@ -1073,11 +1094,13 @@
         give_start(pairs + pair)
 
     def head_step(it, carry):
-        pair, g = it // groups, it % groups
+        late = it // groups
+        pair = (1 - late) * (it % 2) + it // 9
+        g = (1 - late) * (it // 2) + late * (3 + it % 3)
         base = g * 128
         off = pl.multiple_of(base, 128)
 
-        @pl.when(it == groups)
+        @pl.when(it == 9)
         def _():
             finish_pair(0, *project_back(0))
 
@@ -1112,7 +1135,7 @@
         r.gproj[pair, :, pl.ds(pl.multiple_of(base + width, 128), 128)] = gk.astype(BF16)
         r.gproj[pair, :, pl.ds(pl.multiple_of(base + 2 * width, 128), 128)] = gv.astype(BF16)
 
-        @pl.when(it >= (pairs - 1) * groups)
+        @pl.when(pair == pairs - 1)
         def _():
             pieces = [
                 r.gproj[:, :, pl.ds(pl.multiple_of(base + part * width, 128), 128)].reshape(every, 128)
@@ -1261,6 +1284,27 @@
     )(*[value for value, _ in operands.values()])
 
 
+def closing_kernel(*refs):
+    count = len(refs) // 2
+    for index in range(count):
+        value = refs[index][...]
+        if index < 2:
+            slot = lax.broadcasted_iota(jnp.int32, value.shape, 2)
+            last = TEXT + lax.axis_index("mod") * value.shape[2]
+            value = jnp.where(slot < last, value, jnp.zeros_like(value))
+        refs[count + index][...] = value
+
+
+def run_closing(*arrays):
+    return pl.pallas_call(
+        closing_kernel,
+        out_shape=[shape(array.shape, array.dtype) for array in arrays],
+        in_specs=[whole_spec()] * len(arrays),
+        out_specs=[whole_spec()] * len(arrays),
+        name="closing",
+    )(*arrays)
+
+
 def pair_bits():
     return lax.axis_size("pairs").bit_length() - 1
 
@@ -1362,7 +1406,7 @@
     if lax.axis_size("pairs") == 16:
         parts = [norm1_gain, norm1_bias, query_bias, value_bias, out_bias, norm2_gain, norm2_bias, down_bias, hidden_bias]
         made = run_opening(text_len, patch_count, inputs, cotangent, parts, qkv_weight, out_weight)
-        vecs, q, k, v, hidden, mixed, normal, normal2, normal2_t, seq, cot, order = made
+        vecs, q, k, v, hidden, seq, order, mixed, normal, normal2, normal2_t, cot = made
         made = run_fused(
             text_len,
             patch_count,
@@ -1385,12 +1429,10 @@
             slots,
         )
         block_out, input_grad, wd_out, wh_out, qkv_out, wo_out, vectors = made
-        slot = lax.broadcasted_iota(jnp.int32, (1, 1, slots, 1), 2)
-        blank = is_text & (slot >= TEXT)
-        block_out = jnp.where(blank, jnp.zeros((), BF16), block_out)
-        input_grad = jnp.where(blank, jnp.zeros((), BF16), input_grad)
         flat = lambda array: array.reshape(-1, array.shape[-1])
         wd_out, wh_out, qkv_out, wo_out = flat(wd_out), flat(wh_out), flat(qkv_out), flat(wo_out)
+        made = run_closing(block_out, input_grad, wd_out, wh_out, qkv_out, wo_out)
+        block_out, input_grad, wd_out, wh_out, qkv_out, wo_out = made
         vec_out = [vectors[0, index, : width // 32] for index in range(8)]
         hb_out = vectors[1, 0, : hidden_bias.shape[0] // 32]
     else:

time: 148 us -> 140 us (0.946)
  other arithmetic: 3.78 us -> 0 us
  local copies, waits for them, and re-layouts: 3.82 us -> 1.06 us
    pallas_call x0 -> x1, Pallas kernels: none -> 4 us  [run_closing(): pl.pallas_call(closing_kernel, out_shape=[shape(array.shape, array.dtype)...]
    select_n x1 -> x0, other arithmetic: 3.78 us -> none  [on_device(): input_grad = jnp.where(blank, jnp.zeros((), BF16), input_grad)]
    pallas_call x1, Pallas kernels: 41.1 us -> 38.1 us  [run_opening(): pl.pallas_call(functools.partial(opening_kernel, pairs, slots, names), ou...]
    unnamed x14 -> x2, local copies, waits for them, and re-layouts: 2.77 us -> 0.01 us
    pallas_call x1, Pallas kernels: 97.9 us -> 96 us  [run_fused(): pl.pallas_call(functools.partial(fused_kernel, pairs, slots, names), out_...]
where the time goes in v6:
time: 140 us
  Pallas kernels  138 us (99%)
    pallas_call x1, Pallas kernels, run_fused(): pl.pallas_call(functools.partial(fused_kernel, pairs, slots, names), out_...  96 us
    pallas_call x1, Pallas kernels, run_opening(): pl.pallas_call(functools.partial(opening_kernel, pairs, slots, names), ou...  38.1 us
    pallas_call x1, Pallas kernels, run_closing(): pl.pallas_call(closing_kernel, out_shape=[shape(array.shape, array.dtype)...  4 us

profile of v6, /device:TPU:0, one launch (start us, length us, event | category | flops | bytes accessed | tf_op | source)
XLA Modules:
  0.0 139.8 jit_solution(5243412648118036523)
XLA Ops:
  0.6 38.1 %opening.1 = (f32[12,768]{1,0:T(8,128)}, bf16[2,288,768]{2,1,0:T(8,128)(2,1)}, bf16[2,288,768]{2,1,0:T(8,128)(2,1)}, bf16[2,288,768]{2,1,0:T(8,128)(2,1)}, f32[5...) custom-call(s32[4]{0:T(128)} %refs_0_.3, ...), custom_call_target="tpu_custom_call" | custom-call | tf_op jit(solution)/shard_map/opening/pallas_call | solution.py:726
  38.8 96.0 %fused.1 = (bf16[1,4,240,768]{3,2,1,0:T(8,128)(2,1)}, bf16[1,4,240,768]{3,2,1,0:T(8,128)(2,1)}, f32[12,8,768]{2,1,0:T(8,128)}, f32[3,8,3072]{2,1,0:T(8,128)}, f3...) custom-call(s32[4]{0:T(128)} %refs_0_.3, s32[4]{0:T(128)} %refs_1_.3, ...), custom_call_target="tpu_custom_call" | custom-call | tf_op jit(solution)/shard_map/fused/pallas_call | solution.py:1274
  134.8 0.0 copy-start
  134.8 4.0 %closing.1 = (bf16[1,4,240,768]{3,2,1,0:T(8,128)(2,1)}, bf16[1,4,240,768]{3,2,1,0:T(8,128)(2,1)}, f32[96,768]{1,0:T(8,128)}, f32[24,3072]{1,0:T(8,128)}, f32[24,2304]{1,0:T(8,128)}, /*index=5*/f32[24,768]{1,0:T(8,128)}) custom-call(bf16[1,4,240,768]{3,2,1,0:T(8,128)(2,1)} %get-tuple-element.52.refs_0_, bf16[1,4,240,768]{3,2,1,0:T(8,128)(2,1)} %get-tuple-element.53.refs_1_, ...), custom_call_target="tpu_custom_call" | custom-call | tf_op jit(solution)/shard_map/closing/pallas_call | solution.py:1299
  138.8 0.0 copy-done
  138.8 0.5 slice_bitcast_fusion.1
  139.3 0.5 slice_bitcast_fusion
Async XLA Ops:
  134.8 4.0 %copy-start = (f32[2,8,128]{2,1,0:T(8,128)S(1)}, f32[2,8,128]{2,1,0:T(8,128)}, u32[]{:S(2)}) copy-start(f32[2,8,128]{2,1,0:T(8,128)} %get-tuple-element.60) | copy-start | bytes 24580

commit v7 on v6

--- a/solution.py
+++ b/solution.py
@@ -737,42 +737,39 @@
 A, B, C, O, H, V, R = range(7)
 PLAN = {
     3: [(A, 0, 0)],
-    4: [(B, 0, 0)],
-    5: [(A, 0, 1)],
-    6: [(B, 1, 0)],
+    4: [(A, 0, 1), (B, 0, 0)],
+    5: [(B, 1, 0)],
     7: [(A, 0, 2), (A, 1, 0)],
-    8: [(B, 2, 0), (B, 2, 1)],
-    9: [(A, 1, 1)],
-    10: [(B, 3, 0), (B, 3, 1)],
-    11: [(A, 1, 2), (A, 2, 0), (B, 4, 0), (B, 3, 2)],
-    12: [(A, 2, 1), (B, 0, 1), (B, 2, 2)],
-    13: [(A, 0, 3)],
-    14: [(B, 1, 1), (B, 2, 3), (B, 3, 3), (B, 5, 0)],
-    15: [(A, 2, 2), (A, 3, 0), (B, 1, 2), (B, 6, 0), (B, 6, 1)],
-    16: [(A, 3, 1), (B, 0, 2), (B, 1, 3), (R, 0, 0)],
-    17: [(R, 0, 1)],
-    18: [(B, 0, 3), (B, 7, 0), (B, 7, 1), (H, 0, 0), (R, 0, 2)],
-    19: [(R, 0, 3)],
-    20: [(A, 3, 2), (O, 0, 0), (B, 7, 2)],
-    21: [(B, 6, 2)],
+    8: [(A, 1, 1), (B, 2, 0), (B, 2, 1)],
+    9: [(B, 3, 0), (B, 3, 1)],
+    11: [(A, 2, 0)],
+    12: [(A, 1, 2), (A, 2, 1), (B, 0, 1), (B, 2, 2), (B, 3, 2), (B, 4, 0), (B, 5, 0)],
+    14: [(B, 1, 1)],
+    15: [(A, 0, 3), (A, 2, 2), (A, 3, 0), (B, 2, 3)],
+    16: [(A, 3, 1), (B, 0, 2), (B, 1, 2), (B, 3, 3), (B, 6, 0), (B, 6, 1), (B, 7, 0), (B, 7, 1), (H, 0, 0), (R, 0, 0)],
+    17: [(B, 0, 3), (R, 0, 1)],
+    18: [(B, 1, 3), (R, 0, 2)],
+    19: [(B, 7, 2), (R, 0, 3)],
+    20: [(A, 3, 2), (B, 6, 2)],
+    21: [(O, 0, 0), (B, 7, 3), (B, 7, 4)],
     22: [(C, 0, 0), (B, 4, 1), (R, 0, 4)],
-    23: [(A, 1, 3), (A, 0, 4), (R, 0, 5)],
-    24: [(C, 1, 0), (B, 5, 1), (B, 6, 3), (B, 7, 3), (H, 0, 1), (B, 6, 4), (B, 7, 4), (R, 0, 6)],
-    25: [(O, 0, 1), (R, 0, 7)],
-    26: [(C, 0, 1), (C, 2, 0), (B, 5, 2), (B, 2, 4), (B, 3, 4), (R, 0, 8)],
-    27: [(O, 0, 2), (C, 1, 1), (B, 4, 2), (B, 5, 3), (H, 0, 2), (B, 5, 4)],
-    28: [(C, 0, 2), (R, 0, 9)],
-    29: [(O, 0, 3), (C, 2, 1), (B, 4, 3), (H, 0, 3), (B, 1, 4), (B, 4, 4), (C, 1, 2), (R, 1, 0)],
-    30: [(C, 0, 3), (C, 3, 0), (R, 1, 1)],
-    31: [(C, 1, 3), (C, 2, 2), (C, 4, 0), (B, 0, 4), (O, 0, 4), (H, 0, 4), (R, 1, 2)],
-    32: [(C, 5, 0), (C, 0, 4), (R, 1, 3)],
+    23: [(B, 3, 4), (B, 5, 1), (R, 0, 5)],
+    24: [(A, 1, 3), (C, 1, 0), (B, 6, 3), (H, 0, 1), (A, 0, 4), (B, 6, 4), (R, 0, 6)],
+    25: [(R, 0, 7)],
+    26: [(C, 0, 1), (O, 0, 1), (C, 2, 0), (B, 2, 4), (R, 0, 8)],
+    27: [(B, 4, 2), (B, 5, 2), (R, 0, 9)],
+    28: [(O, 0, 2), (C, 1, 1), (H, 0, 2)],
+    29: [(C, 0, 2), (B, 4, 3), (B, 5, 3), (B, 4, 4), (B, 5, 4), (R, 1, 0)],
+    30: [(C, 1, 2), (C, 3, 0), (C, 2, 1), (O, 0, 3), (C, 4, 0), (H, 0, 3), (B, 0, 4), (R, 1, 1)],
+    31: [(C, 0, 3), (B, 1, 4), (R, 1, 2)],
+    32: [(C, 1, 3), (C, 5, 0), (O, 0, 4), (H, 0, 4), (R, 1, 3)],
 }
 TAIL = [
-    (C, 2, 3), (C, 3, 1), (R, 1, 4), (V, 0, 0), (C, 4, 1), (R, 2, 0),
-    (C, 1, 4), (C, 3, 2), (C, 5, 1), (V, 0, 1), (R, 2, 1), (C, 4, 2),
-    (V, 0, 2), (C, 2, 4), (C, 3, 3), (R, 2, 2), (C, 5, 2), (C, 4, 3),
-    (R, 2, 3), (V, 0, 3), (C, 5, 3), (R, 2, 4), (C, 3, 4), (C, 4, 4),
-    (V, 0, 4), (C, 5, 4),
+    (C, 3, 1), (V, 0, 0), (R, 1, 4), (C, 2, 2), (C, 0, 4), (C, 5, 1),
+    (R, 2, 0), (C, 4, 1), (R, 2, 1), (C, 1, 4), (C, 3, 2), (C, 2, 3),
+    (V, 0, 1), (C, 5, 2), (V, 0, 2), (R, 2, 2), (C, 4, 2), (C, 3, 3),
+    (C, 5, 3), (R, 2, 3), (V, 0, 3), (C, 2, 4), (C, 4, 3), (R, 2, 4),
+    (C, 3, 4), (C, 5, 4), (V, 0, 4), (C, 4, 4),
 ]
 
 
@@ -826,9 +823,9 @@
         copy.start()
     r.gnormal[...] = jnp.zeros_like(r.gnormal)
     live = live_rows(lens, pairs, rows, slots)
-    for copy in early:
+    r.total[...] = jnp.zeros_like(r.total)
+    for copy in early[:3]:
         copy.wait()
-    r.total[...] = r.hidden[...] + vec_in(7)
     r.gdown[...] = (r.cot[...].reshape(every, width).astype(F32) * live).astype(BF16)
     r.unit_h[...] = jnp.zeros_like(r.unit_h)
     for copy in late:
@@ -902,7 +899,7 @@
         units[B, u].peers = {"y": units[B, u ^ 1], "z0": units[B, u ^ 2], "z1": units[B, u ^ 4]}
     groups = width // 128
     for g in range(groups):
-        units[C, g] = Unit(r.c_own.at[g], arrivals("c", g), ORDERS[(1, 0, 1, 1, 0, 1)[g]], sems, 60 + 5 * g, c_finish(g))
+        units[C, g] = Unit(r.c_own.at[g], arrivals("c", g), ORDERS[(1, 0, 0, 1, 1, 0)[g]], sems, 60 + 5 * g, c_finish(g))
     units[O, 0] = Unit(r.o_own, arrivals("o", 0), ORDERS[0], sems, 90, plain(r.out_o))
     units[H, 0] = Unit(r.unit_h, arrivals("h", 0), ORDERS[1], sems, 95, plain(r.out_v.at[pl.ds(1, 1)]))
     units[V, 0] = Unit(r.unit_v, arrivals("v", 0), ORDERS[0], sems, 100, plain(r.out_v.at[pl.ds(0, 1)]))
@@ -996,7 +993,7 @@
             before = dot(r.normal2[...], wh) + r.vecs[pl.ds(8 + block_of(t), 1), pl.ds(start, size)]
             active, slope = gelu_parts(before)
             active = active.astype(BF16)
-            r.total[...] += dot(active, wd)
+            r.gproj[:, :, pl.ds(start, size)] = active.reshape(pairs, rows, size)
             fresh = dot(active, r.gdown[...], 0, 0)
             quarter = size // 4
             for core in range(2):
@@ -1007,7 +1004,8 @@
             a_core(t, y).start()
             run_tasks([4 * k + 2 * sub + 1 for k in range(4)], 4 * t + 2 * sub + 1)
             gbefore = (dot(r.gdown[...], wd, 1, 1) * slope).astype(BF16)
-            r.gnormal[...] += dot(gbefore, wh, 1, 1)
+            right = pl.multiple_of(width + start, 128)
+            r.gproj[:, :, pl.ds(right, size)] = gbefore.reshape(pairs, rows, size)
             fresh = dot(r.normal2_t[...], gbefore)
             fresh = fresh.reshape((2,) * 5 + (width // 256, 8, size)).astype(BF16)
             unit = 2 * t + sub
@@ -1021,6 +1019,8 @@
                     r.unit_h[
                         flip(core, here["core"]), y, z0, flip(mod, here["x"]), z1, 0, 0:1, 0:quarter
                     ] = sums[:, first : first + quarter]
+        r.total[...] += dot(r.gproj[:, :, 0:width].reshape(every, width), r.wbuf[2 + slot])
+        r.gnormal[...] += dot(r.gproj[:, :, width : 2 * width].reshape(every, width), r.wbuf[slot], 1, 1)
         return carry
 
     lax.fori_loop(0, 4, feed_step, 0)
@@ -1036,7 +1036,8 @@
     for copy in wqkv_loads:
         copy.start()
     units[H, 0].start()
-    r.result[...] = (r.total[...] * live).astype(BF16).reshape(pairs, rows, width)
+    early[3].wait()
+    r.result[...] = ((r.hidden[...] + r.total[...] + vec_in(7)) * live).astype(BF16).reshape(pairs, rows, width)
 
     for pair in range(pairs):
         give_start(pair)

time: 140 us -> 144 us (1.029)
  Pallas kernels: 138 us -> 142 us
    pallas_call x1, Pallas kernels: 96 us -> 100 us  [run_fused(): pl.pallas_call(functools.partial(fused_kernel, pairs, slots, names), out_...]
where the time goes in v7:
time: 144 us
  Pallas kernels  142 us (99%)
    pallas_call x1, Pallas kernels, run_fused(): pl.pallas_call(functools.partial(fused_kernel, pairs, slots, names), out_...  100 us
    pallas_call x1, Pallas kernels, run_opening(): pl.pallas_call(functools.partial(opening_kernel, pairs, slots, names), ou...  38.1 us
    pallas_call x1, Pallas kernels, run_closing(): pl.pallas_call(closing_kernel, out_shape=[shape(array.shape, array.dtype)...  4 us

profile of v7, /device:TPU:0, one launch (start us, length us, event | category | flops | bytes accessed | tf_op | source)
XLA Modules:
  0.0 144.1 jit_solution(7238457660688790482)
XLA Ops:
  0.6 38.1 %opening.1 = (f32[12,768]{1,0:T(8,128)}, bf16[2,288,768]{2,1,0:T(8,128)(2,1)}, bf16[2,288,768]{2,1,0:T(8,128)(2,1)}, bf16[2,288,768]{2,1,0:T(8,128)(2,1)}, f32[5...) custom-call(s32[4]{0:T(128)} %refs_0_.3, ...), custom_call_target="tpu_custom_call" | custom-call | tf_op jit(solution)/shard_map/opening/pallas_call | solution.py:726
  38.8 100.3 %fused.1 = (bf16[1,4,240,768]{3,2,1,0:T(8,128)(2,1)}, bf16[1,4,240,768]{3,2,1,0:T(8,128)(2,1)}, f32[12,8,768]{2,1,0:T(8,128)}, f32[3,8,3072]{2,1,0:T(8,128)}, f3...) custom-call(s32[4]{0:T(128)} %refs_0_.3, s32[4]{0:T(128)} %refs_1_.3, ...), custom_call_target="tpu_custom_call" | custom-call | tf_op jit(solution)/shard_map/fused/pallas_call | solution.py:1275
  139.0 0.0 copy-start
  139.0 4.0 %closing.1 = (bf16[1,4,240,768]{3,2,1,0:T(8,128)(2,1)}, bf16[1,4,240,768]{3,2,1,0:T(8,128)(2,1)}, f32[96,768]{1,0:T(8,128)}, f32[24,3072]{1,0:T(8,128)}, f32[24,2304]{1,0:T(8,128)}, /*index=5*/f32[24,768]{1,0:T(8,128)}) custom-call(bf16[1,4,240,768]{3,2,1,0:T(8,128)(2,1)} %get-tuple-element.52.refs_0_, bf16[1,4,240,768]{3,2,1,0:T(8,128)(2,1)} %get-tuple-element.53.refs_1_, ...), custom_call_target="tpu_custom_call" | custom-call | tf_op jit(solution)/shard_map/closing/pallas_call | solution.py:1300
  143.0 0.0 copy-done
  143.0 0.5 slice_bitcast_fusion.1
  143.6 0.5 slice_bitcast_fusion
Async XLA Ops:
  139.0 4.0 %copy-start = (f32[2,8,128]{2,1,0:T(8,128)S(1)}, f32[2,8,128]{2,1,0:T(8,128)}, u32[]{:S(2)}) copy-start(f32[2,8,128]{2,1,0:T(8,128)} %get-tuple-element.60) | copy-start | bytes 24580

commit v8 on v6

--- a/solution.py
+++ b/solution.py
@@ -740,39 +740,41 @@
     4: [(B, 0, 0)],
     5: [(A, 0, 1)],
     6: [(B, 1, 0)],
-    7: [(A, 0, 2), (A, 1, 0)],
-    8: [(B, 2, 0), (B, 2, 1)],
+    7: [(A, 1, 0)],
+    8: [(A, 0, 2), (B, 2, 0), (B, 2, 1)],
     9: [(A, 1, 1)],
     10: [(B, 3, 0), (B, 3, 1)],
-    11: [(A, 1, 2), (A, 2, 0), (B, 4, 0), (B, 3, 2)],
-    12: [(A, 2, 1), (B, 0, 1), (B, 2, 2)],
-    13: [(A, 0, 3)],
-    14: [(B, 1, 1), (B, 2, 3), (B, 3, 3), (B, 5, 0)],
-    15: [(A, 2, 2), (A, 3, 0), (B, 1, 2), (B, 6, 0), (B, 6, 1)],
-    16: [(A, 3, 1), (B, 0, 2), (B, 1, 3), (R, 0, 0)],
+    11: [(A, 2, 0)],
+    12: [(B, 3, 2), (B, 4, 0)],
+    13: [(A, 1, 2), (A, 2, 1), (B, 2, 2)],
+    14: [(B, 0, 1), (B, 3, 3), (B, 5, 0)],
+    15: [(A, 3, 0), (B, 1, 1)],
+    16: [(A, 0, 3), (A, 2, 2), (B, 1, 2), (B, 2, 3), (B, 6, 0), (B, 6, 1), (A, 3, 1), (R, 0, 0)],
     17: [(R, 0, 1)],
-    18: [(B, 0, 3), (B, 7, 0), (B, 7, 1), (H, 0, 0), (R, 0, 2)],
+    18: [(B, 1, 3), (B, 7, 0), (B, 7, 1), (H, 0, 0), (R, 0, 2)],
     19: [(R, 0, 3)],
-    20: [(A, 3, 2), (O, 0, 0), (B, 7, 2)],
-    21: [(B, 6, 2)],
-    22: [(C, 0, 0), (B, 4, 1), (R, 0, 4)],
-    23: [(A, 1, 3), (A, 0, 4), (R, 0, 5)],
-    24: [(C, 1, 0), (B, 5, 1), (B, 6, 3), (B, 7, 3), (H, 0, 1), (B, 6, 4), (B, 7, 4), (R, 0, 6)],
-    25: [(O, 0, 1), (R, 0, 7)],
-    26: [(C, 0, 1), (C, 2, 0), (B, 5, 2), (B, 2, 4), (B, 3, 4), (R, 0, 8)],
-    27: [(O, 0, 2), (C, 1, 1), (B, 4, 2), (B, 5, 3), (H, 0, 2), (B, 5, 4)],
-    28: [(C, 0, 2), (R, 0, 9)],
-    29: [(O, 0, 3), (C, 2, 1), (B, 4, 3), (H, 0, 3), (B, 1, 4), (B, 4, 4), (C, 1, 2), (R, 1, 0)],
-    30: [(C, 0, 3), (C, 3, 0), (R, 1, 1)],
-    31: [(C, 1, 3), (C, 2, 2), (C, 4, 0), (B, 0, 4), (O, 0, 4), (H, 0, 4), (R, 1, 2)],
-    32: [(C, 5, 0), (C, 0, 4), (R, 1, 3)],
+    20: [(R, 0, 4)],
+    21: [(B, 0, 2), (O, 0, 0), (R, 0, 5)],
+    22: [(B, 7, 2), (B, 6, 2), (A, 3, 2), (C, 0, 0)],
+    23: [(B, 0, 3)],
+    24: [(C, 1, 0), (B, 4, 1), (R, 0, 6)],
+    25: [(B, 6, 3), (B, 7, 3), (B, 6, 4), (B, 7, 4), (R, 0, 7)],
+    26: [(B, 5, 1)],
+    27: [(A, 1, 3), (O, 0, 1), (C, 1, 1), (C, 2, 0), (H, 0, 1), (A, 0, 4), (B, 2, 4), (B, 3, 4), (C, 0, 1), (R, 0, 8)],
+    28: [(B, 5, 2), (R, 0, 9)],
+    29: [(B, 4, 2), (H, 0, 2), (R, 1, 0)],
+    30: [(C, 0, 2), (O, 0, 2), (C, 3, 0), (B, 5, 3), (B, 5, 4)],
+    31: [(C, 1, 2), (C, 4, 0)],
+    32: [(B, 4, 3), (H, 0, 3), (B, 4, 4), (R, 1, 1)],
 }
 TAIL = [
-    (C, 2, 3), (C, 3, 1), (R, 1, 4), (V, 0, 0), (C, 4, 1), (R, 2, 0),
-    (C, 1, 4), (C, 3, 2), (C, 5, 1), (V, 0, 1), (R, 2, 1), (C, 4, 2),
-    (V, 0, 2), (C, 2, 4), (C, 3, 3), (R, 2, 2), (C, 5, 2), (C, 4, 3),
-    (R, 2, 3), (V, 0, 3), (C, 5, 3), (R, 2, 4), (C, 3, 4), (C, 4, 4),
-    (V, 0, 4), (C, 5, 4),
+    (C, 5, 0), (C, 2, 1), (C, 0, 3), (O, 0, 3), (R, 1, 2), (V, 0, 0),
+    (C, 1, 3), (C, 3, 1), (R, 1, 3), (C, 4, 1), (B, 1, 4), (C, 2, 2),
+    (V, 0, 1), (R, 1, 4), (B, 0, 4), (C, 5, 1), (H, 0, 4), (C, 3, 2),
+    (C, 0, 4), (C, 2, 3), (R, 2, 0), (C, 4, 2), (V, 0, 2), (O, 0, 4),
+    (C, 5, 2), (C, 1, 4), (C, 3, 3), (C, 4, 3), (R, 2, 1), (V, 0, 3),
+    (C, 5, 3), (R, 2, 2), (C, 2, 4), (C, 3, 4), (C, 4, 4), (R, 2, 3),
+    (V, 0, 4), (C, 5, 4), (R, 2, 4),
 ]
 
 
@@ -826,9 +828,9 @@
         copy.start()
     r.gnormal[...] = jnp.zeros_like(r.gnormal)
     live = live_rows(lens, pairs, rows, slots)
-    for copy in early:
+    r.total[...] = jnp.zeros_like(r.total)
+    for copy in early[:3]:
         copy.wait()
-    r.total[...] = r.hidden[...] + vec_in(7)
     r.gdown[...] = (r.cot[...].reshape(every, width).astype(F32) * live).astype(BF16)
     r.unit_h[...] = jnp.zeros_like(r.unit_h)
     for copy in late:
@@ -1036,7 +1038,8 @@
     for copy in wqkv_loads:
         copy.start()
     units[H, 0].start()
-    r.result[...] = (r.total[...] * live).astype(BF16).reshape(pairs, rows, width)
+    early[3].wait()
+    r.result[...] = ((r.hidden[...] + r.total[...] + vec_in(7)) * live).astype(BF16).reshape(pairs, rows, width)
 
     for pair in range(pairs):
         give_start(pair)

time: 140 us -> 137 us (0.979)
  Pallas kernels: 138 us -> 135 us
    pallas_call x1, Pallas kernels: 96 us -> 93.3 us  [run_fused(): pl.pallas_call(functools.partial(fused_kernel, pairs, slots, names), out_...]
where the time goes in v8:
time: 137 us
  Pallas kernels  135 us (99%)
    pallas_call x1, Pallas kernels, run_fused(): pl.pallas_call(functools.partial(fused_kernel, pairs, slots, names), out_...  93.3 us
    pallas_call x1, Pallas kernels, run_opening(): pl.pallas_call(functools.partial(opening_kernel, pairs, slots, names), ou...  38.1 us
    pallas_call x1, Pallas kernels, run_closing(): pl.pallas_call(closing_kernel, out_shape=[shape(array.shape, array.dtype)...  4 us

profile of v8, /device:TPU:0, one launch (start us, length us, event | category | flops | bytes accessed | tf_op | source)
XLA Modules:
  0.0 137.2 jit_solution(18238490161452129949)
XLA Ops:
  0.6 38.1 %opening.1 = (f32[12,768]{1,0:T(8,128)}, bf16[2,288,768]{2,1,0:T(8,128)(2,1)}, bf16[2,288,768]{2,1,0:T(8,128)(2,1)}, bf16[2,288,768]{2,1,0:T(8,128)(2,1)}, f32[5...) custom-call(s32[4]{0:T(128)} %refs_0_.3, ...), custom_call_target="tpu_custom_call" | custom-call | tf_op jit(solution)/shard_map/opening/pallas_call | solution.py:726
  38.8 93.3 %fused.1 = (bf16[1,4,240,768]{3,2,1,0:T(8,128)(2,1)}, bf16[1,4,240,768]{3,2,1,0:T(8,128)(2,1)}, f32[12,8,768]{2,1,0:T(8,128)}, f32[3,8,3072]{2,1,0:T(8,128)}, f3...) custom-call(s32[4]{0:T(128)} %refs_0_.3, s32[4]{0:T(128)} %refs_1_.3, ...), custom_call_target="tpu_custom_call" | custom-call | tf_op jit(solution)/shard_map/fused/pallas_call | solution.py:1277
  132.1 0.0 copy-start
  132.1 4.0 %closing.1 = (bf16[1,4,240,768]{3,2,1,0:T(8,128)(2,1)}, bf16[1,4,240,768]{3,2,1,0:T(8,128)(2,1)}, f32[96,768]{1,0:T(8,128)}, f32[24,3072]{1,0:T(8,128)}, f32[24,2304]{1,0:T(8,128)}, /*index=5*/f32[24,768]{1,0:T(8,128)}) custom-call(bf16[1,4,240,768]{3,2,1,0:T(8,128)(2,1)} %get-tuple-element.52.refs_0_, bf16[1,4,240,768]{3,2,1,0:T(8,128)(2,1)} %get-tuple-element.53.refs_1_, ...), custom_call_target="tpu_custom_call" | custom-call | tf_op jit(solution)/shard_map/closing/pallas_call | solution.py:1302
  136.1 0.0 copy-done
  136.1 0.5 slice_bitcast_fusion.1
  136.6 0.5 slice_bitcast_fusion
Async XLA Ops:
  132.1 4.0 %copy-start = (f32[2,8,128]{2,1,0:T(8,128)S(1)}, f32[2,8,128]{2,1,0:T(8,128)}, u32[]{:S(2)}) copy-start(f32[2,8,128]{2,1,0:T(8,128)} %get-tuple-element.60) | copy-start | bytes 24580
